TPU v7x, 32 devices: a whole 2x2x4 slice. The times are simulated.
32 devices in a mesh: wide: 8 (over z, core), narrow: 4 (over y, x).
Axes of the slice: x: 2, y: 2, z: 4, core: 2. Of those that a mesh axis runs over, the one named last changes fastest.
Arguments:
- block_input: bfloat16 [16384, 1536], P(('wide', 'narrow')), may hold values from -23 to 23
- routes: int32 [16384, 2], P('wide'), may hold values from 0 to 15, all different within a row
- first_gain: bfloat16 [1536], P('narrow'), may hold values from 0.099609375 to 1.8984375
- query_key_value_weight: bfloat16 [1536, 2560], P('wide', 'narrow'), may hold values from -0.15625 to 0.15625
- output_weight: bfloat16 [1536, 1536], P('narrow', 'wide'), may hold values from -4 to 4
- second_gain: bfloat16 [1536], P('narrow'), may hold values from 0.099609375 to 1.8984375
- router_weight: bfloat16 [1536, 16], P('wide'), may hold values from -0.109375 to 0.109375
- gate_weight: bfloat16 [16, 1536, 1024], P(None, 'wide', 'narrow'), may hold values from -0.15625 to 0.15625
- up_weight: bfloat16 [16, 1536, 1024], P(None, 'wide', 'narrow'), may hold values from -0.15625 to 0.15625
- down_weight: bfloat16 [16, 1536, 1024], P(None, 'wide', 'narrow'), may hold values from -0.375 to 0.375
- cotangent: bfloat16 [16384, 1536], P(('wide', 'narrow')), may hold values from -6 to 6
Outputs:
- block_output: bfloat16 [16384, 1536], P(('wide', 'narrow'))
- input_grad: float32 [16384, 1536], P(('wide', 'narrow'))
- first_gain_grad: float32 [1536], P('narrow')
- input_weight_grad: float32 [1536, 2560], P('wide', 'narrow')
- output_weight_grad: float32 [1536, 1536], P('narrow', 'wide')
- second_gain_grad: float32 [1536], P('narrow')
- router_weight_grad: float32 [1536, 16], P('wide')
- gate_weight_grad: float32 [16, 1536, 1024], P(None, 'wide', 'narrow')
- up_weight_grad: float32 [16, 1536, 1024], P(None, 'wide', 'narrow')
- down_weight_grad: float32 [16, 1536, 1024], P(None, 'wide', 'narrow')
All inputs are finite; a program needn't handle non-finite values.
Results may differ from a plain program's by a relative error of at most 0.015.
The roundings to bfloat16 on the way count: a program that leaves them out, or rounds other values in their place, can miss the bound.
Values may be sent and summed in bfloat16 or wider, within the bound.
A program may use at most 576 MiB of HBM per device.

v0:
```python
import jax
import jax.numpy as jnp
from jax import lax
from jax.sharding import PartitionSpec as P

QUERY_HEADS = 24
KEY_VALUE_HEADS = 8
HEAD_SIZE = 64
E = 16
TOPK = 2
SEQUENCE_LENGTH = 2048
QBLK = 512
BLOCK = 256
GROUP = 4


EPSILON = 1e-05


def arrange(experts_of):
    assigned = experts_of.shape[0] * experts_of.shape[1]
    flat_ids = experts_of.reshape(assigned)
    one_hot = (flat_ids[:, None] == jnp.arange(E, dtype=jnp.int32)[None, :]).astype(jnp.int32)
    expert_rows = jnp.sum(one_hot, axis=0, dtype=jnp.int32)
    padded = (expert_rows + BLOCK - 1) // BLOCK * BLOCK
    block_ends = jnp.cumsum(padded, dtype=jnp.int32)
    starts = block_ends - padded
    before = jnp.cumsum(one_hot, axis=0, dtype=jnp.int32) - one_hot
    slot_of = jnp.sum((before + starts[None, :]) * one_hot, axis=1, dtype=jnp.int32)
    buffer_rows = assigned + E * BLOCK
    row_owner = (
        jnp.zeros((buffer_rows,), jnp.int32).at[slot_of].set(jnp.arange(assigned, dtype=jnp.int32))
    )
    row_live = (
        jnp.zeros((buffer_rows,), jnp.int32).at[slot_of].set(jnp.ones((assigned,), jnp.int32))
    )
    firsts = jnp.arange(buffer_rows // BLOCK, dtype=jnp.int32) * BLOCK
    later = (firsts[:, None] >= block_ends[None, :]).astype(jnp.int32)
    block_expert = jnp.minimum(jnp.sum(later, axis=1, dtype=jnp.int32), E - 1)
    return (slot_of, row_owner, row_live, block_expert)


def visible(first, stop):
    return (first + jnp.arange(stop - first))[:, None] >= jnp.arange(stop)[None, :]


def pick_blocks(weights, owners):
    return jnp.stack(
        [
            lax.dynamic_index_in_dim(weights, owners[index], 0, keepdims=False)
            for index in range(GROUP)
        ]
    )


def add_blocks(total, owners, blocks):
    for index in range(GROUP):
        current = lax.dynamic_index_in_dim(total, owners[index], 0, keepdims=False)
        total = lax.dynamic_update_index_in_dim(total, current + blocks[index], owners[index], 0)
    return total


def combine_slots(buffer, slots, weights):
    total = jnp.take(buffer, slots[:, 0], axis=0) * weights[:, 0:1]
    total = total + jnp.take(buffer, slots[:, 1], axis=0) * weights[:, 1:2]
    return total


def attend_forward(weight_pieces):
    head_group = weight_pieces.shape[2] - 2
    queries = weight_pieces[:, :, :head_group, :]
    key_rows = weight_pieces[:, :, head_group, :]
    value_rows = weight_pieces[:, :, head_group + 1, :]
    outputs = []
    totals = []
    for index in range(SEQUENCE_LENGTH // QBLK):
        first = index * QBLK
        stop = first + QBLK
        scores = (
            jnp.einsum(
                "qgrd,kgd->grqk",
                queries[first:stop],
                key_rows[:stop],
                preferred_element_type=jnp.float32,
            )
            * 0.125
        )
        scores = jnp.where(visible(first, stop), scores, -1e30)
        highest = jnp.max(scores, axis=-1, keepdims=True)
        raised = jnp.exp(scores - highest)
        denominator = jnp.sum(raised, axis=-1, keepdims=True)
        attn_probs = (raised / denominator).astype(jnp.bfloat16)
        outputs.append(
            jnp.einsum(
                "grqk,kgd->qgrd", attn_probs, value_rows[:stop], preferred_element_type=jnp.float32
            )
        )
        totals.append(highest[..., 0] + jnp.log(denominator[..., 0]))
    mixed = jnp.concatenate(outputs, axis=0)
    return (
        mixed.reshape(SEQUENCE_LENGTH, -1).astype(jnp.bfloat16),
        jnp.concatenate(totals, axis=2),
    )


def attend_backward(item):
    weight_pieces, totals, grads = item
    head_group = weight_pieces.shape[2] - 2
    queries = weight_pieces[:, :, :head_group, :]
    key_rows = weight_pieces[:, :, head_group, :]
    value_rows = weight_pieces[:, :, head_group + 1, :]
    grad_keys = jnp.zeros(key_rows.shape, jnp.float32)
    grad_values = jnp.zeros(value_rows.shape, jnp.float32)
    grad_queries = []
    for index in range(SEQUENCE_LENGTH // QBLK):
        first = index * QBLK
        stop = first + QBLK
        tail = SEQUENCE_LENGTH - stop
        query_rows = queries[first:stop]
        grad_rows = grads[first:stop]
        scores = (
            jnp.einsum(
                "qgrd,kgd->grqk", query_rows, key_rows[:stop], preferred_element_type=jnp.float32
            )
            * 0.125
        )
        scores = jnp.where(visible(first, stop), scores, -1e30)
        attn_probs = jnp.exp(scores - totals[:, :, first:stop, None])
        grad_probs = jnp.einsum(
            "qgrd,kgd->grqk", grad_rows, value_rows[:stop], preferred_element_type=jnp.float32
        )
        centre = jnp.sum(grad_probs * attn_probs, axis=-1, keepdims=True)
        grad_scores = (attn_probs * (grad_probs - centre)).astype(jnp.bfloat16)
        value_term = jnp.einsum(
            "grqk,qgrd->kgd",
            attn_probs.astype(jnp.bfloat16),
            grad_rows,
            preferred_element_type=jnp.float32,
        )
        key_term = (
            jnp.einsum(
                "grqk,qgrd->kgd", grad_scores, query_rows, preferred_element_type=jnp.float32
            )
            * 0.125
        )
        grad_values = grad_values + jnp.pad(value_term, ((0, tail), (0, 0), (0, 0)))
        grad_keys = grad_keys + jnp.pad(key_term, ((0, tail), (0, 0), (0, 0)))
        grad_queries.append(
            jnp.einsum(
                "grqk,kgd->qgrd", grad_scores, key_rows[:stop], preferred_element_type=jnp.float32
            )
            * 0.125
        )
    merged = jnp.concatenate(
        [
            jnp.concatenate(grad_queries, axis=0),
            grad_keys[:, :, None, :],
            grad_values[:, :, None, :],
        ],
        axis=2,
    )
    return merged.reshape(SEQUENCE_LENGTH, -1).astype(jnp.bfloat16)


def local(
    block_input,
    routes,
    first_gain,
    query_key_value_weight,
    output_weight,
    second_gain,
    router_weight,
    gate_weight,
    up_weight,
    down_weight,
    cotangent,
):
    narrow_count = lax.axis_size("narrow")
    wide_count = lax.axis_size("wide")
    row_part = block_input.shape[0]
    row_offset = lax.axis_index("narrow") * row_part
    gain_part = first_gain.shape[0]
    gain_offset = lax.axis_index("narrow") * gain_part
    inputs, grad_full, gain_one, gain_two = (
        lax.all_gather(block_input, "narrow", axis=0, tiled=True),
        lax.all_gather(cotangent, "narrow", axis=0, tiled=True),
        lax.all_gather(first_gain, "narrow", axis=0, tiled=True),
        lax.all_gather(second_gain, "narrow", axis=0, tiled=True),
    )
    token_count = inputs.shape[0]
    x_full = inputs.astype(jnp.float32)
    width = x_full.shape[1]
    gain_one_f = gain_one.astype(jnp.float32)
    gain_two_f = gain_two.astype(jnp.float32)
    scale_one = lax.rsqrt(jnp.mean(x_full * x_full, axis=1, keepdims=True) + EPSILON)
    normed_one = x_full * scale_one
    gained_one = normed_one * gain_one_f
    attn_in = gained_one.astype(jnp.bfloat16)
    input_full, output_full = (
        lax.all_gather(query_key_value_weight, "wide", axis=0, tiled=True),
        lax.all_gather(output_weight, "wide", axis=1, tiled=True),
    )
    projected_rows = jnp.dot(attn_in, input_full, preferred_element_type=jnp.float32).astype(
        jnp.bfloat16
    )
    head_group = QUERY_HEADS // KEY_VALUE_HEADS
    local_groups = projected_rows.shape[1] // ((head_group + 2) * HEAD_SIZE)
    weight_pieces = projected_rows.reshape(
        token_count // SEQUENCE_LENGTH, SEQUENCE_LENGTH, local_groups, head_group + 2, HEAD_SIZE
    )
    mixed, log_totals = lax.map(attend_forward, weight_pieces)
    mixed = mixed.reshape(token_count, -1)
    branch_part = jnp.dot(mixed, output_full, preferred_element_type=jnp.float32)
    branch_own = lax.psum_scatter(branch_part, "narrow", scatter_dimension=0, tiled=True)
    middle_own = block_input.astype(jnp.float32) + branch_own
    middle_low = lax.all_gather(middle_own.astype(jnp.bfloat16), "narrow", axis=0, tiled=True)
    middle_float = middle_low.astype(jnp.float32)
    scale_two = lax.rsqrt(jnp.mean(middle_float * middle_float, axis=1, keepdims=True) + EPSILON)
    normed_two = middle_float * scale_two
    gained_two = normed_two * gain_two_f
    expert_in = gained_two.astype(jnp.bfloat16)
    router_full, gate_full, up_full, down_full = (
        lax.all_gather(router_weight, "wide", axis=0, tiled=True),
        lax.all_gather(gate_weight, "wide", axis=1, tiled=True),
        lax.all_gather(up_weight, "wide", axis=1, tiled=True),
        lax.all_gather(down_weight, "wide", axis=1, tiled=True),
    )
    logits = jnp.dot(expert_in, router_full, preferred_element_type=jnp.float32)
    picked = (routes[:, :, None] == jnp.arange(E, dtype=jnp.int32)[None, None, :]).astype(
        jnp.float32
    )
    chosen = jnp.sum(picked * logits[:, None, :], axis=2)
    gates = jax.nn.softmax(chosen, axis=1)
    slot_of, row_owner, row_live, block_expert = arrange(routes)
    token_slots = slot_of.reshape(token_count, TOPK)
    token_of = row_owner // TOPK
    alive = row_live.astype(jnp.float32)
    row_gate = jnp.take(gates.reshape(-1), row_owner) * alive
    step_rows = GROUP * BLOCK
    step_count = token_of.shape[0] // step_rows
    rows_all = jnp.take(expert_in, token_of, axis=0) * row_live[:, None].astype(jnp.bfloat16)
    rows_steps = rows_all.reshape(step_count, GROUP, BLOCK, width)
    owner_steps = block_expert.reshape(step_count, GROUP)

    def forward_step(carry, item):
        rows, owners = item
        gate_val = jnp.einsum(
            "gbd,gdf->gbf", rows, pick_blocks(gate_full, owners), preferred_element_type=jnp.float32
        )
        up_val = jnp.einsum(
            "gbd,gdf->gbf", rows, pick_blocks(up_full, owners), preferred_element_type=jnp.float32
        )
        active = (jax.nn.silu(gate_val) * up_val).astype(jnp.bfloat16)
        result = jnp.einsum(
            "gbf,gdf->gbd",
            active,
            pick_blocks(down_full, owners),
            preferred_element_type=jnp.float32,
        )
        return (carry, (result, gate_val, up_val))

    _, (expert_rows, gate_kept, up_kept) = lax.scan(
        forward_step, jnp.zeros((), jnp.float32), (rows_steps, owner_steps)
    )
    expert_part = combine_slots(expert_rows.reshape(-1, width), token_slots, gates)
    expert_rows = None
    expert_own = lax.psum_scatter(
        expert_part.astype(jnp.bfloat16), "narrow", scatter_dimension=0, tiled=True
    ).astype(jnp.float32)
    block_output = (middle_own + expert_own).astype(jnp.bfloat16)
    input_back, output_back, router_back, gate_back, up_back, down_back = (
        lax.all_gather(query_key_value_weight, "wide", axis=0, tiled=True),
        lax.all_gather(output_weight, "wide", axis=1, tiled=True),
        lax.all_gather(router_weight, "wide", axis=0, tiled=True),
        lax.all_gather(gate_weight, "wide", axis=1, tiled=True),
        lax.all_gather(up_weight, "wide", axis=1, tiled=True),
        lax.all_gather(down_weight, "wide", axis=1, tiled=True),
    )
    cot_all = jnp.take(grad_full, token_of, axis=0)
    cot_steps = cot_all.reshape(step_count, GROUP, BLOCK, width)
    weight_steps = row_gate.reshape(step_count, GROUP, BLOCK)

    def backward_step(carry, item):
        grad_gate, grad_up, grad_down = carry
        rows, cot_rows, row_weights, owners, gate_val, up_val = item
        scaled = (cot_rows.astype(jnp.float32) * row_weights[:, :, None]).astype(jnp.bfloat16)
        gate_w = pick_blocks(gate_back, owners)
        up_w = pick_blocks(up_back, owners)
        down_w = pick_blocks(down_back, owners)
        sigma = jax.nn.sigmoid(gate_val)
        silu_val = gate_val * sigma
        active = (silu_val * up_val).astype(jnp.bfloat16)
        raw_grad = jnp.einsum("gbd,gdf->gbf", cot_rows, down_w, preferred_element_type=jnp.float32)
        gate_rows = jnp.sum(active.astype(jnp.float32) * raw_grad, axis=2)
        act_grad = jnp.einsum("gbd,gdf->gbf", scaled, down_w, preferred_element_type=jnp.float32)
        gate_d = (act_grad * up_val * sigma * (1.0 + gate_val * (1.0 - sigma))).astype(jnp.bfloat16)
        up_d = (act_grad * silu_val).astype(jnp.bfloat16)
        grad_gate = add_blocks(
            grad_gate,
            owners,
            jnp.einsum("gbd,gbf->gdf", rows, gate_d, preferred_element_type=jnp.float32),
        )
        grad_up = add_blocks(
            grad_up,
            owners,
            jnp.einsum("gbd,gbf->gdf", rows, up_d, preferred_element_type=jnp.float32),
        )
        grad_down = add_blocks(
            grad_down,
            owners,
            jnp.einsum("gbd,gbf->gdf", scaled, active, preferred_element_type=jnp.float32),
        )
        back_rows = jnp.einsum(
            "gbf,gdf->gbd", gate_d, gate_w, preferred_element_type=jnp.float32
        ) + jnp.einsum("gbf,gdf->gbd", up_d, up_w, preferred_element_type=jnp.float32)
        return ((grad_gate, grad_up, grad_down), (back_rows, gate_rows))

    start_carry = (
        jnp.zeros(gate_full.shape, jnp.float32),
        jnp.zeros(up_full.shape, jnp.float32),
        jnp.zeros(down_full.shape, jnp.float32),
    )
    (grad_gate, grad_up, grad_down), (back_all, gate_rows_all) = lax.scan(
        backward_step,
        start_carry,
        (rows_steps, cot_steps, weight_steps, owner_steps, gate_kept, up_kept),
    )
    expert_back = combine_slots(
        back_all.reshape(-1, width), token_slots, jnp.ones((token_count, TOPK), jnp.float32)
    )
    back_all = None
    gate_part = jnp.take(gate_rows_all.reshape(-1), slot_of).reshape(token_count, TOPK)
    expert_sum, gate_sum = (
        lax.psum_scatter(expert_back, "narrow", scatter_dimension=0, tiled=True),
        lax.psum_scatter(gate_part, "narrow", scatter_dimension=0, tiled=True),
    )
    gates_own = lax.dynamic_slice_in_dim(gates, row_offset, row_part, 0)
    picked_own = lax.dynamic_slice_in_dim(picked, row_offset, row_part, 0)
    centre = jnp.sum(gates_own * gate_sum, axis=1, keepdims=True)
    logit_part = gates_own * (gate_sum - centre)
    logit_grad = jnp.sum(picked_own * logit_part[:, :, None], axis=1).astype(jnp.bfloat16)
    router_rows = jnp.einsum(
        "te,de->td", logit_grad, router_back, preferred_element_type=jnp.float32
    )
    norm_grad = expert_sum + router_rows
    normed_two_own = lax.dynamic_slice_in_dim(normed_two, row_offset, row_part, 0)
    scale_two_own = lax.dynamic_slice_in_dim(scale_two, row_offset, row_part, 0)
    row_dot = jnp.sum(norm_grad * normed_two_own * gain_two_f, axis=1, keepdims=True)
    gain_two_part = jnp.sum(norm_grad * normed_two_own, axis=0)
    mid_grad = cotangent.astype(jnp.float32) + scale_two_own * (
        gain_two_f * norm_grad - normed_two_own * row_dot / width
    )
    branch_grad, logit_full = (
        lax.all_gather(mid_grad.astype(jnp.bfloat16), "narrow", axis=0, tiled=True),
        lax.all_gather(logit_grad, "narrow", axis=0, tiled=True),
    )
    grad_router = jnp.einsum("td,te->de", expert_in, logit_full, preferred_element_type=jnp.float32)
    router_grad, gate_grad, up_grad, down_grad = (
        lax.psum_scatter(grad_router, "wide", scatter_dimension=0, tiled=True),
        lax.psum_scatter(grad_gate, "wide", scatter_dimension=1, tiled=True),
        lax.psum_scatter(grad_up, "wide", scatter_dimension=1, tiled=True),
        lax.psum_scatter(grad_down, "wide", scatter_dimension=1, tiled=True),
    )
    grad_output_w = jnp.einsum("tc,td->cd", mixed, branch_grad, preferred_element_type=jnp.float32)
    mixed_grad = jnp.einsum(
        "td,cd->tc", branch_grad, output_back, preferred_element_type=jnp.float32
    ).astype(jnp.bfloat16)
    mixed_grad = mixed_grad.reshape(
        token_count // SEQUENCE_LENGTH, SEQUENCE_LENGTH, local_groups, head_group, HEAD_SIZE
    )
    projected_grad = lax.map(attend_backward, (weight_pieces, log_totals, mixed_grad)).reshape(
        token_count, -1
    )
    grad_input_w = jnp.einsum(
        "td,tc->dc", attn_in, projected_grad, preferred_element_type=jnp.float32
    )
    input_part = jnp.einsum(
        "tc,dc->td", projected_grad, input_back, preferred_element_type=jnp.float32
    )
    gain_one_part = jnp.sum(input_part * normed_one, axis=0)
    gain_tiles = jnp.tile(
        jnp.concatenate([gain_one_part, gain_two_part])[None, :], (narrow_count, 1)
    )
    input_sum, gain_narrow = (
        lax.psum_scatter(input_part, "narrow", scatter_dimension=0, tiled=True),
        lax.psum_scatter(gain_tiles, "narrow", scatter_dimension=0, tiled=True),
    )
    normed_one_own = lax.dynamic_slice_in_dim(normed_one, row_offset, row_part, 0)
    scale_one_own = lax.dynamic_slice_in_dim(scale_one, row_offset, row_part, 0)
    input_dot = jnp.sum(input_sum * normed_one_own * gain_one_f, axis=1, keepdims=True)
    input_grad = mid_grad + scale_one_own * (
        gain_one_f * input_sum - normed_one_own * input_dot / width
    )
    gain_rows = jnp.tile(gain_narrow, (wide_count, 1))
    input_w_grad, output_w_grad, gain_pair = (
        lax.psum_scatter(grad_input_w, "wide", scatter_dimension=0, tiled=True),
        lax.psum_scatter(grad_output_w, "wide", scatter_dimension=1, tiled=True),
        lax.psum_scatter(gain_rows, "wide", scatter_dimension=0, tiled=True),
    )
    first_gain_grad = lax.dynamic_slice_in_dim(gain_pair[0], gain_offset, gain_part, 0)
    second_gain_grad = lax.dynamic_slice_in_dim(gain_pair[0], width + gain_offset, gain_part, 0)
    return (
        block_output,
        input_grad,
        first_gain_grad,
        input_w_grad,
        output_w_grad,
        second_gain_grad,
        router_grad,
        gate_grad,
        up_grad,
        down_grad,
    )


def solution(mesh):
    placed = (
        P(("wide", "narrow"), None),
        P("wide", None),
        P("narrow"),
        P("wide", "narrow"),
        P("narrow", "wide"),
        P("narrow"),
        P("wide", None),
        P(None, "wide", "narrow"),
        P(None, "wide", "narrow"),
        P(None, "wide", "narrow"),
        P(("wide", "narrow"), None),
    )
    return jax.shard_map(
        local,
        mesh=mesh,
        in_specs=placed,
        out_specs=(
            P(("wide", "narrow"), None),
            P(("wide", "narrow"), None),
            P("narrow"),
            P("wide", "narrow"),
            P("narrow", "wide"),
            P("narrow"),
            P("wide", None),
            P(None, "wide", "narrow"),
            P(None, "wide", "narrow"),
            P(None, "wide", "narrow"),
        ),
        check_vma=False,
    )
```

profile of v0, /device:TPU:0, one launch (start us, length us, event | category | flops | bytes accessed | tf_op | source)
XLA Modules:
  0.0 3236.6 jit_solution(7500915411528722774)
XLA Ops:
  24.1 58.7 %all-gather.13.cloned.1.call-done = bf16[2048,1536]{1,0:T(8,128)(2,1)} async-done(((bf16[512,1536]{1,0:T(8,128)(2,1)}), bf16[2048,1536]{1,0:T(8,128)(2,1)}) %all-gather.13.cloned.1.call-update) | async-done | bytes 6291472 | tf_op jit(solution)/shard_map/all_gather | solution.py:185
  86.8 25.6 all-gather.15.cloned.1.call-done
  208.7 119.8 %reduce-scatter.16.cloned.1.call-done = f32[512,1536]{1,0:T(8,128)} async-done(((f32[2048,1536]{1,0:T(8,128)}), f32[512,1536]{1,0:T(8,128)}) %reduce-scatter.16.cloned.1.call-update) | async-done | bytes 3145744 | tf_op jit(solution)/shard_map/reduce_scatter | solution.py:214
  400.4 53.0 %gather_fusion.5 = bf16[8192,1536]{1,0:T(8,128)(2,1)} fusion(bf16[2048,1536]{1,0:T(8,128)(2,1)} %all-gather.27.cloned.1.call-done, s32[8192]{0:T(1024)S(1)} %get-tuple-element.409), kind=kCustom, calls=%fused_computation.2.clone | custom fusion | bytes 50364416 | tf_op jit(solution)/shard_map/jit(_take)/gather | solution.py:279
  453.4 19.4 all-gather.19.cloned.1.call-done
  489.0 53.0 %gather_fusion.2 = bf16[8192,1536]{1,0:T(8,128)(2,1)} fusion(bf16[2048,1536]{1,0:T(8,128)(2,1)} %get-tuple-element.403, s32[8192]{0:T(1024)S(1)} %get-tuple-element.409), kind=kCustom, calls=%fused_computation.clone | custom fusion | bytes 50364416 | tf_op jit(solution)/shard_map/jit(_take)/gather | solution.py:241
  547.6 45.5 %gather_fusion = f32[8192]{0:T(1024)S(1)} fusion(f32[4096]{0:T(1024)S(1)} %div.132, s32[8192]{0:T(1024)S(1)} %get-tuple-element.408), kind=kCustom, calls=%fused_computation.6 | custom fusion | bytes 98304 | tf_op jit(solution)/shard_map/jit(_take)/gather | solution.py:238
  594.4 34.2 %broadcast_select_fusion = (bf16[8192,1536]{1,0:T(8,128)(2,1)}, bf16[8192,1536]{1,0:T(8,128)(2,1)}) fusion(bf16[8192,1536]{1,0:T(8,128)(2,1)} %gather_fusion.5, pred[8192]{0:T(1024)(128)(4,1)S(1)} %compare_and_fusion, bf16[8192]{0:T(1024)(128)(2,1)S(1)} %convert_element_type.173, bf16[8192,1536]{1,0:T(8,128)(2,1)} %gather_fusion.2), kind=kLoop, calls=%fused_computation.165 | loop fusion | flops 37748736 | bytes 100687872 | tf_op jit(solution)/shard_map/jit(_take)/select_n | solution.py:279
  628.6 79.2 %all-gather.23.cloned.1.call-done = bf16[16,1536,256]{2,1,0:T(8,128)(2,1)} async-done(((bf16[16,192,256]{2,1,0:T(8,128)(2,1)}), bf16[16,1536,256]{2,1,0:T(8,128)(2,1)}) %all-gather.23.cloned.1.call-update) | async-done | bytes 12582928 | tf_op jit(solution)/shard_map/all_gather | solution.py:225
  707.8 116.6 %all-gather.25.cloned.1.call-done = bf16[16,1536,256]{2,1,0:T(8,128)(2,1)} async-done(((bf16[16,192,256]{2,1,0:T(8,128)(2,1)}), bf16[16,1536,256]{2,1,0:T(8,128)(2,1)}) %all-gather.25.cloned.1.call-update) | async-done | bytes 12582928 | tf_op jit(solution)/shard_map/all_gather | solution.py:226
  824.4 16.5 broadcast.419.clone
  840.9 210.2 %while.9 = (s32[]{:T(128)}, f32[8,4,256,1536]{3,2,1,0:T(8,128)}, f32[8,4,256,256]{3,2,1,0:T(8,128)}, f32[8,4,256,256]{3,2,1,0:T(8,128)}, bf16[8,4,256,1536]{3,2,...) while((s32[]{:T(128)}, f32[8,4,256,1536]{3,2,1,0:T(8,128)}, ...), condition=%wide.region_20.22_spmd, body=%wide.region_19.21_spmd.sunk | while | flops 2431647744 | bytes 47188332 | solution.py:262
  1051.1 29.7 gather_fusion.4
  1080.8 29.6 gather_fusion.3
  1143.2 16.5 broadcast.419
  1159.8 564.2 %while.10 = (s32[]{:T(128)}, f32[16,1536,256]{2,1,0:T(8,128)}, f32[16,1536,256]{2,1,0:T(8,128)}, f32[16,1536,256]{2,1,0:T(8,128)}, f32[8,4,256,1536]{3,2,1,0:T(8...) while((s32[]{:T(128)}, f32[16,1536,256]{2,1,0:T(8,128)}, ...), condition=%wide.region_27.30_spmd, body=%wide.region_25.29_spmd.sunk | while | flops 5676465152 | bytes 150500832 | solution.py:323
  1724.0 29.9 gather_fusion.7
  1753.9 29.7 gather_fusion.6
  1783.7 23.0 gather_fusion.1
  1809.0 24.9 select_add_fusion
  1836.6 122.6 %reduce-scatter.20.cloned.1.call-done = f32[512,1536]{1,0:T(8,128)} async-done(((f32[2048,1536]{1,0:T(8,128)}), f32[512,1536]{1,0:T(8,128)}) %reduce-scatter.20.cloned.1.call-update) | async-done | bytes 3145744 | tf_op jit(solution)/shard_map/reduce_scatter | solution.py:334
  1986.3 53.2 %all-gather.29.cloned.1.call-done = bf16[2048,1536]{1,0:T(8,128)(2,1)} async-done(((bf16[512,1536]{1,0:T(8,128)(2,1)}), bf16[2048,1536]{1,0:T(8,128)(2,1)}) %all-gather.29.cloned.1.call-update) | async-done | bytes 6291472 | tf_op jit(solution)/shard_map/all_gather | solution.py:354
  2120.5 17.5 fusion.96
  2138.0 17.4 fusion.98
  2199.4 17.7 all-reduce.6
  2246.7 23.0 all-reduce.10.cloned.1.call-done
  2271.1 124.1 %reduce-scatter.22.cloned.1.call-done = f32[512,1536]{1,0:T(8,128)} async-done(((f32[2048,1536]{1,0:T(8,128)}), f32[512,1536]{1,0:T(8,128)}) %reduce-scatter.22.cloned.1.call-update) | async-done | bytes 3145744 | tf_op jit(solution)/shard_map/reduce_scatter | solution.py:385
  2404.2 30.1 reduce-scatter.26.cloned.1.call-done
  2434.3 49.7 %reduce-scatter.24.cloned.1.call-done = f32[192,640]{1,0:T(8,128)} async-done(((f32[1536,640]{1,0:T(8,128)}), f32[192,640]{1,0:T(8,128)}) %reduce-scatter.24.cloned.1.call-update) | async-done | bytes 491536 | tf_op jit(solution)/shard_map/reduce_scatter | solution.py:396
  2484.0 248.4 %reduce-scatter.28.cloned.1.call-done = f32[16,192,256]{2,1,0:T(8,128)} async-done(((f32[16,1536,256]{2,1,0:T(8,128)}), f32[16,192,256]{2,1,0:T(8,128)}) %reduce-scatter.28.cloned.1.call-update) | async-done | bytes 3145744 | tf_op jit(solution)/shard_map/reduce_scatter | solution.py:360
  2732.4 248.4 %reduce-scatter.30.cloned.1.call-done = f32[16,192,256]{2,1,0:T(8,128)} async-done(((f32[16,1536,256]{2,1,0:T(8,128)}), f32[16,192,256]{2,1,0:T(8,128)}) %reduce-scatter.30.cloned.1.call-update) | async-done | bytes 3145744 | tf_op jit(solution)/shard_map/reduce_scatter | solution.py:361
  2980.9 248.6 %reduce-scatter.32.cloned.1.call-done = f32[16,192,256]{2,1,0:T(8,128)} async-done(((f32[16,1536,256]{2,1,0:T(8,128)}), f32[16,192,256]{2,1,0:T(8,128)}) %reduce-scatter.32.cloned.1.call-update) | async-done | bytes 3145744 | tf_op jit(solution)/shard_map/reduce_scatter | solution.py:362
  (610 shorter events, 1091.6 us)
Async XLA Ops:
  7.2 75.6 %all-gather.13.cloned.1.call-start = ((), (), s32[]{:S(2)}) async-start(), calls=%async_computation.11 | async-start | bytes 7864320 | tf_op jit(solution)/shard_map/all_gather | solution.py:185
  7.9 104.5 %all-gather.15.cloned.1.call-start = ((), (), s32[]{:S(2)}) async-start(), calls=%async_computation.12 | async-start | bytes 2211840 | tf_op jit(solution)/shard_map/all_gather | solution.py:200
  8.7 191.1 %all-gather.17.cloned.1.call-start = ((), (), s32[]{:S(2)}) async-start(), calls=%async_computation.13 | async-start | bytes 1327104 | tf_op jit(solution)/shard_map/all_gather | solution.py:201
  9.4 319.1 %reduce-scatter.16.cloned.1.call-start = ((), (), s32[]{:S(2)}) async-start(), calls=%async_computation.14 | async-start | bytes 15728640 | tf_op jit(solution)/shard_map/reduce_scatter | solution.py:214
  208.1 192.3 %all-gather.27.cloned.1.call-start = ((), (), s32[]{:S(2)}) async-start(), calls=%async_computation.20 | async-start | bytes 7864320 | tf_op jit(solution)/shard_map/all_gather | solution.py:186
  208.7 125.6 %copy-start.36 = (s32[2048,2]{0,1:T(2,128)S(1)}, s32[2048,2]{0,1:T(2,128)}, u32[]{:S(2)}) copy-start(s32[2048,2]{0,1:T(2,128)} %param.20) | copy-start | bytes 49156
  208.7 264.2 %all-gather.19.cloned.1.call-start = ((), (), s32[]{:S(2)}) async-start(), calls=%async_computation.15 | async-start | bytes 7864320 | tf_op jit(solution)/shard_map/all_gather | solution.py:216
  332.0 296.6 %all-gather.21.cloned.1.call-start = ((), (), s32[]{:S(2)}) async-start(), calls=%async_computation.16 | async-start | bytes 14155776 | tf_op jit(solution)/shard_map/all_gather | solution.py:224
  332.8 375.0 %all-gather.23.cloned.1.call-start = ((), (), s32[]{:S(2)}) async-start(), calls=%async_computation.17 | async-start | bytes 14155776 | tf_op jit(solution)/shard_map/all_gather | solution.py:225
  333.5 490.8 %all-gather.25.cloned.1.call-start = ((), (), s32[]{:S(2)}) async-start(), calls=%async_computation.18 | async-start | bytes 14155776 | tf_op jit(solution)/shard_map/all_gather | solution.py:226
  334.2 1501.2 %reduce-scatter.34.cloned.1.call-start = ((), (), s32[]{:S(2)}) async-start(), calls=%async_computation.29 | async-start | bytes 1310720
  343.6 133.3 %copy-start.29 = (f32[1536]{0:T(1024)}, f32[1536]{0:T(1024)S(1)}, u32[]{:S(2)}) copy-start(f32[1536]{0:T(1024)S(1)} %reshape.460) | copy-start | bytes 18436
  357.8 184.2 %copy-start.21 = (bf16[1536,16]{0,1:T(8,128)(2,1)}, bf16[1536,16]{0,1:T(8,128)(2,1)S(1)}, u32[]{:S(2)}) copy-start(bf16[1536,16]{0,1:T(8,128)(2,1)S(1)} %reshape.458) | copy-start | bytes 147460
  840.9 210.2 %copy-start.42 = (s32[2048]{0:T(1024)S(1)}, s32[2048]{0:T(1024)}, u32[]{:S(2)}) copy-start(s32[2048]{0:T(1024)} %get-tuple-element.437) | copy-start | bytes 24580
  1159.8 564.2 %copy-start.43 = (s32[2048]{0:T(1024)S(1)}, s32[2048]{0:T(1024)}, u32[]{:S(2)}) copy-start(s32[2048]{0:T(1024)} %get-tuple-element.437) | copy-start | bytes 24580
  1809.0 150.3 %reduce-scatter.20.cloned.1.call-start = ((), (), s32[]{:S(2)}) async-start(), calls=%async_computation.21 | async-start | bytes 15728640 | tf_op jit(solution)/shard_map/reduce_scatter | solution.py:334
  1834.0 131.2 %copy-start.7 = (bf16[512,1536]{1,0:T(8,128)(2,1)S(1)}, bf16[512,1536]{1,0:T(8,128)(2,1)}, u32[]{:S(2)}) copy-start(bf16[512,1536]{1,0:T(8,128)(2,1)} %param.29) | copy-start | bytes 4718596
  1834.0 205.5 %all-gather.29.cloned.1.call-start = ((), (), s32[]{:S(2)}) async-start(), calls=%async_computation.22 | async-start | bytes 7864320 | tf_op jit(solution)/shard_map/all_gather | solution.py:354
  1835.5 133.7 %copy-start.66 = (f32[512]{0:T(512)}, f32[512]{0:T(512)S(1)}, u32[]{:S(2)}) copy-start(f32[512]{0:T(512)S(1)} %dynamic-slice.9) | copy-start | bytes 6148
  1969.2 271.1 %reduce-scatter.36.cloned.1.call-start = ((), (), s32[]{:S(2)}) async-start(), calls=%async_computation.30 | async-start | bytes 884736
  1985.3 256.6 %reduce-scatter.18.cloned.1.call-start = ((), (), s32[]{:S(2)}) async-start(), calls=%async_computation.19 | async-start | bytes 7864320 | tf_op jit(solution)/shard_map/reduce_scatter | solution.py:267
  1986.1 283.6 %all-reduce.10.cloned.1.call-start = ((), (), s32[]{:S(2)}) async-start(), calls=%async_computation.31 | async-start | bytes 196608
  2218.5 176.6 %reduce-scatter.22.cloned.1.call-start = ((), (), s32[]{:S(2)}) async-start(), calls=%async_computation.23 | async-start | bytes 15728640 | tf_op jit(solution)/shard_map/reduce_scatter | solution.py:385
  2219.1 215.2 %reduce-scatter.26.cloned.1.call-start = ((), (), s32[]{:S(2)}) async-start(), calls=%async_computation.25 | async-start | bytes 2654208 | tf_op jit(solution)/shard_map/reduce_scatter | solution.py:397
  2227.6 256.5 %reduce-scatter.24.cloned.1.call-start = ((), (), s32[]{:S(2)}) async-start(), calls=%async_computation.24 | async-start | bytes 4423680 | tf_op jit(solution)/shard_map/reduce_scatter | solution.py:396
  2236.9 495.5 %reduce-scatter.28.cloned.1.call-start = ((), (), s32[]{:S(2)}) async-start(), calls=%async_computation.26 | async-start | bytes 28311552 | tf_op jit(solution)/shard_map/reduce_scatter | solution.py:360
  2237.7 743.2 %reduce-scatter.30.cloned.1.call-start = ((), (), s32[]{:S(2)}) async-start(), calls=%async_computation.27 | async-start | bytes 28311552 | tf_op jit(solution)/shard_map/reduce_scatter | solution.py:361
  2238.2 991.2 %reduce-scatter.32.cloned.1.call-start = ((), (), s32[]{:S(2)}) async-start(), calls=%async_computation.28 | async-start | bytes 28311552 | tf_op jit(solution)/shard_map/reduce_scatter | solution.py:362
  2241.9 156.7 %copy-start.3 = (f32[512,1536]{1,0:T(8,128)S(1)}, f32[512,1536]{1,0:T(8,128)}, u32[]{:S(2)}) copy-start(f32[512,1536]{1,0:T(8,128)} %copy-done.2) | copy-start | bytes 9437188
  2241.9 156.7 %copy-start.31 = (f32[1536]{0:T(1024)S(1)}, f32[1536]{0:T(1024)}, u32[]{:S(2)}) copy-start(f32[1536]{0:T(1024)} %copy-done.29) | copy-start | bytes 18436
  2241.9 156.7 %copy-start.67 = (f32[512]{0:T(512)S(1)}, f32[512]{0:T(512)}, u32[]{:S(2)}) copy-start(f32[512]{0:T(512)} %copy-done.66) | copy-start | bytes 6148
  2241.9 156.7 %copy-start.69 = (f32[512]{0:T(512)S(1)}, f32[512]{0:T(512)}, u32[]{:S(2)}) copy-start(f32[512]{0:T(512)} %copy-done.68) | copy-start | bytes 6148
  (75 other events, 1444.7 us)
Sparse Core Ops, SparseCore 0:
  9.9 72.8 all-gather.12
  84.4 28.0 all-gather.14
  114.1 22.1 all-gather.16
  208.2 120.2 reduce-scatter.15
  330.2 70.1 all-gather.26
  402.7 70.1 all-gather.18
  474.5 116.7 all-gather.20
  592.8 114.9 all-gather.22
  709.4 114.9 all-gather.24
  1809.1 25.9 reduce-scatter.33
  1838.5 120.6 reduce-scatter.19
  1969.3 70.1 all-gather.28
  2041.9 31.6 reduce-scatter.35
  2076.4 68.3 reduce-scatter.17
  2218.7 50.9 all-reduce.9
  2272.9 122.1 reduce-scatter.21
  2398.0 36.2 reduce-scatter.25
  2437.2 46.8 reduce-scatter.23
  2487.1 245.3 reduce-scatter.27
  2735.3 245.5 reduce-scatter.29
  2983.9 245.5 reduce-scatter.31
where the time goes:
time: 3250 us; the launch traced here: 3240 us
  waiting for transfers between devices  1580 us (49%)
  local copies, waits for them, and re-layouts  533 us (16%)
  matrix products  495 us (15%)
  other arithmetic  436 us (13%)
  loops' own time  123 us (4%)
  blocking collectives  57.2 us (2%)
    dynamic_update_slice x88, other arithmetic, add_blocks(): lax.dynamic_update_index_in_dim(total, current + blocks[index], owners[in...  254 us
    reduce_scatter x1, waiting for transfers between devices, local(): lax.psum_scatter(grad_down, 'wide', scatter_dimension=1, tiled=True)  249 us
    reduce_scatter x1, waiting for transfers between devices, local(): lax.psum_scatter(grad_up, 'wide', scatter_dimension=1, tiled=True)  248 us
    reduce_scatter x1, waiting for transfers between devices, local(): lax.psum_scatter(grad_gate, 'wide', scatter_dimension=1, tiled=True)  248 us
    reduce_scatter x1, waiting for transfers between devices, local(): lax.psum_scatter(input_part, 'narrow', scatter_dimension=0, tiled=True)  124 us
    reduce_scatter x1, waiting for transfers between devices, local(): lax.psum_scatter(expert_back, 'narrow', scatter_dimension=0, tiled=True)  123 us
    reduce_scatter x1, waiting for transfers between devices, local(): lax.psum_scatter(branch_part, 'narrow', scatter_dimension=0, tiled=True)  120 us
    all_gather x1, waiting for transfers between devices, local(): lax.all_gather(down_weight, 'wide', axis=1, tiled=True)  117 us
  transfers between devices with their start and end apart: 21, of which 16 were waited for; matrix products, arithmetic and copies ran while one was open for 18% of the time, Pallas kernels for 0%

commit v1 on v0

v1 whole, which is shorter than its diff:
```python
import functools

import jax
import jax.numpy as jnp
from jax import lax
from jax.experimental import pallas as pl
from jax.experimental.pallas import tpu as pltpu
from jax.sharding import PartitionSpec as P

QUERY_HEADS = 24
KEY_VALUE_HEADS = 8
HEAD_SIZE = 64
E = 16
TOPK = 2
SEQUENCE_LENGTH = 2048
BLOCK = 256
QB = 256
KB = 256
LANES = 128
PITCH = 16
UNROLL = 8
CHUNKS = (4, 4, 4, 4)
EPSILON = 1e-05
F32 = jnp.float32
BF16 = jnp.bfloat16

def stack_heads(ref, row, first, heads):
    return jnp.concatenate(
        [ref[row + h * HEAD_SIZE : row + (h + 1) * HEAD_SIZE, pl.ds(first, QB)] for h in range(heads)], axis=1
    )

def rows_of(block):
    return block.astype(jnp.float32).T.astype(jnp.bfloat16)

def forward_kernel(heads, qkv_ref, out_ref, total_ref, key_ref):
    index = pl.program_id(1)
    first = pl.multiple_of(index * QB, QB)
    key_row = heads * HEAD_SIZE
    value_row = key_row + HEAD_SIZE
    @pl.when(index == 0)
    def _():
        key_ref[...] = rows_of(qkv_ref[key_row:value_row, :])
    queries = stack_heads(qkv_ref, 0, first, heads) * jnp.bfloat16(0.125)
    lanes = heads * QB

    def step(block, carry, masked):
        highest, denominator, mixed = carry
        start = pl.multiple_of(block * KB, KB)
        scores = jnp.dot(key_ref[pl.ds(start, KB), :], queries, preferred_element_type=jnp.float32)
        if masked:
            key_at = lax.broadcasted_iota(jnp.int32, (KB, QB), 0)
            query_at = lax.broadcasted_iota(jnp.int32, (KB, QB), 1)
            seen = jnp.concatenate([key_at <= query_at] * heads, axis=1)
            scores = jnp.where(seen, scores, -1e30)
        raised_to = jnp.maximum(highest, jnp.max(scores, axis=0, keepdims=True))
        shrink = jnp.exp(highest - raised_to)
        raised = jnp.exp(scores - raised_to)
        denominator = denominator * shrink + jnp.sum(raised, axis=0, keepdims=True)
        mixed = mixed * shrink + jnp.dot(
            qkv_ref[value_row : value_row + HEAD_SIZE, pl.ds(start, KB)], raised.astype(jnp.bfloat16),
            preferred_element_type=jnp.float32)
        return raised_to, denominator, mixed

    carry = (jnp.full((1, lanes), -1e30, jnp.float32), jnp.zeros((1, lanes), jnp.float32), jnp.zeros((HEAD_SIZE, lanes), jnp.float32))
    carry = lax.fori_loop(0, index, lambda b, c: step(b, c, False), carry)
    highest, denominator, mixed = step(index, carry, True)
    mixed = (mixed / denominator).astype(jnp.bfloat16)
    for h in range(heads):
        out_ref[h * HEAD_SIZE : (h + 1) * HEAD_SIZE, :] = mixed[:, h * QB : (h + 1) * QB]
    total_ref[0, 0] = highest + jnp.log(denominator)

def attend_forward(qkv, groups, heads):
    tokens = qkv.shape[1]
    blocks = tokens // QB
    rows = (heads + 2) * HEAD_SIZE
    flops = groups * heads * tokens * tokens * HEAD_SIZE * 2
    return pl.pallas_call(
        functools.partial(forward_kernel, heads),
        grid=(groups, blocks),
        in_specs=[pl.BlockSpec((rows, tokens), lambda g, i: (g, 0))],
        out_specs=[pl.BlockSpec((heads * HEAD_SIZE, QB), lambda g, i: (g, i)),
                   pl.BlockSpec((1, 1, 1, heads * QB), lambda g, i: (g, i, 0, 0))],
        out_shape=[jax.ShapeDtypeStruct((groups * heads * HEAD_SIZE, tokens), jnp.bfloat16),
                   jax.ShapeDtypeStruct((groups, blocks, 1, heads * QB), jnp.float32)],
        scratch_shapes=[pltpu.VMEM((tokens, HEAD_SIZE), jnp.bfloat16)],
        cost_estimate=pl.CostEstimate(flops=flops * 4, bytes_accessed=qkv.size * 4, transcendentals=0),
        compiler_params=pltpu.CompilerParams(vmem_limit_bytes=32 << 20),
    )(qkv)

def backward_kernel(heads, qkv_ref, out_ref, total_ref, grad_ref, result_ref, key_ref, value_ref, grad_key_ref, grad_value_ref):
    index = pl.program_id(1)
    first = pl.multiple_of(index * QB, QB)
    key_row = heads * HEAD_SIZE
    value_row = key_row + HEAD_SIZE
    @pl.when(index == 0)
    def _():
        key_ref[...] = rows_of(qkv_ref[key_row:value_row, :])
        value_ref[...] = rows_of(qkv_ref[value_row : value_row + HEAD_SIZE, :])
        grad_key_ref[...] = jnp.zeros_like(grad_key_ref)
        grad_value_ref[...] = jnp.zeros_like(grad_value_ref)
    queries = stack_heads(qkv_ref, 0, first, heads) * jnp.bfloat16(0.125)
    grads = stack_heads(grad_ref, 0, 0, heads)
    outs = stack_heads(out_ref, 0, 0, heads)
    centre = jnp.sum(grads.astype(jnp.float32) * outs.astype(jnp.float32), axis=0, keepdims=True)
    totals = total_ref[0, 0]
    query_rows = rows_of(queries)
    grad_rows = rows_of(grads)

    def step(block, grad_query, masked):
        start = pl.multiple_of(block * KB, KB)
        keys = key_ref[pl.ds(start, KB), :]
        scores = jnp.dot(keys, queries, preferred_element_type=jnp.float32)
        probs = jnp.exp(scores - totals)
        if masked:
            key_at = lax.broadcasted_iota(jnp.int32, (KB, QB), 0)
            query_at = lax.broadcasted_iota(jnp.int32, (KB, QB), 1)
            seen = jnp.concatenate([key_at <= query_at] * heads, axis=1)
            probs = jnp.where(seen, probs, 0.0)
        grad_probs = jnp.dot(value_ref[pl.ds(start, KB), :], grads, preferred_element_type=jnp.float32)
        grad_scores = (probs * (grad_probs - centre)).astype(jnp.bfloat16)
        grad_value_ref[pl.ds(start, KB), :] += jnp.dot(probs.astype(jnp.bfloat16), grad_rows, preferred_element_type=jnp.float32)
        grad_key_ref[pl.ds(start, KB), :] += jnp.dot(grad_scores, query_rows, preferred_element_type=jnp.float32)
        return grad_query + jnp.dot(qkv_ref[key_row:value_row, pl.ds(start, KB)], grad_scores, preferred_element_type=jnp.float32)

    grad_query = lax.fori_loop(0, index, lambda b, c: step(b, c, False), jnp.zeros((HEAD_SIZE, heads * QB), jnp.float32))
    grad_query = (step(index, grad_query, True) * 0.125).astype(jnp.bfloat16)
    for h in range(heads):
        result_ref[h * HEAD_SIZE : (h + 1) * HEAD_SIZE, pl.ds(first, QB)] = grad_query[:, h * QB : (h + 1) * QB]
    @pl.when(index == pl.num_programs(1) - 1)
    def _():
        result_ref[key_row:value_row, :] = grad_key_ref[...].T.astype(jnp.bfloat16)
        result_ref[value_row : value_row + HEAD_SIZE, :] = grad_value_ref[...].T.astype(jnp.bfloat16)

def attend_backward(qkv, out, totals, grad, groups, heads):
    tokens = qkv.shape[1]
    blocks = tokens // QB
    rows = (heads + 2) * HEAD_SIZE
    flops = groups * heads * tokens * tokens * HEAD_SIZE * 5
    return pl.pallas_call(
        functools.partial(backward_kernel, heads),
        grid=(groups, blocks),
        in_specs=[pl.BlockSpec((rows, tokens), lambda g, i: (g, 0)),
                  pl.BlockSpec((heads * HEAD_SIZE, QB), lambda g, i: (g, i)),
                  pl.BlockSpec((1, 1, 1, heads * QB), lambda g, i: (g, i, 0, 0)),
                  pl.BlockSpec((heads * HEAD_SIZE, QB), lambda g, i: (g, i))],
        out_specs=pl.BlockSpec((rows, tokens), lambda g, i: (g, 0)),
        out_shape=jax.ShapeDtypeStruct((groups * rows, tokens), jnp.bfloat16),
        scratch_shapes=[pltpu.VMEM((tokens, HEAD_SIZE), jnp.bfloat16), pltpu.VMEM((tokens, HEAD_SIZE), jnp.bfloat16),
                        pltpu.VMEM((tokens, HEAD_SIZE), jnp.float32), pltpu.VMEM((tokens, HEAD_SIZE), jnp.float32)],
        cost_estimate=pl.CostEstimate(flops=flops * 4, bytes_accessed=qkv.size * 8, transcendentals=0),
        compiler_params=pltpu.CompilerParams(vmem_limit_bytes=40 << 20),
    )(qkv, out, totals, grad)


def arrange(experts_of):
    tokens = experts_of.shape[0]
    assigned = tokens * TOPK
    flat_ids = experts_of.reshape(assigned)
    one_hot = (flat_ids[:, None] == jnp.arange(E, dtype=jnp.int32)[None, :]).astype(jnp.int32)
    counts = jnp.sum(one_hot, axis=0, dtype=jnp.int32)
    blocks = jnp.maximum((counts + BLOCK - 1) // BLOCK, 1)
    block_ends = jnp.cumsum(blocks, dtype=jnp.int32)
    starts = (block_ends - blocks) * BLOCK
    before = jnp.cumsum(one_hot, axis=0, dtype=jnp.int32) - one_hot
    slot_of = jnp.sum((before + starts[None, :]) * one_hot, axis=1, dtype=jnp.int32)
    slots = assigned + E * BLOCK
    slot_token = (
        jnp.full((slots,), tokens, jnp.int32)
        .at[slot_of]
        .set(jnp.arange(assigned, dtype=jnp.int32) // TOPK)
    )
    firsts = jnp.arange(slots // BLOCK, dtype=jnp.int32)
    later = (firsts[:, None] >= block_ends[None, :]).astype(jnp.int32)
    block_expert = jnp.minimum(jnp.sum(later, axis=1, dtype=jnp.int32), E - 1)
    return slot_token, block_expert, block_ends


def row_at(index):
    return pl.ds(pl.multiple_of(index * PITCH, PITCH), PITCH)


def dispatch_kernel(gated, token_ref, expert_ref, live_ref, source_ref, *refs):
    if gated:
        weight_ref, out_ref, gate_ref, held, moved = refs
    else:
        out_ref, held, moved = refs
    step = pl.program_id(0)
    tokens, width = source_ref.shape
    parts = width // LANES

    @pl.when(step == 0)
    def _():
        held[tokens * PITCH : (tokens + 1) * PITCH, :] = jnp.zeros((PITCH, LANES), F32)
        for first in range(0, tokens, BLOCK):
            for part in range(parts):
                held[pl.ds(first * PITCH + part, BLOCK, stride=PITCH), :] = source_ref[
                    first : first + BLOCK, part * LANES : (part + 1) * LANES
                ].astype(F32)
            if gated:
                held[pl.ds(first * PITCH + parts, BLOCK, stride=PITCH), :] = weight_ref[
                    first : first + BLOCK, :
                ]

    @pl.when(step < live_ref[0])
    def _():
        def move(group, carry):
            base = group * UNROLL
            for j in range(UNROLL):
                moved[row_at(base + j), :] = held[row_at(token_ref[step * BLOCK + base + j]), :]
            return carry

        lax.fori_loop(0, BLOCK // UNROLL, move, 0)
        for part in range(parts):
            out_ref[:, part * LANES : (part + 1) * LANES] = moved[
                pl.ds(part, BLOCK, stride=PITCH), :
            ].astype(BF16)
        if gated:
            lanes = lax.broadcasted_iota(jnp.int32, (BLOCK, LANES), 1)
            spare = moved[pl.ds(parts, BLOCK, stride=PITCH), :]
            own = jnp.where(lanes == expert_ref[step], spare, 0.0)
            gate_ref[...] = jnp.sum(own, axis=1, keepdims=True)


def dispatch(source, weights, slot_token, block_expert, live):
    tokens, width = source.shape
    slots = slot_token.shape[0]
    gated = weights is not None
    at = lambda i, t, e, n: (jnp.minimum(i, n[0] - 1), 0)
    rows = pl.BlockSpec((BLOCK, width), at)
    column = pl.BlockSpec((BLOCK, 1), at)

    def whole(columns):
        return pl.BlockSpec((tokens, columns), lambda i, t, e, n: (0, 0), pipeline_mode=pl.Buffered(1))

    out = jax.ShapeDtypeStruct((slots, width), BF16)
    gate = jax.ShapeDtypeStruct((slots, 1), F32)
    return pl.pallas_call(
        functools.partial(dispatch_kernel, gated),
        grid_spec=pltpu.PrefetchScalarGridSpec(
            num_scalar_prefetch=3,
            grid=(slots // BLOCK,),
            in_specs=[whole(width), whole(LANES)] if gated else [whole(width)],
            out_specs=[rows, column] if gated else rows,
            scratch_shapes=[
                pltpu.VMEM(((tokens + 1) * PITCH, LANES), F32),
                pltpu.VMEM((BLOCK * PITCH, LANES), F32),
            ],
        ),
        out_shape=[out, gate] if gated else out,
        cost_estimate=pl.CostEstimate(
            flops=20 * 10**9, bytes_accessed=24 * BLOCK * width * 2, transcendentals=0
        ),
        compiler_params=pltpu.CompilerParams(vmem_limit_bytes=48 << 20),
    )(*((slot_token, block_expert, live, source) + ((weights,) if gated else ())))


def expert_kernel(
    span_ref,
    expert_ref,
    token_ref,
    row_ref,
    cot_ref,
    gate_ref,
    weight_ref,
    out_ref,
    back_ref,
    score_ref,
    grad_ref,
    gate_sum,
    up_sum,
    down_sum,
    out_sum,
    back_sum,
    moved,
    staging,
    sems,
):
    step = pl.program_id(0)
    total = span_ref[1]
    block = span_ref[0] + jnp.minimum(step, total - 1)
    expert = expert_ref[block]
    width = row_ref.shape[1]
    parts = width // LANES
    tokens = out_sum.shape[0] // PITCH - 1
    following = expert_ref[jnp.minimum(block + 1, expert_ref.shape[0] - 1)]
    closing = jnp.logical_or(step == total - 1, following != expert)

    @pl.when(step == 0)
    def _():
        for ref in (out_sum, back_sum, moved, gate_sum, up_sum, down_sum):
            ref[...] = jnp.zeros_like(ref)

    @pl.when(step < total)
    def _():
        rows = row_ref[...]
        cots = cot_ref[...]
        gates = gate_ref[...]
        gate_weight = weight_ref[0, 0]
        up_weight = weight_ref[1, 0]
        down_weight = weight_ref[2, 0]
        gate_val = jnp.dot(rows, gate_weight, preferred_element_type=F32)
        up_val = jnp.dot(rows, up_weight, preferred_element_type=F32)
        raw_grad = jnp.dot(cots, down_weight, preferred_element_type=F32)
        sigma = jax.nn.sigmoid(gate_val)
        silu_val = gate_val * sigma
        active = (silu_val * up_val).astype(BF16).astype(F32)
        scores = jnp.sum(active * raw_grad, axis=1, keepdims=True)
        act_grad = raw_grad * gates
        gate_d = (act_grad * up_val * sigma * (1.0 + gate_val * (1.0 - sigma))).astype(BF16)
        up_d = (act_grad * silu_val).astype(BF16)
        weighted = (active * gates).astype(BF16)
        over_rows = (((0,), (0,)), ((), ()))
        over_hidden = (((1,), (1,)), ((), ()))
        gate_sum[...] += lax.dot_general(gate_d, rows, over_rows, preferred_element_type=F32)
        up_sum[...] += lax.dot_general(up_d, rows, over_rows, preferred_element_type=F32)
        down_sum[...] += lax.dot_general(weighted, cots, over_rows, preferred_element_type=F32)

        def spread(value):
            for part in range(parts):
                moved[pl.ds(part, BLOCK, stride=PITCH), :] = value[:, part * LANES : (part + 1) * LANES]

        def combine(sum_ref):
            def add(group, carry):
                base = group * UNROLL
                at = [row_at(token_ref[block * BLOCK + base + j]) for j in range(UNROLL)]
                new = [sum_ref[at[j], :] + moved[row_at(base + j), :] for j in range(UNROLL)]
                for j in range(UNROLL):
                    sum_ref[at[j], :] = new[j]
                return carry

            lax.fori_loop(0, BLOCK // UNROLL, add, 0)

        spread(lax.dot_general(weighted, down_weight, over_hidden, preferred_element_type=F32))
        combine(out_sum)
        spread(
            lax.dot_general(gate_d, gate_weight, over_hidden, preferred_element_type=F32)
            + lax.dot_general(up_d, up_weight, over_hidden, preferred_element_type=F32)
        )
        lanes = lax.broadcasted_iota(jnp.int32, (BLOCK, LANES), 1)
        moved[pl.ds(parts, BLOCK, stride=PITCH), :] = jnp.where(lanes == expert, scores, 0.0)
        combine(back_sum)

        @pl.when(closing)
        def _():
            for index, ref in enumerate((gate_sum, up_sum, down_sum)):
                grad_ref[index, 0] = ref[...].T.astype(BF16)
                ref[...] = jnp.zeros_like(ref)

    @pl.when(step == total - 1)
    def _():
        for first in range(0, tokens, BLOCK):
            score_ref[first : first + BLOCK, :] = back_sum[
                pl.ds(first * PITCH + parts, BLOCK, stride=PITCH), :
            ]

        jobs = [
            (first, source, target)
            for first in range(0, tokens, BLOCK)
            for source, target in ((out_sum, out_ref), (back_sum, back_ref))
        ]

        def copy(number):
            first, _, target = jobs[number]
            slot = number % 2
            return pltpu.make_async_copy(
                staging.at[slot], target.at[pl.ds(first, BLOCK), :], sems.at[slot]
            )

        for number, (first, source, _) in enumerate(jobs):
            if number >= 2:
                copy(number - 2).wait()
            for part in range(parts):
                staging[number % 2, :, part * LANES : (part + 1) * LANES] = source[
                    pl.ds(first * PITCH + part, BLOCK, stride=PITCH), :
                ].astype(BF16)
            copy(number).start()
        copy(len(jobs) - 2).wait()
        copy(len(jobs) - 1).wait()


def run_experts(span, slot_token, block_expert, rows, cots, gates, weights, low, tokens):
    width = rows.shape[1]
    experts, hidden = weights.shape[1], weights.shape[3]
    index = lambda i, s: s[0] + jnp.minimum(i, s[1] - 1)
    at = lambda i, s, e, t: (index(i, s), 0)
    pick = pl.BlockSpec(
        (3, 1, width, hidden), lambda i, s, e, t: (0, e[index(i, s)] - low, 0, 0)
    )
    anywhere = pl.BlockSpec(memory_space=pl.ANY)
    block_count = experts * 3 // 2
    return pl.pallas_call(
        expert_kernel,
        grid_spec=pltpu.PrefetchScalarGridSpec(
            num_scalar_prefetch=3,
            grid=(tokens * TOPK // BLOCK + experts,),
            in_specs=[
                pl.BlockSpec((BLOCK, width), at),
                pl.BlockSpec((BLOCK, width), at),
                pl.BlockSpec((BLOCK, 1), at),
                pick,
            ],
            out_specs=[
                anywhere,
                anywhere,
                pl.BlockSpec((tokens, LANES), lambda i, s, e, t: (0, 0)),
                pick,
            ],
            scratch_shapes=[pltpu.VMEM((hidden, width), F32)] * 3
            + [pltpu.VMEM(((tokens + 1) * PITCH, LANES), F32)] * 2
            + [
                pltpu.VMEM((BLOCK * PITCH, LANES), F32),
                pltpu.VMEM((2, BLOCK, width), BF16),
                pltpu.SemaphoreType.DMA((2,)),
            ],
        ),
        out_shape=[
            jax.ShapeDtypeStruct((tokens, width), BF16),
            jax.ShapeDtypeStruct((tokens, width), BF16),
            jax.ShapeDtypeStruct((tokens, LANES), F32),
            jax.ShapeDtypeStruct(weights.shape, BF16),
        ],
        cost_estimate=pl.CostEstimate(
            flops=block_count * 2 * BLOCK * width * hidden * 9 * 3,
            bytes_accessed=weights.size * 4 + block_count * BLOCK * width * 4,
            transcendentals=0,
        ),
        compiler_params=pltpu.CompilerParams(vmem_limit_bytes=62 << 20),
    )(span, block_expert, slot_token, rows, cots, gates, weights)


def swap(value, bit):
    count = lax.axis_size("narrow")
    return lax.ppermute(value, "narrow", [(index, index ^ bit) for index in range(count)])


def gather_rows(value):
    count = lax.axis_size("narrow")
    if count != 4:
        return lax.all_gather(value, "narrow", axis=0, tiled=True)
    me = lax.axis_index("narrow")
    rows = value.shape[0]
    half = rows // 2
    one = swap(value, 1)
    two = swap(value, 2)
    far_low = swap(two[:half], 1)
    far_high = swap(one[half:], 2)
    full = jnp.zeros((count * rows,) + value.shape[1:], value.dtype)
    for piece, other, offset in (
        (value, 0, 0),
        (one, 1, 0),
        (two, 2, 0),
        (far_low, 3, 0),
        (far_high, 3, half),
    ):
        full = lax.dynamic_update_slice_in_dim(full, piece, (me ^ other) * rows + offset, 0)
    return full


def sum_rows(part):
    count = lax.axis_size("narrow")
    if count != 4:
        low = part.astype(BF16)
        return lax.psum_scatter(low, "narrow", scatter_dimension=0, tiled=True).astype(F32)
    me = lax.axis_index("narrow")
    rows = part.shape[0] // count
    half = rows // 2

    def block(other, offset):
        return lax.dynamic_slice_in_dim(part, (me ^ other) * rows + offset, half, 0)

    def send(pieces, bit):
        return swap(jnp.concatenate([piece.astype(BF16) for piece in pieces], axis=0), bit)

    low = send([block(1, 0), block(3, 0)], 1).astype(F32)
    high = send([block(2, half), block(3, half)], 2).astype(F32)
    low_far = send([block(2, 0).astype(F32) + low[half:]], 2).astype(F32)
    high_far = send([block(1, half).astype(F32) + high[half:]], 1).astype(F32)
    return jnp.concatenate(
        [
            block(0, 0).astype(F32) + low[:half] + low_far,
            block(0, half).astype(F32) + high[:half] + high_far,
        ],
        axis=0,
    )


def local(
    block_input,
    routes,
    first_gain,
    query_key_value_weight,
    output_weight,
    second_gain,
    router_weight,
    gate_weight,
    up_weight,
    down_weight,
    cotangent,
):
    row_part, width = block_input.shape
    me = lax.axis_index("narrow")
    row_offset = me * row_part
    gain_part = first_gain.shape[0]
    tokens = routes.shape[0]
    heads = QUERY_HEADS // KEY_VALUE_HEADS
    head_columns = query_key_value_weight.shape[1]
    groups = head_columns // ((heads + 2) * HEAD_SIZE)

    def own_rows(value):
        return lax.dynamic_slice_in_dim(value, row_offset, row_part, 0)

    inputs = gather_rows(block_input)
    gains = lax.all_gather(
        jnp.stack([first_gain, second_gain]), "narrow", axis=1, tiled=True
    ).astype(F32)
    gain_one, gain_two = gains[0], gains[1]
    router_padded = jnp.pad(router_weight, ((0, 0), (0, LANES - E)))
    input_router = lax.all_gather(
        jnp.concatenate([query_key_value_weight, router_padded], axis=1), "wide", axis=0, tiled=True
    )
    input_full = input_router[:, :head_columns]
    router_full = input_router[:, head_columns : head_columns + E]
    output_full = lax.all_gather(output_weight, "wide", axis=1, tiled=True)
    lows = [sum(CHUNKS[:index]) for index in range(len(CHUNKS))]
    chunk_weights = []
    for low, size in zip(lows, CHUNKS):
        packed = jnp.stack([w[low : low + size] for w in (gate_weight, up_weight, down_weight)])
        chunk_weights.append(lax.all_gather(packed, "wide", axis=2, tiled=True))
    slot_token, block_expert, block_ends = arrange(routes)

    x_full = inputs.astype(F32)
    scale_one = lax.rsqrt(jnp.mean(x_full * x_full, axis=1, keepdims=True) + EPSILON)
    normed_one = x_full * scale_one
    attn_in = (normed_one * gain_one).astype(BF16)
    late_cotangent, _ = lax.optimization_barrier((cotangent, inputs))
    cot_full = gather_rows(late_cotangent)
    projected = jnp.einsum(
        "td,dc->ct", attn_in, input_full, preferred_element_type=F32
    ).astype(BF16)
    mixed, log_totals = attend_forward(projected, groups, heads)
    branch_part = jnp.einsum("ct,cd->td", mixed, output_full, preferred_element_type=F32)
    middle_own = block_input.astype(F32) + sum_rows(branch_part)
    middle = gather_rows(middle_own.astype(BF16)).astype(F32)
    scale_two = lax.rsqrt(jnp.mean(middle * middle, axis=1, keepdims=True) + EPSILON)
    normed_two = middle * scale_two
    expert_in = (normed_two * gain_two).astype(BF16)
    logits = jnp.dot(expert_in, router_full, preferred_element_type=F32)
    picked = (routes[:, :, None] == jnp.arange(E, dtype=jnp.int32)[None, None, :]).astype(F32)
    chosen = jnp.sum(picked * logits[:, None, :], axis=2)
    gates = jax.nn.softmax(chosen, axis=1)
    gate_lanes = jnp.pad(jnp.sum(picked * gates[:, :, None], axis=1), ((0, 0), (0, LANES - E)))
    live = block_ends[E - 1 :]
    cot_rows = dispatch(cot_full, None, slot_token, block_expert, live)
    rows, slot_gates = dispatch(expert_in, gate_lanes, slot_token, block_expert, live)

    outs, backs, scores, grads = [], [], [], []
    for low, size, weights in zip(lows, CHUNKS, chunk_weights):
        first = block_ends[low - 1 : low] if low else jnp.zeros((1,), jnp.int32)
        count = block_ends[low + size - 1 : low + size] - first
        out, back, score, grad = run_experts(
            jnp.concatenate([first, count]), slot_token, block_expert, rows, cot_rows, slot_gates, weights, low, tokens
        )
        outs.append(out)
        backs.append(back)
        scores.append(score)
        grads.append(lax.psum_scatter(grad, "wide", scatter_dimension=2, tiled=True))

    def total(values):
        return sum(value.astype(F32) for value in values)

    expert_sum = sum_rows(total(backs))
    score_part = jnp.sum(picked * total(scores)[:, None, :E], axis=2)
    score_sum = lax.psum_scatter(score_part, "narrow", scatter_dimension=0, tiled=True)
    block_output = (middle_own + sum_rows(total(outs))).astype(BF16)

    gates_own = own_rows(gates)
    centre = jnp.sum(gates_own * score_sum, axis=1, keepdims=True)
    logit_part = gates_own * (score_sum - centre)
    logit_grad = jnp.sum(own_rows(picked) * logit_part[:, :, None], axis=1).astype(BF16)
    norm_grad = expert_sum + jnp.einsum(
        "te,de->td", logit_grad, router_full, preferred_element_type=F32
    )
    normed_two_own = own_rows(normed_two)
    row_dot = jnp.sum(norm_grad * normed_two_own * gain_two, axis=1, keepdims=True)
    gain_two_part = jnp.sum(norm_grad * normed_two_own, axis=0)
    mid_grad = cotangent.astype(F32) + own_rows(scale_two) * (
        gain_two * norm_grad - normed_two_own * row_dot / width
    )
    branch_grad = gather_rows(mid_grad.astype(BF16))
    logit_full = lax.all_gather(logit_grad, "narrow", axis=0, tiled=True)
    mixed_grad = jnp.einsum(
        "td,cd->ct", branch_grad, output_full, preferred_element_type=F32
    ).astype(BF16)
    projected_grad = attend_backward(projected, mixed, log_totals, mixed_grad, groups, heads)
    input_part = jnp.einsum("ct,dc->td", projected_grad, input_full, preferred_element_type=F32)
    grad_input_w = jnp.einsum(
        "td,ct->dc", attn_in, projected_grad, preferred_element_type=F32
    ).astype(BF16)
    grad_output_w = jnp.einsum(
        "ct,td->cd", mixed, branch_grad, preferred_element_type=F32
    ).astype(BF16)
    grad_router = jnp.einsum("td,te->de", expert_in, logit_full, preferred_element_type=F32)
    router_grad = lax.psum_scatter(grad_router, "wide", scatter_dimension=0, tiled=True)
    output_w_grad = lax.psum_scatter(grad_output_w, "wide", scatter_dimension=1, tiled=True)
    input_w_grad = lax.psum_scatter(grad_input_w, "wide", scatter_dimension=0, tiled=True)
    gain_one_part = jnp.sum(input_part * normed_one, axis=0)
    gain_pair = lax.psum(jnp.stack([gain_one_part, gain_two_part]), ("wide", "narrow"))
    gain_own = lax.dynamic_slice_in_dim(gain_pair, me * gain_part, gain_part, 1)
    input_sum = sum_rows(input_part)
    normed_one_own = own_rows(normed_one)
    input_dot = jnp.sum(input_sum * normed_one_own * gain_one, axis=1, keepdims=True)
    input_grad = mid_grad + own_rows(scale_one) * (
        gain_one * input_sum - normed_one_own * input_dot / width
    )
    gate_grad, up_grad, down_grad = (
        jnp.concatenate([grad[index] for grad in grads], axis=0).astype(F32) for index in range(3)
    )
    return (
        block_output,
        input_grad,
        gain_own[0],
        input_w_grad.astype(F32),
        output_w_grad.astype(F32),
        gain_own[1],
        router_grad,
        gate_grad,
        up_grad,
        down_grad,
    )


def solution(mesh):
    placed = (
        P(("wide", "narrow"), None),
        P("wide", None),
        P("narrow"),
        P("wide", "narrow"),
        P("narrow", "wide"),
        P("narrow"),
        P("wide", None),
        P(None, "wide", "narrow"),
        P(None, "wide", "narrow"),
        P(None, "wide", "narrow"),
        P(("wide", "narrow"), None),
    )
    return jax.shard_map(
        local,
        mesh=mesh,
        in_specs=placed,
        out_specs=(
            P(("wide", "narrow"), None),
            P(("wide", "narrow"), None),
            P("narrow"),
            P("wide", "narrow"),
            P("narrow", "wide"),
            P("narrow"),
            P("wide", None),
            P(None, "wide", "narrow"),
            P(None, "wide", "narrow"),
            P(None, "wide", "narrow"),
        ),
        check_vma=False,
    )
```

time: 3250 us -> 1350 us (0.42)
  waiting for transfers between devices: 1580 us -> 483 us
  local copies, waits for them, and re-layouts: 533 us -> 89.5 us
  matrix products: 495 us -> 56.9 us
  Pallas kernels: 0 us -> 403 us
  other arithmetic: 436 us -> 125 us
  loops' own time: 123 us -> 0 us
  blocking collectives: 57.2 us -> 126 us
  starting transfers between devices: 1.26 us -> 36.9 us
    reduce_scatter x7 -> x4, waiting for transfers between devices: 1110 us -> 238 us  [local(): lax.psum_scatter(grad, 'wide', scatter_dimension=2, tiled=True)]
    dot_general x112 -> x8, matrix products: 488 us -> 53.3 us  [the longest x1 12 us: local(): jnp.einsum('ct,dc->td', projected_grad, input_full, preferred_element_typ...]
    pallas_call x0 -> x8, Pallas kernels: none -> 403 us  [the longest x4 240 us: run_experts(): pl.pallas_call(expert_kernel, grid_spec=pltpu.PrefetchScalarGridSpec(num_...]
    all_gather x9 -> x6, waiting for transfers between devices: 353 us -> 0.09 us  [the longest x4 0.06 us: local(): chunk_weights.append(lax.all_gather(packed, 'wide', axis=2, tiled=True))]
    gather x9 -> x0, local copies, waits for them, and re-layouts: 295 us -> none  [the longest x2 59.6 us: combine_slots(): total = total + jnp.take(buffer, slots[:, 1], axis=0) * weights[:, 1:2]]
    dynamic_update_slice x88 -> x2, other arithmetic: 254 us -> 6.84 us  [gather_rows(): lax.dynamic_update_slice_in_dim(full, piece, (me ^ other) * rows + offset...]
    ppermute x0 -> x32, waiting for transfers between devices: none -> 218 us  [swap(): lax.ppermute(value, 'narrow', [(index, index ^ bit) for index in range(co...]
    another operation x2 -> x0, loops' own time: 123 us -> none  [the longest x1 63 us: local(): lax.scan(backward_step, start_carry, (rows_steps, cot_steps, weight_steps...]
  transfers between devices with their start and end apart: 21 -> 46, of which waited for: 16 -> 25; matrix products, arithmetic and copies ran while one was open for 18% -> 16% of each run, Pallas kernels for 0% -> 25%
where the time goes in v1:
time: 1350 us; the launch traced here: 1340 us
  waiting for transfers between devices  483 us (36%)
  Pallas kernels  403 us (30%)
  blocking collectives  126 us (9%)
  other arithmetic  125 us (9%)
  local copies, waits for them, and re-layouts  89.5 us (7%)
  matrix products  56.9 us (4%)
  starting transfers between devices  36.9 us (3%)
  between operations  19.3 us (1%)
    pallas_call x4, Pallas kernels, run_experts(): pl.pallas_call(expert_kernel, grid_spec=pltpu.PrefetchScalarGridSpec(num_...  240 us
    reduce_scatter x4, waiting for transfers between devices, local(): lax.psum_scatter(grad, 'wide', scatter_dimension=2, tiled=True)  238 us
    ppermute x32, waiting for transfers between devices, swap(): lax.ppermute(value, 'narrow', [(index, index ^ bit) for index in range(co...  218 us
    pallas_call x2, Pallas kernels, dispatch(): pl.pallas_call(functools.partial(dispatch_kernel, gated), grid_spec=pltpu...  76.4 us
    psum x1, blocking collectives, local(): lax.psum(jnp.stack([gain_one_part, gain_two_part]), ('wide', 'narrow'))  50.4 us
    pallas_call x1, Pallas kernels, attend_backward(): pl.pallas_call(functools.partial(backward_kernel, heads), grid=(groups, b...  48.1 us
    pallas_call x1, Pallas kernels, attend_forward(): pl.pallas_call(functools.partial(forward_kernel, heads), grid=(groups, bl...  38.2 us
    all_gather x1, blocking collectives, local(): logit_full = lax.all_gather(logit_grad, 'narrow', axis=0, tiled=True)  38 us
  transfers between devices with their start and end apart: 46, of which 25 were waited for; matrix products, arithmetic and copies ran while one was open for 16% of the time, Pallas kernels for 25%

profile of v1, /device:TPU:0, one launch (start us, length us, event | category | flops | bytes accessed | tf_op | source)
XLA Modules:
  0.0 1338.6 jit_solution(11309152713184925297)
XLA Ops:
  23.6 37.5 %all_gather.25 = bf16[2,1536]{1,0:T(2,128)(2,1)S(1)} all-gather(bf16[2,384]{1,0:T(2,128)(2,1)S(1)} %pad_maximum_fusion.14), channel_id=1, replica_groups=mesh['wide'=8,'narrow'=4] {'narrow'}, dimensions={1}, use_global_device_ids=true | all-gather | bytes 7680 | tf_op jit(solution)/shard_map/all_gather | solution.py:513
  66.9 12.0 collective-permute-done.2
  85.6 8.0 convolution_convert_fusion.1.qkv_ref
  93.6 38.2 %shard_map.186 = (bf16[384,2048]{1,0:T(8,128)(2,1)S(1)}, f32[2,8,1,768]{3,2,1,0:T(1,128)S(1)}) custom-call(bf16[640,2048]{1,0:T(8,128)(2,1)S(1)} %convolution_convert_fusion.1.qkv_ref), custom_call_target="tpu_custom_call" | custom-call | flops 12884901888 | bytes 5242880 | tf_op jit(solution)/shard_map/pallas_call | solution.py:77
  159.5 19.1 %collective-permute-done.4 = bf16[512,1536]{1,0:T(8,128)(2,1)} collective-permute-done((bf16[512,1536]{1,0:T(8,128)(2,1)}, bf16[512,1536]{1,0:T(8,128)(2,1)}, u32[]{:S(2)}, u32[]{:S(2)}) %collective-permute-start.4) | collective-permute-done | bytes 1572896 | tf_op jit(solution)/shard_map/ppermute | solution.py:433
  193.4 11.0 collective-permute-done.5
  212.5 14.9 %collective-permute-done.7 = bf16[256,1536]{1,0:T(8,128)(2,1)S(1)} collective-permute-done((bf16[256,1536]{1,0:T(8,128)(2,1)S(1)}, bf16[256,1536]{1,0:T(8,128)(2,1)S(1)}, u32[]{:S(2)}, u32[]{:S(2)}) %collective-permute-start.7) | collective-permute-done | bytes 786464 | tf_op jit(solution)/shard_map/ppermute | solution.py:433
  236.0 15.9 %scatter_custom_fusion.token_ref = s32[8192]{0:T(1024)S(1)} fusion(s32[4096]{0:T(1024)S(1)} %bitcast.101, s32[4096]{0:T(1024)S(1)} %add_select_fusion, s32[]{:T(128)} %constant.75.clone.1), kind=kCustom, calls=%fused_computation.153 | custom fusion | bytes 32772 | tf_op jit(solution)/shard_map/scatter | solution.py:170
  273.4 17.9 %collective-permute-done.15 = bf16[256,1536]{1,0:T(8,128)(2,1)S(1)} collective-permute-done((bf16[256,1536]{1,0:T(8,128)(2,1)S(1)}, bf16[256,1536]{1,0:T(8,128)(2,1)S(1)}, u32[]{:S(2)}, u32[]{:S(2)}) %collective-permute-start.15) | collective-permute-done | bytes 786464 | tf_op jit(solution)/shard_map/ppermute | solution.py:433
  295.4 37.4 %shard_map.188.cot_ref = bf16[8192,1536]{1,0:T(8,128)(2,1)} custom-call(s32[8192]{0:T(1024)S(1)} %scatter_custom_fusion.token_ref, s32[32]{0:T(128)S(1)} %broadcast_minimum_fusion.expert_ref, s32[1]{0:T(128)} %bitcast.5.live_ref, bf16[2048,1536]{1,0:T(8,128)(2,1)} %copy-done.31), custom_call_target="tpu_custom_call" | custom-call | flops 20000000000 | bytes 18874368 | tf_op jit(solution)/shard_map/pallas_call | solution.py:237
  350.7 11.7 convert_multiply_fusion
  367.7 39.0 %shard_map.187 = (bf16[8192,1536]{1,0:T(8,128)(2,1)}, f32[8192,1]{1,0:T(8,128)S(1)}) custom-call(s32[8192]{0:T(1024)S(1)} %scatter_custom_fusion.token_ref, s32[32]{0:T(128)S(1)} %broadcast_minimum_fusion.expert_ref, s32[1]{0:T(128)} %bitcast.5.live_ref, bf16[2048,1536]{1,0:T(8,128)(2,1)} %get-tuple-element.89.source_ref, f32[2048,128]{1,0:T(8,128)S(1)} %pad.9.refs_0_), custom_call_target="tpu_custom_call" | custom-call | flops 20000000000 | bytes 18874368 | tf_op jit(solution)/shard_map/pallas_call | solution.py:237
  408.7 44.6 %shard_map.189 = (bf16[2048,1536]{1,0:T(8,128)(2,1)}, bf16[2048,1536]{1,0:T(8,128)(2,1)}, f32[2048,128]{1,0:T(8,128)}, bf16[3,4,1536,256]{3,2,1,0:T(8,128)(2,1)}) custom-call(s32[2]{0:T(128)} %pad_add_fusion.span_ref, s32[32]{0:T(128)} %copy-done.4, s32[8192]{0:T(1024)} %copy-done.3, bf16[8192,1536]{1,0:T(8,128)(2,1)} %get-tuple-element.32.row_ref, ...), custom_call_target="tpu_custom_call" | custom-call | flops 32614907904 | bytes 28311552 | tf_op jit(solution)/shard_map/pallas_call | solution.py:391
  453.4 62.1 %shard_map.190 = (bf16[2048,1536]{1,0:T(8,128)(2,1)}, bf16[2048,1536]{1,0:T(8,128)(2,1)}, f32[2048,128]{1,0:T(8,128)}, bf16[3,4,1536,256]{3,2,1,0:T(8,128)(2,1)}) custom-call(s32[2]{0:T(128)} %pad_add_fusion.1.span_ref, s32[32]{0:T(128)} %copy-done.4, s32[8192]{0:T(1024)} %copy-done.3, bf16[8192,1536]{1,0:T(8,128)(2,1)} %get-tuple-element.32.row_ref, ...), custom_call_target="tpu_custom_call" | custom-call | flops 32614907904 | bytes 28311552 | tf_op jit(solution)/shard_map/pallas_call | solution.py:391
  515.5 62.1 %shard_map.191 = (bf16[2048,1536]{1,0:T(8,128)(2,1)}, bf16[2048,1536]{1,0:T(8,128)(2,1)}, f32[2048,128]{1,0:T(8,128)}, bf16[3,4,1536,256]{3,2,1,0:T(8,128)(2,1)}) custom-call(s32[2]{0:T(128)} %pad_add_fusion.2.span_ref, s32[32]{0:T(128)} %copy-done.4, s32[8192]{0:T(1024)} %copy-done.3, bf16[8192,1536]{1,0:T(8,128)(2,1)} %get-tuple-element.32.row_ref, ...), custom_call_target="tpu_custom_call" | custom-call | flops 32614907904 | bytes 28311552 | tf_op jit(solution)/shard_map/pallas_call | solution.py:391
  577.6 71.3 %shard_map.192 = (bf16[2048,1536]{1,0:T(8,128)(2,1)}, bf16[2048,1536]{1,0:T(8,128)(2,1)}, f32[2048,128]{1,0:T(8,128)}, bf16[3,4,1536,256]{3,2,1,0:T(8,128)(2,1)}) custom-call(s32[2]{0:T(128)} %pad_add_fusion.3.span_ref, s32[32]{0:T(128)} %copy-done.4, s32[8192]{0:T(1024)} %copy-done.3, bf16[8192,1536]{1,0:T(8,128)(2,1)} %get-tuple-element.32.row_ref, ...), custom_call_target="tpu_custom_call" | custom-call | flops 32614907904 | bytes 28311552 | tf_op jit(solution)/shard_map/pallas_call | solution.py:391
  649.0 9.8 convert_add_fusion
  661.4 22.2 %collective-permute-done.20 = bf16[512,1536]{1,0:T(8,128)(2,1)S(1)} collective-permute-done((bf16[512,1536]{1,0:T(8,128)(2,1)S(1)}, bf16[512,1536]{1,0:T(8,128)(2,1)S(1)}, u32[]{:S(2)}, u32[]{:S(2)}) %collective-permute-start.20) | collective-permute-done | bytes 1572896 | tf_op jit(solution)/shard_map/ppermute | solution.py:433
  706.2 23.1 %reduce-scatter.25.cloned.1.call-done = f32[512,2]{1,0:T(8,128)} async-done(((f32[2048,2]{1,0:T(8,128)}), f32[512,2]{1,0:T(8,128)}) %reduce-scatter.25.cloned.1.call-update) | async-done | bytes 4112
  747.1 38.0 %all_gather.31 = bf16[2048,16]{0,1:T(8,128)(2,1)S(1)} all-gather(bf16[512,16]{0,1:T(8,128)(2,1)S(1)} %multiply_reduce_fusion.3), channel_id=1, replica_groups=mesh['wide'=8,'narrow'=4] {'narrow'}, dimensions={0}, use_global_device_ids=true | all-gather | bytes 81920 | tf_op jit(solution)/shard_map/all_gather | solution.py:590
  809.7 7.5 convolution_convert_fusion.2
  822.9 48.1 %shard_map.193 = bf16[640,2048]{1,0:T(8,128)(2,1)S(1)} custom-call(bf16[640,2048]{1,0:T(8,128)(2,1)S(1)} %copy-done.6, bf16[384,2048]{1,0:T(8,128)(2,1)S(1)} %copy-done.2, f32[2,8,1,768]{3,2,1,0:T(1,128)S(1)} %get-tuple-element.47.total_ref, bf16[384,2048]{1,0:T(8,128)(2,1)S(1)} %fusion.3.grad_ref), custom_call_target="tpu_custom_call" | custom-call | flops 32212254720 | bytes 10485760 | tf_op jit(solution)/shard_map/pallas_call | solution.py:139
  881.0 10.5 convert_add_fusion.1
  898.9 12.0 multiply_reduce_fusion
  914.9 19.3 %collective-permute-done.16 = bf16[512,1536]{1,0:T(8,128)(2,1)} collective-permute-done((bf16[512,1536]{1,0:T(8,128)(2,1)S(1)}, bf16[512,1536]{1,0:T(8,128)(2,1)}, u32[]{:S(2)}, u32[]{:S(2)}) %collective-permute-start.16) | collective-permute-done | bytes 1572896 | tf_op jit(solution)/shard_map/ppermute | solution.py:433
  941.7 21.6 %collective-permute-done.28 = bf16[512,1536]{1,0:T(8,128)(2,1)S(1)} collective-permute-done((bf16[512,1536]{1,0:T(8,128)(2,1)S(1)}, bf16[512,1536]{1,0:T(8,128)(2,1)S(1)}, u32[]{:S(2)}, u32[]{:S(2)}) %collective-permute-start.28) | collective-permute-done | bytes 1572896 | tf_op jit(solution)/shard_map/ppermute | solution.py:433
  968.7 20.6 %collective-permute-done.17 = bf16[256,1536]{1,0:T(8,128)(2,1)S(1)} collective-permute-done((bf16[256,1536]{1,0:T(8,128)(2,1)S(1)}, bf16[256,1536]{1,0:T(8,128)(2,1)S(1)}, u32[]{:S(2)}, u32[]{:S(2)}) %collective-permute-start.17) | collective-permute-done | bytes 786464 | tf_op jit(solution)/shard_map/ppermute | solution.py:433
  1004.4 8.2 collective-permute-done.19
  1016.8 50.4 %psum.7 = f32[2,1536]{1,0:T(2,128)S(1)} all-reduce(f32[2,1536]{1,0:T(2,128)S(1)} %pad_maximum_fusion.13), channel_id=1, replica_groups=mesh['wide'=8,'narrow'=4] {'wide','narrow'}, use_global_device_ids=true, to_apply=%region_21.22 | all-reduce | flops 3072 | bytes 24576 | tf_op jit(solution)/shard_map/psum | solution.py:607
  1083.7 40.5 %reduce-scatter.19.cloned.1.call-done = bf16[3,4,192,256]{3,2,1,0:T(8,128)(2,1)} async-done(((bf16[3,4,1536,256]{3,2,1,0:T(8,128)(2,1)}), bf16[3,4,192,256]{3,2,1,0:T(8,128)(2,1)}) %reduce-scatter.19.cloned.1.call-update) | async-done | bytes 1179664 | tf_op jit(solution)/shard_map/reduce_scatter | solution.py:566
  1125.5 99.0 %reduce-scatter.21.cloned.1.call-done = bf16[3,4,192,256]{3,2,1,0:T(8,128)(2,1)} async-done(((bf16[3,4,1536,256]{3,2,1,0:T(8,128)(2,1)}), bf16[3,4,192,256]{3,2,1,0:T(8,128)(2,1)}) %reduce-scatter.21.cloned.1.call-update) | async-done | bytes 1179664 | tf_op jit(solution)/shard_map/reduce_scatter | solution.py:566
  1225.9 98.8 %reduce-scatter.23.cloned.1.call-done = bf16[3,4,192,256]{3,2,1,0:T(8,128)(2,1)} async-done(((bf16[3,4,1536,256]{3,2,1,0:T(8,128)(2,1)}), bf16[3,4,192,256]{3,2,1,0:T(8,128)(2,1)}) %reduce-scatter.23.cloned.1.call-update) | async-done | bytes 1179664 | tf_op jit(solution)/shard_map/reduce_scatter | solution.py:566
  (370 shorter events, 286.8 us)
Async XLA Ops:
  7.2 77.8 %all-gather.7.cloned.1.call-start = ((), (), s32[]{:S(2)}) async-start(), calls=%async_computation.8 | async-start | bytes 2654208 | tf_op jit(solution)/shard_map/all_gather | solution.py:518
  9.9 123.5 %all-gather.9.cloned.1.call-start = ((), (), s32[]{:S(2)}) async-start(), calls=%async_computation.9 | async-start | bytes 1327104 | tf_op jit(solution)/shard_map/all_gather | solution.py:523
  10.6 398.1 %all-gather.11.cloned.1.call-start = ((), (), s32[]{:S(2)}) async-start(), calls=%async_computation.10 | async-start | bytes 10616832 | tf_op jit(solution)/shard_map/all_gather | solution.py:528
  15.4 438.0 %all-gather.13.cloned.1.call-start = ((), (), s32[]{:S(2)}) async-start(), calls=%async_computation.11 | async-start | bytes 10616832 | tf_op jit(solution)/shard_map/all_gather | solution.py:528
  17.7 497.8 %all-gather.15.cloned.1.call-start = ((), (), s32[]{:S(2)}) async-start(), calls=%async_computation.12 | async-start | bytes 10616832 | tf_op jit(solution)/shard_map/all_gather | solution.py:528
  18.9 558.7 %all-gather.17.cloned.1.call-start = ((), (), s32[]{:S(2)}) async-start(), calls=%async_computation.13 | async-start | bytes 10616832 | tf_op jit(solution)/shard_map/all_gather | solution.py:528
  19.0 42.2 %collective-permute-start.1 = (bf16[512,1536]{1,0:T(8,128)(2,1)S(1)}, bf16[512,1536]{1,0:T(8,128)(2,1)S(1)}, u32[]{:S(2)}, u32[]{:S(2)}) collective-permute-start(bf16[512,1536]{1,0:T(8,128)(2,1)S(1)} %copy-done.18), channel_id=1, source_target_pairs={{0,2},{1,3},{2,0},{3,1},{4,6},{5,7},{6,4},{7,5},{8,10},{9,11},{10,... | collective-permute-start | bytes 4718600 | tf_op jit(solution)/shard_map/ppermute | solution.py:433
  22.0 40.4 %collective-permute-start = (bf16[512,1536]{1,0:T(8,128)(2,1)S(1)}, bf16[512,1536]{1,0:T(8,128)(2,1)}, u32[]{:S(2)}, u32[]{:S(2)}) collective-permute-start(bf16[512,1536]{1,0:T(8,128)(2,1)S(1)} %copy-done.18), channel_id=1, source_target_pairs={{0,1},{1,0},{2,3},{3,2},{4,5},{5,4},{6,7},{7,6},{8,9},{9,8},{10,11... | collective-permute-start | bytes 4718600 | tf_op jit(solution)/shard_map/ppermute | solution.py:433
  144.6 34.0 %collective-permute-start.4 = (bf16[512,1536]{1,0:T(8,128)(2,1)}, bf16[512,1536]{1,0:T(8,128)(2,1)}, u32[]{:S(2)}, u32[]{:S(2)}) collective-permute-start(bf16[512,1536]{1,0:T(8,128)(2,1)} %pad_maximum_fusion.1), channel_id=1, source_target_pairs={{0,1},{1,0},{2,3},{3,2},{4,5},{5,4},{6,7},{7,6},{8,9},{9,8},{10,11... | collective-permute-start | bytes 4718600 | tf_op jit(solution)/shard_map/ppermute | solution.py:433
  147.2 582.1 %reduce-scatter.25.cloned.1.call-start = ((), (), s32[]{:S(2)}) async-start(), calls=%async_computation.20 | async-start | bytes 1310720
  154.1 37.5 %collective-permute-start.6 = (bf16[512,1536]{1,0:T(8,128)(2,1)S(1)}, bf16[512,1536]{1,0:T(8,128)(2,1)}, u32[]{:S(2)}, u32[]{:S(2)}) collective-permute-start(bf16[512,1536]{1,0:T(8,128)(2,1)S(1)} %pad_maximum_fusion.2), channel_id=1, source_target_pairs={{0,2},{1,3},{2,0},{3,1},{4,6},{5,7},{6,4},{7,5},{8,10},{9,11},{10,... | collective-permute-start | bytes 4718600 | tf_op jit(solution)/shard_map/ppermute | solution.py:433
  207.8 44.2 %collective-permute-start.13 = (bf16[512,1536]{1,0:T(8,128)(2,1)}, bf16[512,1536]{1,0:T(8,128)(2,1)}, u32[]{:S(2)}, u32[]{:S(2)}) collective-permute-start(bf16[512,1536]{1,0:T(8,128)(2,1)} %param.21), channel_id=1, source_target_pairs={{0,2},{1,3},{2,0},{3,1},{4,6},{5,7},{6,4},{7,5},{8,10},{9,11},{10,... | collective-permute-start | bytes 4718600 | tf_op jit(solution)/shard_map/ppermute | solution.py:433
  211.6 49.7 %collective-permute-start.12 = (bf16[512,1536]{1,0:T(8,128)(2,1)}, bf16[512,1536]{1,0:T(8,128)(2,1)}, u32[]{:S(2)}, u32[]{:S(2)}) collective-permute-start(bf16[512,1536]{1,0:T(8,128)(2,1)} %param.21), channel_id=1, source_target_pairs={{0,1},{1,0},{2,3},{3,2},{4,5},{5,4},{6,7},{7,6},{8,9},{9,8},{10,11... | collective-permute-start | bytes 4718600 | tf_op jit(solution)/shard_map/ppermute | solution.py:433
  233.3 59.0 %collective-permute-start.9 = (bf16[512,1536]{1,0:T(8,128)(2,1)}, bf16[512,1536]{1,0:T(8,128)(2,1)}, u32[]{:S(2)}, u32[]{:S(2)}) collective-permute-start(bf16[512,1536]{1,0:T(8,128)(2,1)} %get-tuple-element.61), channel_id=1, source_target_pairs={{0,2},{1,3},{2,0},{3,1},{4,6},{5,7},{6,4},{7,5},{8,10},{9,11},{10,... | collective-permute-start | bytes 4718600 | tf_op jit(solution)/shard_map/ppermute | solution.py:433
  291.3 41.5 %collective-permute-start.8 = (bf16[512,1536]{1,0:T(8,128)(2,1)}, bf16[512,1536]{1,0:T(8,128)(2,1)S(1)}, u32[]{:S(2)}, u32[]{:S(2)}) collective-permute-start(bf16[512,1536]{1,0:T(8,128)(2,1)} %get-tuple-element.61), channel_id=1, source_target_pairs={{0,1},{1,0},{2,3},{3,2},{4,5},{5,4},{6,7},{7,6},{8,9},{9,8},{10,11... | collective-permute-start | bytes 4718600 | tf_op jit(solution)/shard_map/ppermute | solution.py:433
  294.3 46.0 %collective-permute-start.10 = (bf16[256,1536]{1,0:T(8,128)(2,1)S(1)}, bf16[256,1536]{1,0:T(8,128)(2,1)S(1)}, u32[]{:S(2)}, u32[]{:S(2)}) collective-permute-start(bf16[256,1536]{1,0:T(8,128)(2,1)S(1)} %slice.276), channel_id=1, source_target_pairs={{0,1},{1,0},{2,3},{3,2},{4,5},{5,4},{6,7},{7,6},{8,9},{9,8},{10,11... | collective-permute-start | bytes 2359304 | tf_op jit(solution)/shard_map/ppermute | solution.py:433
  660.1 32.0 %collective-permute-start.22 = (bf16[512,1536]{1,0:T(8,128)(2,1)S(1)}, bf16[512,1536]{1,0:T(8,128)(2,1)}, u32[]{:S(2)}, u32[]{:S(2)}) collective-permute-start(bf16[512,1536]{1,0:T(8,128)(2,1)S(1)} %pad_maximum_fusion.6), channel_id=1, source_target_pairs={{0,2},{1,3},{2,0},{3,1},{4,6},{5,7},{6,4},{7,5},{8,10},{9,11},{10,... | collective-permute-start | bytes 4718600 | tf_op jit(solution)/shard_map/ppermute | solution.py:433
  690.9 303.1 %reduce-scatter.27.cloned.1.call-start = ((), (), s32[]{:S(2)}) async-start(), calls=%async_computation.21 | async-start | bytes 884736
  745.1 40.0 %collective-permute-start.25 = (bf16[512,1536]{1,0:T(8,128)(2,1)}, bf16[512,1536]{1,0:T(8,128)(2,1)S(1)}, u32[]{:S(2)}, u32[]{:S(2)}) collective-permute-start(bf16[512,1536]{1,0:T(8,128)(2,1)} %get-tuple-element.59), channel_id=1, source_target_pairs={{0,2},{1,3},{2,0},{3,1},{4,6},{5,7},{6,4},{7,5},{8,10},{9,11},{10,... | collective-permute-start | bytes 4718600 | tf_op jit(solution)/shard_map/ppermute | solution.py:433
  746.5 43.9 %collective-permute-start.24 = (bf16[512,1536]{1,0:T(8,128)(2,1)}, bf16[512,1536]{1,0:T(8,128)(2,1)}, u32[]{:S(2)}, u32[]{:S(2)}) collective-permute-start(bf16[512,1536]{1,0:T(8,128)(2,1)} %get-tuple-element.59), channel_id=1, source_target_pairs={{0,1},{1,0},{2,3},{3,2},{4,5},{5,4},{6,7},{7,6},{8,9},{9,8},{10,11... | collective-permute-start | bytes 4718600 | tf_op jit(solution)/shard_map/ppermute | solution.py:433
  790.3 277.6 %reduce-scatter.15.cloned.1.call-start = ((), (), s32[]{:S(2)}) async-start(), calls=%async_computation.15 | async-start | bytes 1327104 | tf_op jit(solution)/shard_map/reduce_scatter | solution.py:604
  817.2 263.4 %reduce-scatter.13.cloned.1.call-start = ((), (), s32[]{:S(2)}) async-start(), calls=%async_computation.14 | async-start | bytes 2211840 | tf_op jit(solution)/shard_map/reduce_scatter | solution.py:605
  878.4 204.0 %reduce-scatter.17.cloned.1.call-start = ((), (), s32[]{:S(2)}) async-start(), calls=%async_computation.16 | async-start | bytes 10616832 | tf_op jit(solution)/shard_map/reduce_scatter | solution.py:566
  879.1 245.1 %reduce-scatter.19.cloned.1.call-start = ((), (), s32[]{:S(2)}) async-start(), calls=%async_computation.17 | async-start | bytes 10616832 | tf_op jit(solution)/shard_map/reduce_scatter | solution.py:566
  879.7 344.9 %reduce-scatter.21.cloned.1.call-start = ((), (), s32[]{:S(2)}) async-start(), calls=%async_computation.18 | async-start | bytes 10616832 | tf_op jit(solution)/shard_map/reduce_scatter | solution.py:566
  880.4 444.3 %reduce-scatter.23.cloned.1.call-start = ((), (), s32[]{:S(2)}) async-start(), calls=%async_computation.19 | async-start | bytes 10616832 | tf_op jit(solution)/shard_map/reduce_scatter | solution.py:566
  896.6 37.5 %collective-permute-start.16 = (bf16[512,1536]{1,0:T(8,128)(2,1)S(1)}, bf16[512,1536]{1,0:T(8,128)(2,1)}, u32[]{:S(2)}, u32[]{:S(2)}) collective-permute-start(bf16[512,1536]{1,0:T(8,128)(2,1)S(1)} %pad_maximum_fusion.3), channel_id=1, source_target_pairs={{0,1},{1,0},{2,3},{3,2},{4,5},{5,4},{6,7},{7,6},{8,9},{9,8},{10,11... | collective-permute-start | bytes 4718600 | tf_op jit(solution)/shard_map/ppermute | solution.py:433
  897.4 42.4 %collective-permute-start.18 = (bf16[512,1536]{1,0:T(8,128)(2,1)S(1)}, bf16[512,1536]{1,0:T(8,128)(2,1)}, u32[]{:S(2)}, u32[]{:S(2)}) collective-permute-start(bf16[512,1536]{1,0:T(8,128)(2,1)S(1)} %pad_maximum_fusion.4), channel_id=1, source_target_pairs={{0,2},{1,3},{2,0},{3,1},{4,6},{5,7},{6,4},{7,5},{8,10},{9,11},{10,... | collective-permute-start | bytes 4718600 | tf_op jit(solution)/shard_map/ppermute | solution.py:433
  914.2 49.2 %collective-permute-start.28 = (bf16[512,1536]{1,0:T(8,128)(2,1)S(1)}, bf16[512,1536]{1,0:T(8,128)(2,1)S(1)}, u32[]{:S(2)}, u32[]{:S(2)}) collective-permute-start(bf16[512,1536]{1,0:T(8,128)(2,1)S(1)} %pad_maximum_fusion.7), channel_id=1, source_target_pairs={{0,1},{1,0},{2,3},{3,2},{4,5},{5,4},{6,7},{7,6},{8,9},{9,8},{10,11... | collective-permute-start | bytes 4718600 | tf_op jit(solution)/shard_map/ppermute | solution.py:433
  936.0 59.5 %collective-permute-start.30 = (bf16[512,1536]{1,0:T(8,128)(2,1)S(1)}, bf16[512,1536]{1,0:T(8,128)(2,1)}, u32[]{:S(2)}, u32[]{:S(2)}) collective-permute-start(bf16[512,1536]{1,0:T(8,128)(2,1)S(1)} %pad_maximum_fusion.8), channel_id=1, source_target_pairs={{0,2},{1,3},{2,0},{3,1},{4,6},{5,7},{6,4},{7,5},{8,10},{9,11},{10,... | collective-permute-start | bytes 4718600 | tf_op jit(solution)/shard_map/ppermute | solution.py:433
  938.3 50.9 %collective-permute-start.17 = (bf16[256,1536]{1,0:T(8,128)(2,1)S(1)}, bf16[256,1536]{1,0:T(8,128)(2,1)S(1)}, u32[]{:S(2)}, u32[]{:S(2)}) collective-permute-start(bf16[256,1536]{1,0:T(8,128)(2,1)S(1)} %fusion.18), channel_id=1, source_target_pairs={{0,2},{1,3},{2,0},{3,1},{4,6},{5,7},{6,4},{7,5},{8,10},{9,11},{10,... | collective-permute-start | bytes 2359304 | tf_op jit(solution)/shard_map/ppermute | solution.py:433
  1003.2 66.3 %collective-permute-start.31 = (bf16[256,1536]{1,0:T(8,128)(2,1)}, bf16[256,1536]{1,0:T(8,128)(2,1)}, u32[]{:S(2)}, u32[]{:S(2)}) collective-permute-start(bf16[256,1536]{1,0:T(8,128)(2,1)} %get-tuple-element.63), channel_id=1, source_target_pairs={{0,1},{1,0},{2,3},{3,2},{4,5},{5,4},{6,7},{7,6},{8,9},{9,8},{10,11... | collective-permute-start | bytes 2359304 | tf_op jit(solution)/shard_map/ppermute | solution.py:433
  (78 other events, 1676.5 us)
Sparse Core Ops, SparseCore 0:
  10.2 34.3 all-gather.6
  46.2 21.7 all-gather.8
  69.6 90.5 all-gather.10
  161.7 89.1 all-gather.12
  252.9 89.1 all-gather.14
  344.1 89.1 all-gather.16
  691.0 38.2 reduce-scatter.24
  790.4 41.6 reduce-scatter.26
  834.4 31.1 reduce-scatter.14
  878.5 44.2 reduce-scatter.12
  925.2 97.7 reduce-scatter.16
  1025.3 98.8 reduce-scatter.18
  1126.6 97.8 reduce-scatter.20
  1226.8 97.8 reduce-scatter.22

commit v2 on v1

--- a/solution.py
+++ b/solution.py
@@ -378,13 +378,13 @@
         copy(len(jobs) - 1).wait()
 
 
-def run_experts(span, slot_token, block_expert, rows, cots, gates, weights, low, tokens):
+def run_experts(span, slot_token, block_expert, rows, cots, gates, weights, tokens):
     width = rows.shape[1]
     experts, hidden = weights.shape[1], weights.shape[3]
     index = lambda i, s: s[0] + jnp.minimum(i, s[1] - 1)
     at = lambda i, s, e, t: (index(i, s), 0)
     pick = pl.BlockSpec(
-        (3, 1, width, hidden), lambda i, s, e, t: (0, e[index(i, s)] - low, 0, 0)
+        (3, 1, width, hidden), lambda i, s, e, t: (0, e[index(i, s)] - s[2], 0, 0)
     )
     anywhere = pl.BlockSpec(memory_space=pl.ANY)
     block_count = experts * 3 // 2
@@ -484,6 +484,91 @@
     )
 
 
+def place(target, piece, start, axis):
+    return lax.dynamic_update_slice_in_dim(target, piece, start, axis)
+
+
+def gather_shared(value):
+    count = lax.axis_size("narrow")
+    if count != 4:
+        return lax.all_gather(value, "narrow", axis=0, tiled=True)
+    me = lax.axis_index("narrow")
+    core = lax.rem(lax.axis_index("wide"), 2)
+    rows = value.shape[0]
+    half = rows // 2
+    quarter = half // 2
+    mine = lax.dynamic_slice_in_dim(value, core * half, half, 0)
+    one = swap(mine, 1)
+    two = swap(mine, 2)
+    far = jnp.concatenate([swap(two[:quarter], 1), swap(one[quarter:], 2)], axis=0)
+    fetched = jnp.concatenate([one, two, far], axis=0)
+    pairs = [(index, index ^ 1) for index in range(lax.axis_size("wide"))]
+    other = lax.ppermute(fetched, "wide", pairs)
+    full = jnp.zeros((count * rows,) + value.shape[1:], value.dtype)
+    full = place(full, value, me * rows, 0)
+    for step in range(1, count):
+        piece = slice((step - 1) * half, step * half)
+        full = place(full, fetched[piece], (me ^ step) * rows + core * half, 0)
+        full = place(full, other[piece], (me ^ step) * rows + (1 - core) * half, 0)
+    return full
+
+
+def exchange(value, split_axis, concat_axis):
+    count = lax.axis_size("narrow")
+    if count != 4:
+        return lax.all_to_all(
+            value, "narrow", split_axis=split_axis, concat_axis=concat_axis, tiled=True
+        )
+    me = lax.axis_index("narrow")
+    size = value.shape[split_axis] // count
+    pitch = value.shape[concat_axis]
+    shape = list(value.shape)
+    shape[split_axis] = size
+    shape[concat_axis] = pitch * count
+    result = jnp.zeros(shape, value.dtype)
+    for step in range(count):
+        piece = lax.dynamic_slice_in_dim(value, (me ^ step) * size, size, split_axis)
+        if step:
+            piece = swap(piece, step)
+        result = place(result, piece, (me ^ step) * pitch, concat_axis)
+    return result
+
+
+def gather_columns(value):
+    count = lax.axis_size("narrow")
+    me = lax.axis_index("narrow")
+    columns = value.shape[1]
+    full = place(jnp.zeros((value.shape[0], count * columns), value.dtype), value, me * columns, 1)
+    for step in range(1, count):
+        full = place(full, swap(value, step), (me ^ step) * columns, 1)
+    return full
+
+
+def sum_columns(part):
+    count = lax.axis_size("narrow")
+    me = lax.axis_index("narrow")
+    columns = part.shape[1] // count
+    result = lax.dynamic_slice_in_dim(part, me * columns, columns, 1)
+    for step in range(1, count):
+        piece = lax.dynamic_slice_in_dim(part, (me ^ step) * columns, columns, 1)
+        result = result + swap(piece, step)
+    return result
+
+
+def sum_all(value):
+    for axis in ("wide", "narrow"):
+        count = lax.axis_size(axis)
+        bit = 1
+        while bit < count:
+            value = value + lax.ppermute(value, axis, [(index, index ^ bit) for index in range(count)])
+            bit *= 2
+    return value
+
+
+def after(value, *others):
+    return lax.optimization_barrier((value,) + others)[0]
+
+
 def local(
     block_input,
     routes,
@@ -510,9 +595,7 @@
         return lax.dynamic_slice_in_dim(value, row_offset, row_part, 0)
 
     inputs = gather_rows(block_input)
-    gains = lax.all_gather(
-        jnp.stack([first_gain, second_gain]), "narrow", axis=1, tiled=True
-    ).astype(F32)
+    gains = gather_columns(jnp.stack([first_gain, second_gain])).astype(F32)
     gain_one, gain_two = gains[0], gains[1]
     router_padded = jnp.pad(router_weight, ((0, 0), (0, LANES - E)))
     input_router = lax.all_gather(
@@ -520,7 +603,8 @@
     )
     input_full = input_router[:, :head_columns]
     router_full = input_router[:, head_columns : head_columns + E]
-    output_full = lax.all_gather(output_weight, "wide", axis=1, tiled=True)
+    output_part = lax.all_gather(output_weight, "wide", axis=1, tiled=True)
+    output_full = gather_shared(after(output_part, inputs))
     lows = [sum(CHUNKS[:index]) for index in range(len(CHUNKS))]
     chunk_weights = []
     for low, size in zip(lows, CHUNKS):
@@ -532,14 +616,15 @@
     scale_one = lax.rsqrt(jnp.mean(x_full * x_full, axis=1, keepdims=True) + EPSILON)
     normed_one = x_full * scale_one
     attn_in = (normed_one * gain_one).astype(BF16)
-    late_cotangent, _ = lax.optimization_barrier((cotangent, inputs))
-    cot_full = gather_rows(late_cotangent)
+    cot_full = gather_rows(after(cotangent, output_full))
     projected = jnp.einsum(
         "td,dc->ct", attn_in, input_full, preferred_element_type=F32
     ).astype(BF16)
     mixed, log_totals = attend_forward(projected, groups, heads)
-    branch_part = jnp.einsum("ct,cd->td", mixed, output_full, preferred_element_type=F32)
-    middle_own = block_input.astype(F32) + sum_rows(branch_part)
+    mixed_own = exchange(mixed, 1, 0)
+    middle_own = block_input.astype(F32) + jnp.einsum(
+        "ct,cd->td", mixed_own, output_full, preferred_element_type=F32
+    )
     middle = gather_rows(middle_own.astype(BF16)).astype(F32)
     scale_two = lax.rsqrt(jnp.mean(middle * middle, axis=1, keepdims=True) + EPSILON)
     normed_two = middle * scale_two
@@ -551,14 +636,18 @@
     gate_lanes = jnp.pad(jnp.sum(picked * gates[:, :, None], axis=1), ((0, 0), (0, LANES - E)))
     live = block_ends[E - 1 :]
     cot_rows = dispatch(cot_full, None, slot_token, block_expert, live)
+    input_back = gather_shared(after(input_full.T, cot_rows))
     rows, slot_gates = dispatch(expert_in, gate_lanes, slot_token, block_expert, live)
 
     outs, backs, scores, grads = [], [], [], []
     for low, size, weights in zip(lows, CHUNKS, chunk_weights):
+        if len(outs) == 1:
+            weights, input_back = lax.optimization_barrier((weights, input_back))
         first = block_ends[low - 1 : low] if low else jnp.zeros((1,), jnp.int32)
         count = block_ends[low + size - 1 : low + size] - first
         out, back, score, grad = run_experts(
-            jnp.concatenate([first, count]), slot_token, block_expert, rows, cot_rows, slot_gates, weights, low, tokens
+            jnp.concatenate([first, count, jnp.full((1,), low, jnp.int32)]),
+            slot_token, block_expert, rows, cot_rows, slot_gates, weights, tokens
         )
         outs.append(out)
         backs.append(back)
@@ -570,8 +659,7 @@
 
     expert_sum = sum_rows(total(backs))
     score_part = jnp.sum(picked * total(scores)[:, None, :E], axis=2)
-    score_sum = lax.psum_scatter(score_part, "narrow", scatter_dimension=0, tiled=True)
-    block_output = (middle_own + sum_rows(total(outs))).astype(BF16)
+    score_sum = sum_columns(score_part.T).T
 
     gates_own = own_rows(gates)
     centre = jnp.sum(gates_own * score_sum, axis=1, keepdims=True)
@@ -586,32 +674,48 @@
     mid_grad = cotangent.astype(F32) + own_rows(scale_two) * (
         gain_two * norm_grad - normed_two_own * row_dot / width
     )
-    branch_grad = gather_rows(mid_grad.astype(BF16))
-    logit_full = lax.all_gather(logit_grad, "narrow", axis=0, tiled=True)
-    mixed_grad = jnp.einsum(
+    branch_grad = mid_grad.astype(BF16)
+    mixed_grad_own = jnp.einsum(
         "td,cd->ct", branch_grad, output_full, preferred_element_type=F32
     ).astype(BF16)
+    mixed_grad = exchange(after(mixed_grad_own, grads[0]), 0, 1)
+    block_output = (middle_own + sum_rows(after(total(outs), mixed_grad))).astype(BF16)
     projected_grad = attend_backward(projected, mixed, log_totals, mixed_grad, groups, heads)
-    input_part = jnp.einsum("ct,dc->td", projected_grad, input_full, preferred_element_type=F32)
     grad_input_w = jnp.einsum(
         "td,ct->dc", attn_in, projected_grad, preferred_element_type=F32
     ).astype(BF16)
-    grad_output_w = jnp.einsum(
-        "ct,td->cd", mixed, branch_grad, preferred_element_type=F32
+    projected_own = exchange(after(projected_grad, grads[1]), 1, 0)
+    input_sum = jnp.einsum("ct,cd->td", after(projected_own, grads[2]), input_back, preferred_element_type=F32)
+    grad_output_w = sum_rows(
+        after(
+            jnp.einsum("ct,td->cd", mixed_own, branch_grad, preferred_element_type=F32),
+            projected_own,
+        )
     ).astype(BF16)
-    grad_router = jnp.einsum("td,te->de", expert_in, logit_full, preferred_element_type=F32)
-    router_grad = lax.psum_scatter(grad_router, "wide", scatter_dimension=0, tiled=True)
-    output_w_grad = lax.psum_scatter(grad_output_w, "wide", scatter_dimension=1, tiled=True)
-    input_w_grad = lax.psum_scatter(grad_input_w, "wide", scatter_dimension=0, tiled=True)
-    gain_one_part = jnp.sum(input_part * normed_one, axis=0)
-    gain_pair = lax.psum(jnp.stack([gain_one_part, gain_two_part]), ("wide", "narrow"))
-    gain_own = lax.dynamic_slice_in_dim(gain_pair, me * gain_part, gain_part, 1)
-    input_sum = sum_rows(input_part)
+    grad_router = jnp.einsum(
+        "te,td->ed", logit_grad, own_rows(expert_in), preferred_element_type=F32
+    )
+    early_sum = sum_all(jnp.concatenate([grad_router, gain_two_part[None]], axis=0))
+    input_w_grad = lax.psum_scatter(
+        grad_input_w, "wide", scatter_dimension=0, tiled=True
+    )
+    output_w_grad = lax.psum_scatter(
+        grad_output_w, "wide", scatter_dimension=1, tiled=True
+    )
+    router_part = router_weight.shape[0]
+    router_grad = lax.dynamic_slice_in_dim(
+        early_sum[:E], lax.axis_index("wide") * router_part, router_part, 1
+    ).T
     normed_one_own = own_rows(normed_one)
+    gain_one_sum = sum_all(jnp.sum(input_sum * normed_one_own, axis=0)[None])
+    gain_own = lax.dynamic_slice_in_dim(
+        jnp.concatenate([gain_one_sum, early_sum[E:]], axis=0), me * gain_part, gain_part, 1
+    )
     input_dot = jnp.sum(input_sum * normed_one_own * gain_one, axis=1, keepdims=True)
     input_grad = mid_grad + own_rows(scale_one) * (
         gain_one * input_sum - normed_one_own * input_dot / width
     )
+    grads, _ = lax.optimization_barrier((grads, input_sum))
     gate_grad, up_grad, down_grad = (
         jnp.concatenate([grad[index] for grad in grads], axis=0).astype(F32) for index in range(3)
     )

time: 1350 us -> 1220 us (0.904)
  waiting for transfers between devices: 483 us -> 281 us
  local copies, waits for them, and re-layouts: 89.5 us -> 274 us
  blocking collectives: 126 us -> 0 us
  starting transfers between devices: 36.9 us -> 66.9 us
  Pallas kernels: 403 us -> 378 us
    reduce_scatter x4, waiting for transfers between devices: 238 us -> 0.03 us  [local(): lax.psum_scatter(grad, 'wide', scatter_dimension=2, tiled=True)]
    dynamic_update_slice x0 -> x26, local copies, waits for them, and re-layouts: none -> 133 us  [place(): return lax.dynamic_update_slice_in_dim(target, piece, start, axis)]
    all_gather x2 -> x0, blocking collectives: 75.5 us -> none  [the longest x1 38 us: local(): logit_full = lax.all_gather(logit_grad, 'narrow', axis=0, tiled=True)]
    psum x1 -> x0, blocking collectives: 50.4 us -> none  [local(): lax.psum(jnp.stack([gain_one_part, gain_two_part]), ('wide', 'narrow'))]
    ppermute x32 -> x47, waiting for transfers between devices: 218 us -> 256 us  [swap(): lax.ppermute(value, 'narrow', [(index, index ^ bit) for index in range(co...]
    unnamed x16 -> x13, waiting for transfers between devices: 26.2 us -> 0.86 us
    ppermute x0 -> x12, waiting for transfers between devices: none -> 24.3 us  [the longest x10 24.3 us: sum_all(): lax.ppermute(value, axis, [(index, index ^ bit) for index in range(count)])]
    unnamed x133 -> x139, local copies, waits for them, and re-layouts: 32.5 us -> 11.2 us
  transfers between devices with their start and end apart: 46 -> 71, of which waited for: 25 -> 29; matrix products, arithmetic and copies ran while one was open for 16% -> 38% of each run, Pallas kernels for 25% -> 31%
where the time goes in v2:
time: 1220 us; the launch traced here: 1210 us
  Pallas kernels  378 us (31%)
  waiting for transfers between devices  281 us (23%)
  local copies, waits for them, and re-layouts  274 us (22%)
  other arithmetic  136 us (11%)
  starting transfers between devices  66.9 us (5%)
  matrix products  56.3 us (5%)
  between operations  19.8 us (2%)
    ppermute x47, waiting for transfers between devices, swap(): lax.ppermute(value, 'narrow', [(index, index ^ bit) for index in range(co...  256 us
    pallas_call x4, Pallas kernels, run_experts(): pl.pallas_call(expert_kernel, grid_spec=pltpu.PrefetchScalarGridSpec(num_...  220 us
    dynamic_update_slice x26, local copies, waits for them, and re-layouts, place(): return lax.dynamic_update_slice_in_dim(target, piece, start, axis)  133 us
    pallas_call x2, Pallas kernels, dispatch(): pl.pallas_call(functools.partial(dispatch_kernel, gated), grid_spec=pltpu...  71.8 us
    ppermute x47, starting transfers between devices, swap(): lax.ppermute(value, 'narrow', [(index, index ^ bit) for index in range(co...  50.4 us
    pallas_call x1, Pallas kernels, attend_backward(): pl.pallas_call(functools.partial(backward_kernel, heads), grid=(groups, b...  48.1 us
    pallas_call x1, Pallas kernels, attend_forward(): pl.pallas_call(functools.partial(forward_kernel, heads), grid=(groups, bl...  38 us
    add x3, other arithmetic, total(): return sum((value.astype(F32) for value in values))  27.1 us
  transfers between devices with their start and end apart: 71, of which 29 were waited for; matrix products, arithmetic and copies ran while one was open for 38% of the time, Pallas kernels for 31%

profile of v2, /device:TPU:0, one launch (start us, length us, event | category | flops | bytes accessed | tf_op | source)
XLA Modules:
  0.0 1211.5 jit_solution(15237294343357987339)
XLA Ops:
  40.0 16.3 %collective-permute-done.1 = bf16[512,1536]{1,0:T(8,128)(2,1)S(1)} collective-permute-done((bf16[512,1536]{1,0:T(8,128)(2,1)}, bf16[512,1536]{1,0:T(8,128)(2,1)S(1)}, u32[]{:S(2)}, u32[]{:S(2)}) %collective-permute-start.1) | collective-permute-done | bytes 1572896 | tf_op jit(solution)/shard_map/ppermute | solution.py:433
  67.8 9.5 collective-permute-done.2
  85.5 10.0 collective-permute-done.10
  115.2 38.0 %shard_map.186 = (bf16[384,2048]{1,0:T(8,128)(2,1)S(1)}, f32[2,8,1,768]{3,2,1,0:T(1,128)S(1)}) custom-call(bf16[640,2048]{1,0:T(8,128)(2,1)S(1)} %convolution_convert_fusion.1.qkv_ref), custom_call_target="tpu_custom_call" | custom-call | flops 12884901888 | bytes 5242880 | tf_op jit(solution)/shard_map/pallas_call | solution.py:77
  250.0 15.5 %scatter_custom_fusion.token_ref = s32[8192]{0:T(1024)S(1)} fusion(s32[4096]{0:T(1024)S(1)} %bitcast.121, s32[4096]{0:T(1024)S(1)} %add_select_fusion, s32[]{:T(128)} %constant.97.clone.1), kind=kCustom, calls=%fused_computation.202 | custom fusion | bytes 32772 | tf_op jit(solution)/shard_map/scatter | solution.py:170
  273.4 12.3 %collective-permute-done.16 = bf16[512,1536]{1,0:T(8,128)(2,1)} collective-permute-done((bf16[512,1536]{1,0:T(8,128)(2,1)}, bf16[512,1536]{1,0:T(8,128)(2,1)}, u32[]{:S(2)}, u32[]{:S(2)}) %collective-permute-start.16) | collective-permute-done | bytes 1572896 | tf_op jit(solution)/shard_map/ppermute | solution.py:433
  289.8 29.5 %collective-permute-done.20 = bf16[512,1536]{1,0:T(8,128)(2,1)} collective-permute-done((bf16[512,1536]{1,0:T(8,128)(2,1)}, bf16[512,1536]{1,0:T(8,128)(2,1)}, u32[]{:S(2)}, u32[]{:S(2)}) %collective-permute-start.20) | collective-permute-done | bytes 1572896 | tf_op jit(solution)/shard_map/ppermute | solution.py:433
  341.2 11.9 convert_multiply_fusion
  361.4 37.0 %shard_map.187 = (bf16[8192,1536]{1,0:T(8,128)(2,1)}, f32[8192,1]{1,0:T(8,128)S(1)}) custom-call(s32[8192]{0:T(1024)S(1)} %scatter_custom_fusion.token_ref, s32[32]{0:T(128)S(1)} %broadcast_minimum_fusion.expert_ref, s32[1]{0:T(128)} %bitcast.5.live_ref, bf16[2048,1536]{1,0:T(8,128)(2,1)} %get-tuple-element.161.source_ref, f32[2048,128]{1,0:T(8,128)S(1)} %pad.9.refs_0_), custom_call_target="tpu_custom_call" | custom-call | flops 20000000000 | bytes 18874368 | tf_op jit(solution)/shard_map/pallas_call | solution.py:237
  400.4 34.8 %shard_map.188.cot_ref = bf16[8192,1536]{1,0:T(8,128)(2,1)} custom-call(s32[8192]{0:T(1024)S(1)} %scatter_custom_fusion.token_ref, s32[32]{0:T(128)S(1)} %broadcast_minimum_fusion.expert_ref, s32[1]{0:T(128)} %bitcast.5.live_ref, bf16[2048,1536]{1,0:T(8,128)(2,1)} %constant_dynamic-update-slice_fusion.7.source_ref), custom_call_target="tpu_custom_call" | custom-call | flops 20000000000 | bytes 18874368 | tf_op jit(solution)/shard_map/pallas_call | solution.py:237
  435.2 49.5 %shard_map.189 = (bf16[2048,1536]{1,0:T(8,128)(2,1)}, bf16[2048,1536]{1,0:T(8,128)(2,1)}, f32[2048,128]{1,0:T(8,128)}, bf16[3,4,1536,256]{3,2,1,0:T(8,128)(2,1)}) custom-call(s32[3]{0:T(128)} %pad_add_fusion.span_ref, s32[32]{0:T(128)} %copy-done.3, s32[8192]{0:T(1024)} %copy-done.2, bf16[8192,1536]{1,0:T(8,128)(2,1)} %get-tuple-element.46.row_ref, ...), custom_call_target="tpu_custom_call" | custom-call | flops 32614907904 | bytes 28311552 | tf_op jit(solution)/shard_map/pallas_call | solution.py:391
  492.9 19.5 %collective-permute-done.23 = bf16[320,1536]{1,0:T(8,128)(2,1)S(1)} collective-permute-done((bf16[320,1536]{1,0:T(8,128)(2,1)}, bf16[320,1536]{1,0:T(8,128)(2,1)S(1)}, u32[]{:S(2)}, u32[]{:S(2)}) %collective-permute-start.23) | collective-permute-done | bytes 983072 | tf_op jit(solution)/shard_map/ppermute | solution.py:433
  535.5 11.4 dynamic_update_slice.166
  561.8 13.2 %dynamic_update_slice.167 = bf16[2560,1536]{0,1:T(8,128)(2,1)} dynamic-update-slice(bf16[2560,1536]{0,1:T(8,128)(2,1)} %dynamic_update_slice.166, bf16[320,1536]{0,1:T(8,128)(2,1)} %copy.80, s32[]{:T(128)S(6)} %select_n.222, s32[]{:T(128)} %constant.96.clone.1) | dynamic-update-slice | bytes 1966084 | tf_op jit(solution)/shard_map/dynamic_update_slice | solution.py:488
  575.0 11.4 dynamic_update_slice.168
  586.4 13.2 %dynamic_update_slice.169 = bf16[2560,1536]{0,1:T(8,128)(2,1)} dynamic-update-slice(bf16[2560,1536]{0,1:T(8,128)(2,1)} %dynamic_update_slice.168, bf16[320,1536]{0,1:T(8,128)(2,1)} %copy.82, s32[]{:T(128)S(6)} %select_n.224, s32[]{:T(128)} %constant.96.clone.1) | dynamic-update-slice | bytes 1966084 | tf_op jit(solution)/shard_map/dynamic_update_slice | solution.py:488
  599.6 11.2 dynamic_update_slice.170
  610.8 11.8 dynamic_update_slice.171
  622.6 44.7 %shard_map.190 = (bf16[2048,1536]{1,0:T(8,128)(2,1)}, bf16[2048,1536]{1,0:T(8,128)(2,1)}, f32[2048,128]{1,0:T(8,128)}, bf16[3,4,1536,256]{3,2,1,0:T(8,128)(2,1)}) custom-call(s32[3]{0:T(128)} %pad_add_fusion.1.span_ref, s32[32]{0:T(128)} %copy-done.3, s32[8192]{0:T(1024)} %copy-done.2, bf16[8192,1536]{1,0:T(8,128)(2,1)} %get-tuple-element.46.row_ref, ...), custom_call_target="tpu_custom_call" | custom-call | flops 32614907904 | bytes 28311552 | tf_op jit(solution)/shard_map/pallas_call | solution.py:391
  669.9 67.5 %shard_map.191 = (bf16[2048,1536]{1,0:T(8,128)(2,1)}, bf16[2048,1536]{1,0:T(8,128)(2,1)}, f32[2048,128]{1,0:T(8,128)}, bf16[3,4,1536,256]{3,2,1,0:T(8,128)(2,1)}) custom-call(s32[3]{0:T(128)} %pad_add_fusion.2.span_ref, s32[32]{0:T(128)} %copy-done.3, s32[8192]{0:T(1024)} %copy-done.2, bf16[8192,1536]{1,0:T(8,128)(2,1)} %get-tuple-element.46.row_ref, ...), custom_call_target="tpu_custom_call" | custom-call | flops 32614907904 | bytes 28311552 | tf_op jit(solution)/shard_map/pallas_call | solution.py:391
  740.0 57.9 %shard_map.192 = (bf16[2048,1536]{1,0:T(8,128)(2,1)}, bf16[2048,1536]{1,0:T(8,128)(2,1)}, f32[2048,128]{1,0:T(8,128)}, bf16[3,4,1536,256]{3,2,1,0:T(8,128)(2,1)}) custom-call(s32[3]{0:T(128)} %pad_add_fusion.3.span_ref, s32[32]{0:T(128)} %copy-done.3, s32[8192]{0:T(1024)} %copy-done.2, bf16[8192,1536]{1,0:T(8,128)(2,1)} %get-tuple-element.46.row_ref, ...), custom_call_target="tpu_custom_call" | custom-call | flops 32614907904 | bytes 28311552 | tf_op jit(solution)/shard_map/pallas_call | solution.py:391
  798.0 15.1 %convert_add_fusion = f32[2048,1536]{1,0:T(8,128)} fusion(bf16[2048,1536]{1,0:T(8,128)(2,1)} %get-tuple-element.58, bf16[2048,1536]{1,0:T(8,128)(2,1)} %get-tuple-element.57, bf16[2048,1536]{1,0:T(8,128)(2,1)} %get-tuple-element.56, bf16[2048,1536]{1,0:T(8,128)(2,1)} %get-tuple-element.55), kind=kLoop, calls=%fused_computation.7 | loop fusion | flops 22020096 | bytes 37748736 | tf_op jit(solution)/shard_map/add | solution.py:658
  821.1 30.5 %collective-permute-done.28 = bf16[512,1536]{1,0:T(8,128)(2,1)} collective-permute-done((bf16[512,1536]{1,0:T(8,128)(2,1)}, bf16[512,1536]{1,0:T(8,128)(2,1)}, u32[]{:S(2)}, u32[]{:S(2)}) %collective-permute-start.28) | collective-permute-done | bytes 1572896 | tf_op jit(solution)/shard_map/ppermute | solution.py:433
  864.4 11.3 collective-permute-done.29
  880.2 16.6 %collective-permute-done.31 = bf16[256,1536]{1,0:T(8,128)(2,1)S(1)} collective-permute-done((bf16[256,1536]{1,0:T(8,128)(2,1)S(1)}, bf16[256,1536]{1,0:T(8,128)(2,1)S(1)}, u32[]{:S(2)}, u32[]{:S(2)}) %collective-permute-start.31) | collective-permute-done | bytes 786464 | tf_op jit(solution)/shard_map/ppermute | solution.py:433
  922.2 11.8 convert_add_fusion.1
  937.4 13.5 %collective-permute-done.52 = f32[17,1536]{1,0:T(8,128)S(1)} collective-permute-done((f32[17,1536]{1,0:T(8,128)S(1)}, f32[17,1536]{1,0:T(8,128)S(1)}, u32[]{:S(2)}, u32[]{:S(2)}) %collective-permute-start.52) | collective-permute-done | bytes 104480 | tf_op jit(solution)/shard_map/ppermute | solution.py:563
  981.6 48.1 %shard_map.193 = bf16[640,2048]{1,0:T(8,128)(2,1)S(1)} custom-call(bf16[640,2048]{1,0:T(8,128)(2,1)S(1)} %copy-done.5, bf16[384,2048]{1,0:T(8,128)(2,1)S(1)} %copy-done.1, f32[2,8,1,768]{3,2,1,0:T(1,128)S(1)} %get-tuple-element.66.total_ref, bf16[384,2048]{1,0:T(8,128)(2,1)S(1)} %constant_dynamic-update-slice_fusion.3.grad_ref), custom_call_target="tpu_custom_call" | custom-call | flops 32212254720 | bytes 10485760 | tf_op jit(solution)/shard_map/pallas_call | solution.py:139
  1055.0 21.9 %collective-permute-done.43 = bf16[640,512]{1,0:T(8,128)(2,1)S(1)} collective-permute-done((bf16[640,512]{1,0:T(8,128)(2,1)S(1)}, bf16[640,512]{1,0:T(8,128)(2,1)S(1)}, u32[]{:S(2)}, u32[]{:S(2)}) %collective-permute-start.43) | collective-permute-done | bytes 655392 | tf_op jit(solution)/shard_map/ppermute | solution.py:433
  1078.7 11.5 fusion.15
  1107.6 17.4 %collective-permute-done.55 = bf16[384,1536]{1,0:T(8,128)(2,1)} collective-permute-done((bf16[384,1536]{1,0:T(8,128)(2,1)}, bf16[384,1536]{1,0:T(8,128)(2,1)}, u32[]{:S(2)}, u32[]{:S(2)}) %collective-permute-start.55) | collective-permute-done | bytes 1179680 | tf_op jit(solution)/shard_map/ppermute | solution.py:433
  1181.9 10.6 collective-permute-done.48
  (482 shorter events, 457.2 us)
Async XLA Ops:
  7.2 72.9 %all-gather.9.cloned.1.call-start = ((), (), s32[]{:S(2)}) async-start(), calls=%async_computation.7 | async-start | bytes 1327104 | tf_op jit(solution)/shard_map/all_gather | solution.py:606
  7.9 99.1 %all-gather.7.cloned.1.call-start = ((), (), s32[]{:S(2)}) async-start(), calls=%async_computation.6 | async-start | bytes 2654208 | tf_op jit(solution)/shard_map/all_gather | solution.py:601
  10.5 424.7 %all-gather.11.cloned.1.call-start = ((), (), s32[]{:S(2)}) async-start(), calls=%async_computation.8 | async-start | bytes 10616832 | tf_op jit(solution)/shard_map/all_gather | solution.py:612
  15.1 607.5 %all-gather.13.cloned.1.call-start = ((), (), s32[]{:S(2)}) async-start(), calls=%async_computation.9 | async-start | bytes 10616832 | tf_op jit(solution)/shard_map/all_gather | solution.py:612
  17.4 652.6 %all-gather.15.cloned.1.call-start = ((), (), s32[]{:S(2)}) async-start(), calls=%async_computation.10 | async-start | bytes 10616832 | tf_op jit(solution)/shard_map/all_gather | solution.py:612
  18.6 721.4 %all-gather.17.cloned.1.call-start = ((), (), s32[]{:S(2)}) async-start(), calls=%async_computation.11 | async-start | bytes 10616832 | tf_op jit(solution)/shard_map/all_gather | solution.py:612
  18.6 37.7 %collective-permute-start.1 = (bf16[512,1536]{1,0:T(8,128)(2,1)}, bf16[512,1536]{1,0:T(8,128)(2,1)S(1)}, u32[]{:S(2)}, u32[]{:S(2)}) collective-permute-start(bf16[512,1536]{1,0:T(8,128)(2,1)} %param.11), channel_id=1, source_target_pairs={{0,2},{1,3},{2,0},{3,1},{4,6},{5,7},{6,4},{7,5},{8,10},{9,11},{10,... | collective-permute-start | bytes 4718600 | tf_op jit(solution)/shard_map/ppermute | solution.py:433
  21.7 63.6 %collective-permute-start.4 = (bf16[2,384]{1,0:T(2,128)(2,1)S(1)}, bf16[2,384]{1,0:T(2,128)(2,1)S(1)}, u32[]{:S(2)}, u32[]{:S(2)}) collective-permute-start(bf16[2,384]{1,0:T(2,128)(2,1)S(1)} %get-tuple-element.141), channel_id=1, source_target_pairs={{0,1},{1,0},{2,3},{3,2},{4,5},{5,4},{6,7},{7,6},{8,9},{9,8},{10,11... | collective-permute-start | bytes 4616 | tf_op jit(solution)/shard_map/ppermute | solution.py:433
  23.3 62.1 %collective-permute-start.5 = (bf16[2,384]{1,0:T(2,128)(2,1)S(1)}, bf16[2,384]{1,0:T(2,128)(2,1)S(1)}, u32[]{:S(2)}, u32[]{:S(2)}) collective-permute-start(bf16[2,384]{1,0:T(2,128)(2,1)S(1)} %get-tuple-element.141), channel_id=1, source_target_pairs={{0,2},{1,3},{2,0},{3,1},{4,6},{5,7},{6,4},{7,5},{8,10},{9,11},{10,... | collective-permute-start | bytes 4616 | tf_op jit(solution)/shard_map/ppermute | solution.py:433
  23.8 61.6 %collective-permute-start.6 = (bf16[2,384]{1,0:T(2,128)(2,1)S(1)}, bf16[2,384]{1,0:T(2,128)(2,1)S(1)}, u32[]{:S(2)}, u32[]{:S(2)}) collective-permute-start(bf16[2,384]{1,0:T(2,128)(2,1)S(1)} %get-tuple-element.141), channel_id=1, source_target_pairs={{0,3},{1,2},{2,1},{3,0},{4,7},{5,6},{6,5},{7,4},{8,11},{9,10},{10,... | collective-permute-start | bytes 4616 | tf_op jit(solution)/shard_map/ppermute | solution.py:433
  25.3 37.4 %collective-permute-start = (bf16[512,1536]{1,0:T(8,128)(2,1)}, bf16[512,1536]{1,0:T(8,128)(2,1)}, u32[]{:S(2)}, u32[]{:S(2)}) collective-permute-start(bf16[512,1536]{1,0:T(8,128)(2,1)} %param.11), channel_id=1, source_target_pairs={{0,1},{1,0},{2,3},{3,2},{4,5},{5,4},{6,7},{7,6},{8,9},{9,8},{10,11... | collective-permute-start | bytes 4718600 | tf_op jit(solution)/shard_map/ppermute | solution.py:433
  27.9 932.0 %reduce-scatter.9.cloned.1.call-start = ((), (), s32[]{:S(2)}) async-start(), calls=%async_computation.12 | async-start | bytes 10616832 | tf_op jit(solution)/shard_map/reduce_scatter | solution.py:655
  107.0 76.5 %collective-permute-start.14 = (bf16[576,1536]{1,0:T(8,128)(2,1)}, bf16[576,1536]{1,0:T(8,128)(2,1)}, u32[]{:S(2)}, u32[]{:S(2)}) collective-permute-start(bf16[576,1536]{1,0:T(8,128)(2,1)} %pad_maximum_fusion.1), channel_id=1, source_target_pairs={{0,4},{4,0},{8,12},{12,8},{16,20},{20,16},{24,28},{28,24},{1,5},{5... | collective-permute-start | bytes 5308424 | tf_op jit(solution)/shard_map/ppermute | solution.py:506
  245.7 41.2 %collective-permute-start.15 = (bf16[512,1536]{1,0:T(8,128)(2,1)}, bf16[512,1536]{1,0:T(8,128)(2,1)}, u32[]{:S(2)}, u32[]{:S(2)}) collective-permute-start(bf16[512,1536]{1,0:T(8,128)(2,1)} %get-tuple-element.139), channel_id=1, source_target_pairs={{0,1},{1,0},{2,3},{3,2},{4,5},{5,4},{6,7},{7,6},{8,9},{9,8},{10,11... | collective-permute-start | bytes 4718600 | tf_op jit(solution)/shard_map/ppermute | solution.py:433
  248.0 37.6 %collective-permute-start.16 = (bf16[512,1536]{1,0:T(8,128)(2,1)}, bf16[512,1536]{1,0:T(8,128)(2,1)}, u32[]{:S(2)}, u32[]{:S(2)}) collective-permute-start(bf16[512,1536]{1,0:T(8,128)(2,1)} %get-tuple-element.139), channel_id=1, source_target_pairs={{0,2},{1,3},{2,0},{3,1},{4,6},{5,7},{6,4},{7,5},{8,10},{9,11},{10,... | collective-permute-start | bytes 4718600 | tf_op jit(solution)/shard_map/ppermute | solution.py:433
  249.6 71.0 %collective-permute-start.19 = (bf16[512,1536]{1,0:T(8,128)(2,1)}, bf16[512,1536]{1,0:T(8,128)(2,1)}, u32[]{:S(2)}, u32[]{:S(2)}) collective-permute-start(bf16[512,1536]{1,0:T(8,128)(2,1)} %param.21), channel_id=1, source_target_pairs={{0,1},{1,0},{2,3},{3,2},{4,5},{5,4},{6,7},{7,6},{8,9},{9,8},{10,11... | collective-permute-start | bytes 4718600 | tf_op jit(solution)/shard_map/ppermute | solution.py:433
  249.6 69.7 %collective-permute-start.20 = (bf16[512,1536]{1,0:T(8,128)(2,1)}, bf16[512,1536]{1,0:T(8,128)(2,1)}, u32[]{:S(2)}, u32[]{:S(2)}) collective-permute-start(bf16[512,1536]{1,0:T(8,128)(2,1)} %param.21), channel_id=1, source_target_pairs={{0,2},{1,3},{2,0},{3,1},{4,6},{5,7},{6,4},{7,5},{8,10},{9,11},{10,... | collective-permute-start | bytes 4718600 | tf_op jit(solution)/shard_map/ppermute | solution.py:433
  286.8 48.2 %collective-permute-start.17 = (bf16[256,1536]{1,0:T(8,128)(2,1)S(1)}, bf16[256,1536]{1,0:T(8,128)(2,1)S(1)}, u32[]{:S(2)}, u32[]{:S(2)}) collective-permute-start(bf16[256,1536]{1,0:T(8,128)(2,1)S(1)} %slice.301), channel_id=1, source_target_pairs={{0,1},{1,0},{2,3},{3,2},{4,5},{5,4},{6,7},{7,6},{8,9},{9,8},{10,11... | collective-permute-start | bytes 2359304 | tf_op jit(solution)/shard_map/ppermute | solution.py:433
  288.1 48.0 %collective-permute-start.18 = (bf16[256,1536]{1,0:T(8,128)(2,1)S(1)}, bf16[256,1536]{1,0:T(8,128)(2,1)S(1)}, u32[]{:S(2)}, u32[]{:S(2)}) collective-permute-start(bf16[256,1536]{1,0:T(8,128)(2,1)S(1)} %slice.302), channel_id=1, source_target_pairs={{0,2},{1,3},{2,0},{3,1},{4,6},{5,7},{6,4},{7,5},{8,10},{9,11},{10,... | collective-permute-start | bytes 2359304 | tf_op jit(solution)/shard_map/ppermute | solution.py:433
  320.5 37.8 %collective-permute-start.21 = (bf16[256,1536]{1,0:T(8,128)(2,1)S(1)}, bf16[256,1536]{1,0:T(8,128)(2,1)S(1)}, u32[]{:S(2)}, u32[]{:S(2)}) collective-permute-start(bf16[256,1536]{1,0:T(8,128)(2,1)S(1)} %slice.305), channel_id=1, source_target_pairs={{0,1},{1,0},{2,3},{3,2},{4,5},{5,4},{6,7},{7,6},{8,9},{9,8},{10,11... | collective-permute-start | bytes 2359304 | tf_op jit(solution)/shard_map/ppermute | solution.py:433
  322.7 36.6 %collective-permute-start.22 = (bf16[256,1536]{1,0:T(8,128)(2,1)}, bf16[256,1536]{1,0:T(8,128)(2,1)}, u32[]{:S(2)}, u32[]{:S(2)}) collective-permute-start(bf16[256,1536]{1,0:T(8,128)(2,1)} %slice.306), channel_id=1, source_target_pairs={{0,2},{1,3},{2,0},{3,1},{4,6},{5,7},{6,4},{7,5},{8,10},{9,11},{10,... | collective-permute-start | bytes 2359304 | tf_op jit(solution)/shard_map/ppermute | solution.py:433
  484.7 545.0 %reduce-scatter.11.cloned.1.call-start = ((), (), s32[]{:S(2)}) async-start(), calls=%async_computation.13 | async-start | bytes 10616832 | tf_op jit(solution)/shard_map/reduce_scatter | solution.py:655
  667.4 411.4 %reduce-scatter.13.cloned.1.call-start = ((), (), s32[]{:S(2)}) async-start(), calls=%async_computation.14 | async-start | bytes 10616832 | tf_op jit(solution)/shard_map/reduce_scatter | solution.py:655
  737.4 360.2 %reduce-scatter.17.cloned.1.call-start = ((), (), s32[]{:S(2)}) async-start(), calls=%async_computation.16 | async-start | bytes 10616832 | tf_op jit(solution)/shard_map/reduce_scatter | solution.py:655
  797.9 402.9 %reduce-scatter.15.cloned.1.call-start = ((), (), s32[]{:S(2)}) async-start(), calls=%async_computation.15 | async-start | bytes 2211840 | tf_op jit(solution)/shard_map/reduce_scatter | solution.py:699
  817.6 34.0 %collective-permute-start.28 = (bf16[512,1536]{1,0:T(8,128)(2,1)}, bf16[512,1536]{1,0:T(8,128)(2,1)}, u32[]{:S(2)}, u32[]{:S(2)}) collective-permute-start(bf16[512,1536]{1,0:T(8,128)(2,1)} %pad_maximum_fusion.2), channel_id=1, source_target_pairs={{0,1},{1,0},{2,3},{3,2},{4,5},{5,4},{6,7},{7,6},{8,9},{9,8},{10,11... | collective-permute-start | bytes 4718600 | tf_op jit(solution)/shard_map/ppermute | solution.py:433
  819.4 44.6 %collective-permute-start.30 = (bf16[512,1536]{1,0:T(8,128)(2,1)}, bf16[512,1536]{1,0:T(8,128)(2,1)S(1)}, u32[]{:S(2)}, u32[]{:S(2)}) collective-permute-start(bf16[512,1536]{1,0:T(8,128)(2,1)} %pad_maximum_fusion.3), channel_id=1, source_target_pairs={{0,2},{1,3},{2,0},{3,1},{4,6},{5,7},{6,4},{7,5},{8,10},{9,11},{10,... | collective-permute-start | bytes 4718600 | tf_op jit(solution)/shard_map/ppermute | solution.py:433
  1049.8 106.2 %collective-permute-start.40 = (bf16[512,1536]{1,0:T(8,128)(2,1)}, bf16[512,1536]{1,0:T(8,128)(2,1)}, u32[]{:S(2)}, u32[]{:S(2)}) collective-permute-start(bf16[512,1536]{1,0:T(8,128)(2,1)} %pad_maximum_fusion.5), channel_id=1, source_target_pairs={{0,2},{1,3},{2,0},{3,1},{4,6},{5,7},{6,4},{7,5},{8,10},{9,11},{10,... | collective-permute-start | bytes 4718600 | tf_op jit(solution)/shard_map/ppermute | solution.py:433
  1051.9 97.5 %collective-permute-start.38 = (bf16[512,1536]{1,0:T(8,128)(2,1)}, bf16[512,1536]{1,0:T(8,128)(2,1)}, u32[]{:S(2)}, u32[]{:S(2)}) collective-permute-start(bf16[512,1536]{1,0:T(8,128)(2,1)} %pad_maximum_fusion.4), channel_id=1, source_target_pairs={{0,1},{1,0},{2,3},{3,2},{4,5},{5,4},{6,7},{7,6},{8,9},{9,8},{10,11... | collective-permute-start | bytes 4718600 | tf_op jit(solution)/shard_map/ppermute | solution.py:433
  1052.8 149.8 %reduce-scatter.19.cloned.1.call-start = ((), (), s32[]{:S(2)}) async-start(), calls=%async_computation.17 | async-start | bytes 1327104
  1090.8 38.1 %collective-permute-start.45 = (f32[1,1536]{1,0:T(1,128)}, f32[1,1536]{1,0:T(1,128)}, u32[]{:S(2)}, u32[]{:S(2)}) collective-permute-start(f32[1,1536]{1,0:T(1,128)} %broadcast_in_dim.25), channel_id=1, source_target_pairs={{0,4},{4,0},{8,12},{12,8},{16,20},{20,16},{24,28},{28,24},{1,5},{5... | collective-permute-start | bytes 18440 | tf_op jit(solution)/shard_map/ppermute | solution.py:563
  1094.5 41.5 %collective-permute-start.57 = (bf16[384,1536]{1,0:T(8,128)(2,1)}, bf16[384,1536]{1,0:T(8,128)(2,1)}, u32[]{:S(2)}, u32[]{:S(2)}) collective-permute-start(bf16[384,1536]{1,0:T(8,128)(2,1)} %pad_maximum_fusion.11), channel_id=1, source_target_pairs={{0,2},{1,3},{2,0},{3,1},{4,6},{5,7},{6,4},{7,5},{8,10},{9,11},{10,... | collective-permute-start | bytes 3538952 | tf_op jit(solution)/shard_map/ppermute | solution.py:433
  (107 other events, 1942.6 us)
Sparse Core Ops, SparseCore 0:
  9.7 25.3 all-gather.8
  37.3 31.4 all-gather.6
  70.4 89.8 all-gather.10
  161.7 89.1 all-gather.12
  252.3 89.1 all-gather.14
  343.0 89.1 all-gather.16
  484.8 102.6 reduce-scatter.8
  667.5 111.3 reduce-scatter.10
  781.2 97.8 reduce-scatter.12
  881.3 104.1 reduce-scatter.16
  1052.9 33.0 reduce-scatter.14
  1164.4 30.5 reduce-scatter.18

commit v3 on v1

--- a/solution.py
+++ b/solution.py
@@ -17,9 +17,9 @@
 QB = 256
 KB = 256
 LANES = 128
-PITCH = 16
+PITCH = 13
 UNROLL = 8
-CHUNKS = (4, 4, 4, 4)
+CHUNKS = (6, 6, 4)
 EPSILON = 1e-05
 F32 = jnp.float32
 BF16 = jnp.bfloat16
@@ -83,7 +83,7 @@
         out_shape=[jax.ShapeDtypeStruct((groups * heads * HEAD_SIZE, tokens), jnp.bfloat16),
                    jax.ShapeDtypeStruct((groups, blocks, 1, heads * QB), jnp.float32)],
         scratch_shapes=[pltpu.VMEM((tokens, HEAD_SIZE), jnp.bfloat16)],
-        cost_estimate=pl.CostEstimate(flops=flops * 4, bytes_accessed=qkv.size * 4, transcendentals=0),
+        cost_estimate=pl.CostEstimate(flops=flops * 14, bytes_accessed=qkv.size * 4, transcendentals=0),
         compiler_params=pltpu.CompilerParams(vmem_limit_bytes=32 << 20),
     )(qkv)
 
@@ -147,7 +147,7 @@
         out_shape=jax.ShapeDtypeStruct((groups * rows, tokens), jnp.bfloat16),
         scratch_shapes=[pltpu.VMEM((tokens, HEAD_SIZE), jnp.bfloat16), pltpu.VMEM((tokens, HEAD_SIZE), jnp.bfloat16),
                         pltpu.VMEM((tokens, HEAD_SIZE), jnp.float32), pltpu.VMEM((tokens, HEAD_SIZE), jnp.float32)],
-        cost_estimate=pl.CostEstimate(flops=flops * 4, bytes_accessed=qkv.size * 8, transcendentals=0),
+        cost_estimate=pl.CostEstimate(flops=flops * 7, bytes_accessed=qkv.size * 8, transcendentals=0),
         compiler_params=pltpu.CompilerParams(vmem_limit_bytes=40 << 20),
     )(qkv, out, totals, grad)
 
@@ -176,30 +176,57 @@
 
 
 def row_at(index):
-    return pl.ds(pl.multiple_of(index * PITCH, PITCH), PITCH)
-
-
-def dispatch_kernel(gated, token_ref, expert_ref, live_ref, source_ref, *refs):
+    return pl.ds(index * PITCH, PITCH)
+
+
+def dispatch_kernel(blocks, gated, token_ref, expert_ref, live_ref, me_ref, *refs):
+    sources, refs = refs[:blocks], refs[blocks:]
     if gated:
-        weight_ref, out_ref, gate_ref, held, moved = refs
+        gain_ref, router_ref, route_ref, out_ref, gate_ref, held, moved = refs
     else:
         out_ref, held, moved = refs
     step = pl.program_id(0)
-    tokens, width = source_ref.shape
+    rows, width = sources[0].shape
+    tokens = rows * blocks
     parts = width // LANES
+    lanes = lax.broadcasted_iota(jnp.int32, (BLOCK, LANES), 1)
+
+    def hold(number, source_ref):
+        def part_of(piece, carry):
+            start = pl.multiple_of(piece * BLOCK, BLOCK)
+            first = pl.multiple_of((me_ref[0] ^ number) * rows + start, BLOCK)
+            value = source_ref[pl.ds(start, BLOCK), :].astype(F32)
+            if gated:
+                scale = lax.rsqrt(jnp.mean(value * value, axis=1, keepdims=True) + EPSILON)
+                low = (value * scale * gain_ref[...]).astype(BF16)
+                logits = jnp.dot(low, router_ref[...], preferred_element_type=F32)
+                routes = route_ref[pl.ds(first, BLOCK), :]
+                picks = [lanes == routes[:, slot : slot + 1] for slot in range(TOPK)]
+                chosen = [
+                    jnp.sum(jnp.where(pick, logits, 0.0), axis=1, keepdims=True) for pick in picks
+                ]
+                highest = jnp.maximum(chosen[0], chosen[1])
+                raised = [jnp.exp(value - highest) for value in chosen]
+                total = raised[0] + raised[1]
+                held[pl.ds(first * PITCH + parts, BLOCK, stride=PITCH), :] = jnp.where(
+                    picks[0],
+                    raised[0] / total,
+                    jnp.where(picks[1], raised[1] / total, 0.0),
+                )
+                value = low.astype(F32)
+            for part in range(parts):
+                held[pl.ds(first * PITCH + part, BLOCK, stride=PITCH), :] = value[
+                    :, part * LANES : (part + 1) * LANES
+                ]
+            return carry
+
+        lax.fori_loop(0, rows // BLOCK, part_of, 0)
 
     @pl.when(step == 0)
     def _():
         held[tokens * PITCH : (tokens + 1) * PITCH, :] = jnp.zeros((PITCH, LANES), F32)
-        for first in range(0, tokens, BLOCK):
-            for part in range(parts):
-                held[pl.ds(first * PITCH + part, BLOCK, stride=PITCH), :] = source_ref[
-                    first : first + BLOCK, part * LANES : (part + 1) * LANES
-                ].astype(F32)
-            if gated:
-                held[pl.ds(first * PITCH + parts, BLOCK, stride=PITCH), :] = weight_ref[
-                    first : first + BLOCK, :
-                ]
+        for number, source_ref in enumerate(sources):
+            hold(number, source_ref)
 
     @pl.when(step < live_ref[0])
     def _():
@@ -215,43 +242,49 @@
                 pl.ds(part, BLOCK, stride=PITCH), :
             ].astype(BF16)
         if gated:
-            lanes = lax.broadcasted_iota(jnp.int32, (BLOCK, LANES), 1)
             spare = moved[pl.ds(parts, BLOCK, stride=PITCH), :]
             own = jnp.where(lanes == expert_ref[step], spare, 0.0)
             gate_ref[...] = jnp.sum(own, axis=1, keepdims=True)
 
 
-def dispatch(source, weights, slot_token, block_expert, live):
-    tokens, width = source.shape
+def dispatch(sources, extras, slot_token, block_expert, live):
+    rows, width = sources[0].shape
+    tokens = rows * len(sources)
     slots = slot_token.shape[0]
-    gated = weights is not None
-    at = lambda i, t, e, n: (jnp.minimum(i, n[0] - 1), 0)
-    rows = pl.BlockSpec((BLOCK, width), at)
-    column = pl.BlockSpec((BLOCK, 1), at)
-
-    def whole(columns):
-        return pl.BlockSpec((tokens, columns), lambda i, t, e, n: (0, 0), pipeline_mode=pl.Buffered(1))
-
-    out = jax.ShapeDtypeStruct((slots, width), BF16)
-    gate = jax.ShapeDtypeStruct((slots, 1), F32)
+    gated = bool(extras)
+    at = lambda i, t, e, n, m: (jnp.minimum(i, n[0] - 1), 0)
+
+    def whole(value):
+        return pl.BlockSpec(
+            value.shape, lambda i, t, e, n, m: (0, 0), pipeline_mode=pl.Buffered(1)
+        )
+
+    out_specs = [pl.BlockSpec((BLOCK, width), at), pl.BlockSpec((BLOCK, 1), at)]
+    out_shape = [
+        jax.ShapeDtypeStruct((slots, width), BF16),
+        jax.ShapeDtypeStruct((slots, 1), F32),
+    ]
+    me = lax.axis_index("narrow").astype(jnp.int32)[None]
+    if len(sources) == 1:
+        me = jnp.zeros((1,), jnp.int32)
     return pl.pallas_call(
-        functools.partial(dispatch_kernel, gated),
+        functools.partial(dispatch_kernel, len(sources), gated),
         grid_spec=pltpu.PrefetchScalarGridSpec(
-            num_scalar_prefetch=3,
+            num_scalar_prefetch=4,
             grid=(slots // BLOCK,),
-            in_specs=[whole(width), whole(LANES)] if gated else [whole(width)],
-            out_specs=[rows, column] if gated else rows,
+            in_specs=[whole(value) for value in (*sources, *extras)],
+            out_specs=out_specs if gated else out_specs[:1],
             scratch_shapes=[
                 pltpu.VMEM(((tokens + 1) * PITCH, LANES), F32),
                 pltpu.VMEM((BLOCK * PITCH, LANES), F32),
             ],
         ),
-        out_shape=[out, gate] if gated else out,
+        out_shape=out_shape if gated else out_shape[:1],
         cost_estimate=pl.CostEstimate(
-            flops=20 * 10**9, bytes_accessed=24 * BLOCK * width * 2, transcendentals=0
+            flops=42 * 10**9, bytes_accessed=24 * BLOCK * width * 2, transcendentals=0
         ),
         compiler_params=pltpu.CompilerParams(vmem_limit_bytes=48 << 20),
-    )(*((slot_token, block_expert, live, source) + ((weights,) if gated else ())))
+    )(slot_token, block_expert, live, me, *sources, *extras)
 
 
 def expert_kernel(
@@ -378,13 +411,13 @@
         copy(len(jobs) - 1).wait()
 
 
-def run_experts(span, slot_token, block_expert, rows, cots, gates, weights, low, tokens):
+def run_experts(span, slot_token, block_expert, rows, cots, gates, weights, tokens):
     width = rows.shape[1]
     experts, hidden = weights.shape[1], weights.shape[3]
     index = lambda i, s: s[0] + jnp.minimum(i, s[1] - 1)
     at = lambda i, s, e, t: (index(i, s), 0)
     pick = pl.BlockSpec(
-        (3, 1, width, hidden), lambda i, s, e, t: (0, e[index(i, s)] - low, 0, 0)
+        (3, 1, width, hidden), lambda i, s, e, t: (0, e[index(i, s)] - s[2], 0, 0)
     )
     anywhere = pl.BlockSpec(memory_space=pl.ANY)
     block_count = experts * 3 // 2
@@ -420,7 +453,7 @@
             jax.ShapeDtypeStruct(weights.shape, BF16),
         ],
         cost_estimate=pl.CostEstimate(
-            flops=block_count * 2 * BLOCK * width * hidden * 9 * 3,
+            flops=block_count * 2 * BLOCK * width * hidden * 9 * 6,
             bytes_accessed=weights.size * 4 + block_count * BLOCK * width * 4,
             transcendentals=0,
         ),
@@ -433,55 +466,134 @@
     return lax.ppermute(value, "narrow", [(index, index ^ bit) for index in range(count)])
 
 
+def ordered(pieces, axis):
+    me = lax.axis_index("narrow")
+    count = len(pieces)
+    return jnp.concatenate(
+        [lax.select_n(me ^ index, *pieces) for index in range(count)], axis=axis
+    )
+
+
+def gather_blocks(value):
+    half = value.shape[0] // 2
+    one = swap(value, 1)
+    two = swap(value, 2)
+    before = yield
+    low, high = (two[:half], one[half:]) if before is None else after((two[:half], one[half:]), before)
+    far = jnp.concatenate([swap(low, 1), swap(high, 2)], axis=0)
+    yield [value, one, two, far]
+
+
+def gather_start(value):
+    if lax.axis_size("narrow") != 4:
+        return [lax.all_gather(value, "narrow", axis=0, tiled=True)]
+    rounds = gather_blocks(value)
+    next(rounds)
+    return rounds
+
+
+def gather_end(rounds, before=None):
+    return rounds if isinstance(rounds, list) else rounds.send(before)
+
+
+def gather_rows_end(rounds, before=None):
+    blocks = gather_end(rounds, before)
+    return ordered(blocks, 0) if len(blocks) > 1 else blocks[0]
+
+
 def gather_rows(value):
+    return gather_rows_end(gather_start(value))
+
+
+def sum_rows(parts, turned):
     count = lax.axis_size("narrow")
     if count != 4:
-        return lax.all_gather(value, "narrow", axis=0, tiled=True)
+        low = sum(part.astype(F32) for part in parts).astype(BF16)
+        return lax.psum_scatter(low, "narrow", scatter_dimension=0, tiled=True).astype(F32)
     me = lax.axis_index("narrow")
-    rows = value.shape[0]
+    rows = parts[0].shape[0] // count
     half = rows // 2
-    one = swap(value, 1)
-    two = swap(value, 2)
-    far_low = swap(two[:half], 1)
-    far_high = swap(one[half:], 2)
-    full = jnp.zeros((count * rows,) + value.shape[1:], value.dtype)
-    for piece, other, offset in (
-        (value, 0, 0),
-        (one, 1, 0),
-        (two, 2, 0),
-        (far_low, 3, 0),
-        (far_high, 3, half),
-    ):
-        full = lax.dynamic_update_slice_in_dim(full, piece, (me ^ other) * rows + offset, 0)
-    return full
-
-
-def sum_rows(part):
+
+    def block(other, offset):
+        if turned:
+            first = other * rows + offset
+            pieces = [lax.slice_in_dim(part, first, first + half) for part in parts]
+        else:
+            first = (me ^ other) * rows + offset
+            pieces = [lax.dynamic_slice_in_dim(part, first, half, 0) for part in parts]
+        return sum(piece.astype(F32) for piece in pieces)
+
+    def send(low_blocks, low_bit, high_blocks, high_bit):
+        both = [
+            jnp.concatenate([piece.astype(BF16) for piece in blocks], axis=0)
+            for blocks in (low_blocks, high_blocks)
+        ]
+        low_send, high_send = lax.optimization_barrier(both)
+        return swap(low_send, low_bit).astype(F32), swap(high_send, high_bit).astype(F32)
+
+    low, high = send([block(1, 0), block(3, 0)], 1, [block(2, half), block(3, half)], 2)
+    low_far, high_far = send(
+        [block(2, 0) + low[half:]], 2, [block(1, half) + high[half:]], 1
+    )
+    return jnp.concatenate(
+        [block(0, 0) + low[:half] + low_far, block(0, half) + high[:half] + high_far], axis=0
+    )
+
+
+def to_rows(value):
     count = lax.axis_size("narrow")
     if count != 4:
-        low = part.astype(BF16)
-        return lax.psum_scatter(low, "narrow", scatter_dimension=0, tiled=True).astype(F32)
+        return [lax.all_to_all(value, "narrow", split_axis=1, concat_axis=0, tiled=True)]
     me = lax.axis_index("narrow")
-    rows = part.shape[0] // count
-    half = rows // 2
-
-    def block(other, offset):
-        return lax.dynamic_slice_in_dim(part, (me ^ other) * rows + offset, half, 0)
-
-    def send(pieces, bit):
-        return swap(jnp.concatenate([piece.astype(BF16) for piece in pieces], axis=0), bit)
-
-    low = send([block(1, 0), block(3, 0)], 1).astype(F32)
-    high = send([block(2, half), block(3, half)], 2).astype(F32)
-    low_far = send([block(2, 0).astype(F32) + low[half:]], 2).astype(F32)
-    high_far = send([block(1, half).astype(F32) + high[half:]], 1).astype(F32)
-    return jnp.concatenate(
-        [
-            block(0, 0).astype(F32) + low[:half] + low_far,
-            block(0, half).astype(F32) + high[:half] + high_far,
-        ],
-        axis=0,
-    )
+    size = value.shape[1] // count
+    pieces = [
+        lax.dynamic_slice_in_dim(value, (me ^ step) * size, size, 1) for step in range(count)
+    ]
+    return [swap(piece, step) if step else piece for step, piece in enumerate(pieces)]
+
+
+def product_sum(equation, lefts, rights):
+    return sum(
+        jnp.einsum(equation, left, right, preferred_element_type=F32)
+        for left, right in zip(lefts, rights)
+    )
+
+
+def to_heads(value):
+    if len(value) == 1:
+        return lax.all_to_all(value[0], "narrow", split_axis=0, concat_axis=1, tiled=True)
+    pieces = value
+    return ordered([swap(piece, step) if step else piece for step, piece in enumerate(pieces)], 1)
+
+
+def gather_columns(value):
+    count = lax.axis_size("narrow")
+    return ordered([value] + [swap(value, step) for step in range(1, count)], 1)
+
+
+def sum_columns(part):
+    count = lax.axis_size("narrow")
+    me = lax.axis_index("narrow")
+    columns = part.shape[1] // count
+    result = lax.dynamic_slice_in_dim(part, me * columns, columns, 1)
+    for step in range(1, count):
+        piece = lax.dynamic_slice_in_dim(part, (me ^ step) * columns, columns, 1)
+        result = result + swap(piece, step)
+    return result
+
+
+def sum_all(value):
+    for axis in ("wide", "narrow"):
+        count = lax.axis_size(axis)
+        bit = 1
+        while bit < count:
+            value = value + lax.ppermute(value, axis, [(index, index ^ bit) for index in range(count)])
+            bit *= 2
+    return value
+
+
+def after(value, *others):
+    return lax.optimization_barrier((value,) + others)[0]
 
 
 def local(
@@ -510,17 +622,20 @@
         return lax.dynamic_slice_in_dim(value, row_offset, row_part, 0)
 
     inputs = gather_rows(block_input)
-    gains = lax.all_gather(
-        jnp.stack([first_gain, second_gain]), "narrow", axis=1, tiled=True
-    ).astype(F32)
+    gains = gather_columns(jnp.stack([first_gain, second_gain])).astype(F32)
     gain_one, gain_two = gains[0], gains[1]
-    router_padded = jnp.pad(router_weight, ((0, 0), (0, LANES - E)))
     input_router = lax.all_gather(
-        jnp.concatenate([query_key_value_weight, router_padded], axis=1), "wide", axis=0, tiled=True
+        jnp.concatenate(
+            [query_key_value_weight, jnp.pad(router_weight, ((0, 0), (0, LANES - E)))], axis=1
+        ),
+        "wide",
+        axis=0,
+        tiled=True,
     )
     input_full = input_router[:, :head_columns]
-    router_full = input_router[:, head_columns : head_columns + E]
-    output_full = lax.all_gather(output_weight, "wide", axis=1, tiled=True)
+    router_padded = input_router[:, head_columns:]
+    router_full = router_padded[:, :E]
+    output_part = lax.all_gather(output_weight, "wide", axis=1, tiled=True)
     lows = [sum(CHUNKS[:index]) for index in range(len(CHUNKS))]
     chunk_weights = []
     for low, size in zip(lows, CHUNKS):
@@ -530,35 +645,32 @@
 
     x_full = inputs.astype(F32)
     scale_one = lax.rsqrt(jnp.mean(x_full * x_full, axis=1, keepdims=True) + EPSILON)
-    normed_one = x_full * scale_one
-    attn_in = (normed_one * gain_one).astype(BF16)
-    late_cotangent, _ = lax.optimization_barrier((cotangent, inputs))
-    cot_full = gather_rows(late_cotangent)
+    attn_in = (x_full * scale_one * gain_one).astype(BF16)
     projected = jnp.einsum(
         "td,dc->ct", attn_in, input_full, preferred_element_type=F32
     ).astype(BF16)
+    output_rounds = gather_start(after(output_part, projected))
+    cot_rounds = gather_start(after(cotangent, projected))
     mixed, log_totals = attend_forward(projected, groups, heads)
-    branch_part = jnp.einsum("ct,cd->td", mixed, output_full, preferred_element_type=F32)
-    middle_own = block_input.astype(F32) + sum_rows(branch_part)
-    middle = gather_rows(middle_own.astype(BF16)).astype(F32)
-    scale_two = lax.rsqrt(jnp.mean(middle * middle, axis=1, keepdims=True) + EPSILON)
-    normed_two = middle * scale_two
-    expert_in = (normed_two * gain_two).astype(BF16)
-    logits = jnp.dot(expert_in, router_full, preferred_element_type=F32)
-    picked = (routes[:, :, None] == jnp.arange(E, dtype=jnp.int32)[None, None, :]).astype(F32)
-    chosen = jnp.sum(picked * logits[:, None, :], axis=2)
-    gates = jax.nn.softmax(chosen, axis=1)
-    gate_lanes = jnp.pad(jnp.sum(picked * gates[:, :, None], axis=1), ((0, 0), (0, LANES - E)))
+    mixed_own = to_rows(mixed)
+    output_blocks = gather_end(output_rounds, mixed)
+    middle_own = block_input.astype(F32) + product_sum("ct,cd->td", mixed_own, output_blocks)
+    middle_low = middle_own.astype(BF16)
+    cot_blocks = gather_end(cot_rounds, middle_low)
     live = block_ends[E - 1 :]
-    cot_rows = dispatch(cot_full, None, slot_token, block_expert, live)
-    rows, slot_gates = dispatch(expert_in, gate_lanes, slot_token, block_expert, live)
+    (cot_rows,) = dispatch(cot_blocks, (), slot_token, block_expert, live)
+    middle_blocks = gather_end(gather_start(middle_low))
+    rows, slot_gates = dispatch(
+        middle_blocks, (gain_two[None], router_padded, routes), slot_token, block_expert, live
+    )
 
     outs, backs, scores, grads = [], [], [], []
     for low, size, weights in zip(lows, CHUNKS, chunk_weights):
         first = block_ends[low - 1 : low] if low else jnp.zeros((1,), jnp.int32)
         count = block_ends[low + size - 1 : low + size] - first
         out, back, score, grad = run_experts(
-            jnp.concatenate([first, count]), slot_token, block_expert, rows, cot_rows, slot_gates, weights, low, tokens
+            jnp.concatenate([first, count, jnp.full((1,), low, jnp.int32)]),
+            slot_token, block_expert, rows, cot_rows, slot_gates, weights, tokens
         )
         outs.append(out)
         backs.append(back)
@@ -568,50 +680,86 @@
     def total(values):
         return sum(value.astype(F32) for value in values)
 
-    expert_sum = sum_rows(total(backs))
+    expert_sum = sum_rows(backs, False)
+    picked = (routes[:, :, None] == jnp.arange(E, dtype=jnp.int32)[None, None, :]).astype(F32)
     score_part = jnp.sum(picked * total(scores)[:, None, :E], axis=2)
-    score_sum = lax.psum_scatter(score_part, "narrow", scatter_dimension=0, tiled=True)
-    block_output = (middle_own + sum_rows(total(outs))).astype(BF16)
-
-    gates_own = own_rows(gates)
+    score_sum = sum_columns(score_part.T).T
+
+    middle_back = after(middle_low, rows).astype(F32)
+    scale_two_own = lax.rsqrt(jnp.mean(middle_back * middle_back, axis=1, keepdims=True) + EPSILON)
+    normed_two_own = middle_back * scale_two_own
+    expert_in_own = (normed_two_own * gain_two).astype(BF16)
+    picked_own = own_rows(picked)
+    logits_own = jnp.dot(expert_in_own, router_full, preferred_element_type=F32)
+    gates_own = jax.nn.softmax(jnp.sum(picked_own * logits_own[:, None, :], axis=2), axis=1)
     centre = jnp.sum(gates_own * score_sum, axis=1, keepdims=True)
     logit_part = gates_own * (score_sum - centre)
-    logit_grad = jnp.sum(own_rows(picked) * logit_part[:, :, None], axis=1).astype(BF16)
+    logit_grad = jnp.sum(picked_own * logit_part[:, :, None], axis=1).astype(BF16)
     norm_grad = expert_sum + jnp.einsum(
         "te,de->td", logit_grad, router_full, preferred_element_type=F32
     )
-    normed_two_own = own_rows(normed_two)
     row_dot = jnp.sum(norm_grad * normed_two_own * gain_two, axis=1, keepdims=True)
     gain_two_part = jnp.sum(norm_grad * normed_two_own, axis=0)
-    mid_grad = cotangent.astype(F32) + own_rows(scale_two) * (
+    mid_grad = cotangent.astype(F32) + scale_two_own * (
         gain_two * norm_grad - normed_two_own * row_dot / width
     )
-    branch_grad = gather_rows(mid_grad.astype(BF16))
-    logit_full = lax.all_gather(logit_grad, "narrow", axis=0, tiled=True)
-    mixed_grad = jnp.einsum(
-        "td,cd->ct", branch_grad, output_full, preferred_element_type=F32
-    ).astype(BF16)
+    branch_grad = mid_grad.astype(BF16)
+    mixed_grad_own = [
+        jnp.einsum("td,cd->ct", branch_grad, block, preferred_element_type=F32).astype(BF16)
+        for block in output_blocks
+    ]
+    mixed_grad = to_heads(mixed_grad_own)
     projected_grad = attend_backward(projected, mixed, log_totals, mixed_grad, groups, heads)
-    input_part = jnp.einsum("ct,dc->td", projected_grad, input_full, preferred_element_type=F32)
     grad_input_w = jnp.einsum(
         "td,ct->dc", attn_in, projected_grad, preferred_element_type=F32
     ).astype(BF16)
-    grad_output_w = jnp.einsum(
-        "ct,td->cd", mixed, branch_grad, preferred_element_type=F32
+    input_part = jnp.einsum(
+        "ct,dc->td", after(projected_grad, grads[0]), input_full, preferred_element_type=F32
     ).astype(BF16)
-    grad_router = jnp.einsum("td,te->de", expert_in, logit_full, preferred_element_type=F32)
-    router_grad = lax.psum_scatter(grad_router, "wide", scatter_dimension=0, tiled=True)
-    output_w_grad = lax.psum_scatter(grad_output_w, "wide", scatter_dimension=1, tiled=True)
-    input_w_grad = lax.psum_scatter(grad_input_w, "wide", scatter_dimension=0, tiled=True)
-    gain_one_part = jnp.sum(input_part * normed_one, axis=0)
-    gain_pair = lax.psum(jnp.stack([gain_one_part, gain_two_part]), ("wide", "narrow"))
-    gain_own = lax.dynamic_slice_in_dim(gain_pair, me * gain_part, gain_part, 1)
-    input_sum = sum_rows(input_part)
-    normed_one_own = own_rows(normed_one)
+    input_sum = sum_rows([input_part], False)
+    grad_output_w = sum_rows(
+        [
+            jnp.concatenate(
+                [
+                    jnp.einsum("ct,td->cd", block, branch_grad, preferred_element_type=F32).astype(
+                        BF16
+                    )
+                    for block in after(mixed_own, input_sum)
+                ],
+                axis=0,
+            )
+        ],
+        True,
+    ).astype(BF16)
+    block_output = (
+        middle_own + sum_rows(after(outs, input_sum), False)
+    ).astype(BF16)
+    grad_router = jnp.einsum(
+        "te,td->ed", logit_grad, expert_in_own, preferred_element_type=F32
+    )
+    x_own = after(block_input, projected_grad).astype(F32)
+    scale_one_own = lax.rsqrt(jnp.mean(x_own * x_own, axis=1, keepdims=True) + EPSILON)
+    normed_one_own = x_own * scale_one_own
+    gain_one_part = jnp.sum(input_sum * normed_one_own, axis=0)
+    small_sum = sum_all(
+        jnp.concatenate([grad_router, gain_one_part[None], gain_two_part[None]], axis=0)
+    )
+    gain_own = lax.dynamic_slice_in_dim(small_sum[E:], me * gain_part, gain_part, 1)
+    router_part = router_weight.shape[0]
+    router_grad = lax.dynamic_slice_in_dim(
+        small_sum[:E], lax.axis_index("wide") * router_part, router_part, 1
+    ).T
     input_dot = jnp.sum(input_sum * normed_one_own * gain_one, axis=1, keepdims=True)
-    input_grad = mid_grad + own_rows(scale_one) * (
+    input_grad = mid_grad + scale_one_own * (
         gain_one * input_sum - normed_one_own * input_dot / width
     )
+    input_w_grad = lax.psum_scatter(
+        after(grad_input_w, grads[1], input_grad), "wide", scatter_dimension=0, tiled=True
+    )
+    output_w_grad = lax.psum_scatter(
+        after(grad_output_w, grads[1]), "wide", scatter_dimension=1, tiled=True
+    )
+    grads = after(grads, block_output, small_sum, grad_output_w, input_grad)
     gate_grad, up_grad, down_grad = (
         jnp.concatenate([grad[index] for grad in grads], axis=0).astype(F32) for index in range(3)
     )

time: 1350 us -> 903 us (0.67)
  waiting for transfers between devices: 483 us -> 310 us
  blocking collectives: 126 us -> 0 us
  Pallas kernels: 403 us -> 286 us
  other arithmetic: 125 us -> 101 us
  starting transfers between devices: 36.9 us -> 57.1 us
  local copies, waits for them, and re-layouts: 89.5 us -> 69.9 us
    reduce_scatter x4 -> x3, waiting for transfers between devices: 238 us -> 13.1 us  [local(): lax.psum_scatter(grad, 'wide', scatter_dimension=2, tiled=True)]
    pallas_call x4 -> x3, Pallas kernels: 240 us -> 149 us  [run_experts(): pl.pallas_call(expert_kernel, grid_spec=pltpu.PrefetchScalarGridSpec(num_...]
    all_gather x2 -> x0, blocking collectives: 75.5 us -> none  [the longest x1 38 us: local(): logit_full = lax.all_gather(logit_grad, 'narrow', axis=0, tiled=True)]
    psum x1 -> x0, blocking collectives: 50.4 us -> none  [local(): lax.psum(jnp.stack([gain_one_part, gain_two_part]), ('wide', 'narrow'))]
    ppermute x0 -> x5, waiting for transfers between devices: none -> 48.4 us  [sum_all(): lax.ppermute(value, axis, [(index, index ^ bit) for index in range(count)])]
    ppermute x32 -> x44, waiting for transfers between devices: 218 us -> 189 us  [swap(): lax.ppermute(value, 'narrow', [(index, index ^ bit) for index in range(co...]
    pallas_call x2, Pallas kernels: 76.4 us -> 50.3 us  [dispatch(): pl.pallas_call(functools.partial(dispatch_kernel, len(sources), gated), g...]
    reduce_scatter x2 -> x1, waiting for transfers between devices: 0.01 us -> 25.2 us  [local(): lax.psum_scatter(after(grad_input_w, grads[1], input_grad), 'wide', scatt...]
  transfers between devices with their start and end apart: 46 -> 59, of which waited for: 25 -> 26; matrix products, arithmetic and copies ran while one was open for 16% -> 22% of each run, Pallas kernels for 25% -> 32%
where the time goes in v3:
time: 903 us; the launch traced here: 894 us
  waiting for transfers between devices  310 us (34%)
  Pallas kernels  286 us (32%)
  other arithmetic  101 us (11%)
  local copies, waits for them, and re-layouts  69.9 us (8%)
  starting transfers between devices  57.1 us (6%)
  matrix products  50.9 us (6%)
  between operations  18.5 us (2%)
    ppermute x44, waiting for transfers between devices, swap(): lax.ppermute(value, 'narrow', [(index, index ^ bit) for index in range(co...  189 us
    pallas_call x3, Pallas kernels, run_experts(): pl.pallas_call(expert_kernel, grid_spec=pltpu.PrefetchScalarGridSpec(num_...  149 us
    ppermute x44, starting transfers between devices, swap(): lax.ppermute(value, 'narrow', [(index, index ^ bit) for index in range(co...  55 us
    pallas_call x2, Pallas kernels, dispatch(): pl.pallas_call(functools.partial(dispatch_kernel, len(sources), gated), g...  50.3 us
    ppermute x5, waiting for transfers between devices, sum_all(): lax.ppermute(value, axis, [(index, index ^ bit) for index in range(count)])  48.4 us
    pallas_call x1, Pallas kernels, attend_backward(): pl.pallas_call(functools.partial(backward_kernel, heads), grid=(groups, b...  48.2 us
    pallas_call x1, Pallas kernels, attend_forward(): pl.pallas_call(functools.partial(forward_kernel, heads), grid=(groups, bl...  38.2 us
    unnamed x11, waiting for transfers between devices  32.6 us
  transfers between devices with their start and end apart: 59, of which 26 were waited for; matrix products, arithmetic and copies ran while one was open for 22% of the time, Pallas kernels for 32%

profile of v3, /device:TPU:0, one launch (start us, length us, event | category | flops | bytes accessed | tf_op | source)
XLA Modules:
  0.0 893.6 jit_solution(6398115823070523090)
XLA Ops:
  35.6 23.0 %collective-permute-done.1 = bf16[512,1536]{1,0:T(8,128)(2,1)} collective-permute-done((bf16[512,1536]{1,0:T(8,128)(2,1)S(1)}, bf16[512,1536]{1,0:T(8,128)(2,1)}, u32[]{:S(2)}, u32[]{:S(2)}) %collective-permute-start.1) | collective-permute-done | bytes 1572896 | tf_op jit(solution)/shard_map/ppermute | solution.py:466
  64.8 13.5 %collective-permute-done.2 = bf16[256,1536]{1,0:T(8,128)(2,1)} collective-permute-done((bf16[256,1536]{1,0:T(8,128)(2,1)}, bf16[256,1536]{1,0:T(8,128)(2,1)}, u32[]{:S(2)}, u32[]{:S(2)}) %collective-permute-start.2) | collective-permute-done | bytes 786464 | tf_op jit(solution)/shard_map/ppermute | solution.py:466
  85.6 10.8 %convolution_convert_fusion.2.qkv_ref = bf16[640,2048]{1,0:T(8,128)(2,1)} fusion(f32[1536]{0:T(1024)S(1)} %get-tuple-element.173, f32[2048]{0:T(1024)S(1)} %add_rsqrt_fusion, bf16[1536,768]{1,0:T(8,128)(2,1)} %all-gather.6.cloned.1.call-done, bf16[512,1536]{1,0:T(8,128)(2,1)} %copy-done.26, bf16[512,1536]{1,0:T(8,128)(2,1)} %copy-done.28, ...), kind=kOutput, calls=%fused_computation.22 | convolution fusion | flops 4062445568 | bytes 10893312 | tf_op jit(solution)/shard_map/td,dc->ct/dot_general | solution.py:649
  102.3 38.2 %shard_map.186 = (bf16[384,2048]{1,0:T(8,128)(2,1)S(1)}, f32[2,8,1,768]{3,2,1,0:T(1,128)S(1)}) custom-call(bf16[640,2048]{1,0:T(8,128)(2,1)S(1)} %copy-done.11), custom_call_target="tpu_custom_call" | custom-call | flops 45097156608 | bytes 5242880 | tf_op jit(solution)/shard_map/pallas_call | solution.py:77
  157.2 11.7 %collective-permute-done.7 = bf16[384,512]{1,0:T(8,128)(2,1)} collective-permute-done((bf16[384,512]{1,0:T(8,128)(2,1)}, bf16[384,512]{1,0:T(8,128)(2,1)}, u32[]{:S(2)}, u32[]{:S(2)}) %collective-permute-start.7) | collective-permute-done | bytes 393248 | tf_op jit(solution)/shard_map/ppermute | solution.py:466
  182.6 4.8 collective-permute-done.13
  197.7 15.5 %scatter_custom_fusion.token_ref = s32[8192]{0:T(1024)S(1)} fusion(s32[4096]{0:T(1024)S(1)} %bitcast.120, s32[4096]{0:T(1024)S(1)} %add_select_fusion, s32[]{:T(128)} %constant.86.clone.1), kind=kCustom, calls=%fused_computation.188 | custom fusion | bytes 32772 | tf_op jit(solution)/shard_map/scatter | solution.py:170
  216.2 25.6 %collective-permute-done.20 = bf16[256,1536]{1,0:T(8,128)(2,1)} collective-permute-done((bf16[256,1536]{1,0:T(8,128)(2,1)}, bf16[256,1536]{1,0:T(8,128)(2,1)}, u32[]{:S(2)}, u32[]{:S(2)}) %collective-permute-start.20) | collective-permute-done | bytes 786464 | tf_op jit(solution)/shard_map/ppermute | solution.py:466
  248.5 22.6 %shard_map.188.cot_ref = bf16[8192,1536]{1,0:T(8,128)(2,1)} custom-call(s32[8192]{0:T(1024)S(1)} %scatter_custom_fusion.token_ref, s32[32]{0:T(128)S(1)} %broadcast_minimum_fusion.expert_ref, s32[1]{0:T(128)} %bitcast.5.live_ref, s32[1]{0:T(128)} %bitcast.6.me_ref, bf16[512,1536]{1,0:T(8,128)(2,1)S(1)} %copy-done.3, ...), custom_call_target="tpu_custom_call" | custom-call | flops 41999998976 | bytes 18874368 | tf_op jit(solution)/shard_map/pallas_call | solution.py:270
  272.4 27.6 %shard_map.187 = (bf16[8192,1536]{1,0:T(8,128)(2,1)}, f32[8192,1]{1,0:T(8,128)}) custom-call(s32[8192]{0:T(1024)S(1)} %scatter_custom_fusion.token_ref, s32[32]{0:T(128)S(1)} %broadcast_minimum_fusion.expert_ref, s32[1]{0:T(128)} %bitcast.5.live_ref, s32[1]{0:T(128)} %bitcast.6.me_ref, bf16[512,1536]{1,0:T(8,128)(2,1)S(1)} %get-tuple-element.76.refs_0_, ...), custom_call_target="tpu_custom_call" | custom-call | flops 41999998976 | bytes 18874368 | tf_op jit(solution)/shard_map/pallas_call | solution.py:270
  300.1 58.0 %shard_map.189 = (bf16[2048,1536]{1,0:T(8,128)(2,1)}, bf16[2048,1536]{1,0:T(8,128)(2,1)}, f32[2048,128]{1,0:T(8,128)}, bf16[3,6,1536,256]{3,2,1,0:T(8,128)(2,1)}) custom-call(s32[3]{0:T(128)} %pad_add_fusion.span_ref, s32[32]{0:T(128)} %copy-done.8, s32[8192]{0:T(1024)} %copy-done.7, bf16[8192,1536]{1,0:T(8,128)(2,1)} %get-tuple-element.67.row_ref, ...), custom_call_target="tpu_custom_call" | custom-call | flops 97844723712 | bytes 42467328 | tf_op jit(solution)/shard_map/pallas_call | solution.py:424
  360.6 54.1 %shard_map.190 = (bf16[2048,1536]{1,0:T(8,128)(2,1)}, bf16[2048,1536]{1,0:T(8,128)(2,1)}, f32[2048,128]{1,0:T(8,128)}, bf16[3,6,1536,256]{3,2,1,0:T(8,128)(2,1)}) custom-call(s32[3]{0:T(128)} %pad_add_fusion.1.span_ref, s32[32]{0:T(128)} %copy-done.8, s32[8192]{0:T(1024)} %copy-done.7, bf16[8192,1536]{1,0:T(8,128)(2,1)} %get-tuple-element.67.row_ref, ...), custom_call_target="tpu_custom_call" | custom-call | flops 97844723712 | bytes 42467328 | tf_op jit(solution)/shard_map/pallas_call | solution.py:424
  419.8 36.9 %shard_map.191 = (bf16[2048,1536]{1,0:T(8,128)(2,1)}, bf16[2048,1536]{1,0:T(8,128)(2,1)}, f32[2048,128]{1,0:T(8,128)}, bf16[3,4,1536,256]{3,2,1,0:T(8,128)(2,1)}) custom-call(s32[3]{0:T(128)} %pad_add_fusion.2.span_ref, s32[32]{0:T(128)} %copy-done.8, s32[8192]{0:T(1024)} %copy-done.7, bf16[8192,1536]{1,0:T(8,128)(2,1)} %get-tuple-element.67.row_ref, ...), custom_call_target="tpu_custom_call" | custom-call | flops 65229815808 | bytes 28311552 | tf_op jit(solution)/shard_map/pallas_call | solution.py:424
  456.7 5.0 add_convert_fusion.5
  471.7 29.3 %collective-permute-done.22 = bf16[512,1536]{1,0:T(8,128)(2,1)} collective-permute-done((bf16[512,1536]{1,0:T(8,128)(2,1)}, bf16[512,1536]{1,0:T(8,128)(2,1)}, u32[]{:S(2)}, u32[]{:S(2)}) %collective-permute-start.22) | collective-permute-done | bytes 1572896 | tf_op jit(solution)/shard_map/ppermute | solution.py:466
  505.8 5.7 fusion.37
  518.2 13.9 %collective-permute-done.26 = f32[2,512]{1,0:T(2,128)S(1)} collective-permute-done((f32[2,512]{1,0:T(2,128)S(1)}, f32[2,512]{1,0:T(2,128)S(1)}, u32[]{:S(2)}, u32[]{:S(2)}) %collective-permute-start.26) | collective-permute-done | bytes 4128 | tf_op jit(solution)/shard_map/ppermute | solution.py:466
  548.3 5.6 collective-permute-done.29
  554.0 8.8 collective-permute-done.30
  565.2 48.2 %shard_map.192 = bf16[640,2048]{1,0:T(8,128)(2,1)S(1)} custom-call(bf16[640,2048]{1,0:T(8,128)(2,1)S(1)} %copy-done.12, bf16[384,2048]{1,0:T(8,128)(2,1)S(1)} %copy-done.6, f32[2,8,1,768]{3,2,1,0:T(1,128)S(1)} %get-tuple-element.75.total_ref, bf16[384,2048]{1,0:T(8,128)(2,1)S(1)} %pad_maximum_fusion.8.grad_ref), custom_call_target="tpu_custom_call" | custom-call | flops 56371445760 | bytes 10485760 | tf_op jit(solution)/shard_map/pallas_call | solution.py:139
  615.0 7.4 convolution_convert_fusion
  626.2 28.6 %collective-permute-done.32 = bf16[512,1536]{1,0:T(8,128)(2,1)S(1)} collective-permute-done((bf16[512,1536]{1,0:T(8,128)(2,1)S(1)}, bf16[512,1536]{1,0:T(8,128)(2,1)S(1)}, u32[]{:S(2)}, u32[]{:S(2)}) %collective-permute-start.32) | collective-permute-done | bytes 1572896 | tf_op jit(solution)/shard_map/ppermute | solution.py:466
  664.2 7.2 convolution_convert_fusion.1
  696.1 13.1 %reduce-scatter.10.cloned.1.call-done = bf16[3,6,192,256]{3,2,1,0:T(8,128)(2,1)} async-done(((bf16[3,6,1536,256]{3,2,1,0:T(8,128)(2,1)}), bf16[3,6,192,256]{3,2,1,0:T(8,128)(2,1)}) %reduce-scatter.10.cloned.1.call-update) | async-done | bytes 1769488 | tf_op jit(solution)/shard_map/reduce_scatter | solution.py:678
  712.4 5.3 add_convert_fusion.1
  720.0 13.0 %collective-permute-done.42 = f32[18,1536]{1,0:T(8,128)S(1)} collective-permute-done((f32[18,1536]{1,0:T(8,128)S(1)}, f32[18,1536]{1,0:T(8,128)S(1)}, u32[]{:S(2)}, u32[]{:S(2)}) %collective-permute-start.42) | collective-permute-done | bytes 110624 | tf_op jit(solution)/shard_map/ppermute | solution.py:590
  736.1 4.7 collective-permute-done.43
  742.9 30.7 %collective-permute-done.44 = f32[18,1536]{1,0:T(8,128)S(1)} collective-permute-done((f32[18,1536]{1,0:T(8,128)S(1)}, f32[18,1536]{1,0:T(8,128)S(1)}, u32[]{:S(2)}, u32[]{:S(2)}) %collective-permute-start.44) | collective-permute-done | bytes 110624 | tf_op jit(solution)/shard_map/ppermute | solution.py:590
  784.9 5.6 fusion.29
  799.3 9.8 %collective-permute-done.38 = bf16[256,1536]{1,0:T(8,128)(2,1)} collective-permute-done((bf16[256,1536]{1,0:T(8,128)(2,1)}, bf16[256,1536]{1,0:T(8,128)(2,1)}, u32[]{:S(2)}, u32[]{:S(2)}) %collective-permute-start.38) | collective-permute-done | bytes 786464 | tf_op jit(solution)/shard_map/ppermute | solution.py:466
  825.8 25.2 %reduce-scatter.12.cloned.1.call-done = bf16[192,640]{1,0:T(8,128)(2,1)} async-done(((bf16[1536,640]{1,0:T(8,128)(2,1)}), bf16[192,640]{1,0:T(8,128)(2,1)}) %reduce-scatter.12.cloned.1.call-update) | async-done | bytes 245776 | tf_op jit(solution)/shard_map/reduce_scatter | solution.py:756
  852.8 31.7 %reduce-scatter.16.cloned.1.call-done = bf16[192,384]{1,0:T(8,128)(2,1)} async-done(((bf16[1536,384]{1,0:T(8,128)(2,1)}), bf16[192,384]{1,0:T(8,128)(2,1)}) %reduce-scatter.16.cloned.1.call-update) | async-done | bytes 147472
  (404 shorter events, 233.6 us)
Async XLA Ops:
  7.2 78.4 %all-gather.6.cloned.1.call-start = ((), (), s32[]{:S(2)}) async-start(), calls=%async_computation.5 | async-start | bytes 2654208 | tf_op jit(solution)/shard_map/all_gather | solution.py:627
  9.9 86.5 %all-gather.8.cloned.1.call-start = ((), (), s32[]{:S(2)}) async-start(), calls=%async_computation.6 | async-start | bytes 1327104 | tf_op jit(solution)/shard_map/all_gather | solution.py:638
  10.6 289.4 %all-gather.10.cloned.1.call-start = ((), (), s32[]{:S(2)}) async-start(), calls=%async_computation.7 | async-start | bytes 15925248 | tf_op jit(solution)/shard_map/all_gather | solution.py:643
  14.8 345.8 %all-gather.12.cloned.1.call-start = ((), (), s32[]{:S(2)}) async-start(), calls=%async_computation.8 | async-start | bytes 15925248 | tf_op jit(solution)/shard_map/all_gather | solution.py:643
  16.3 403.5 %all-gather.14.cloned.1.call-start = ((), (), s32[]{:S(2)}) async-start(), calls=%async_computation.9 | async-start | bytes 10616832 | tf_op jit(solution)/shard_map/all_gather | solution.py:643
  17.0 47.1 %collective-permute-start.5 = (bf16[2,384]{1,0:T(2,128)(2,1)S(1)}, bf16[2,384]{1,0:T(2,128)(2,1)S(1)}, u32[]{:S(2)}, u32[]{:S(2)}) collective-permute-start(bf16[2,384]{1,0:T(2,128)(2,1)S(1)} %pad_maximum_fusion.18), channel_id=1, source_target_pairs={{0,2},{1,3},{2,0},{3,1},{4,6},{5,7},{6,4},{7,5},{8,10},{9,11},{10,... | collective-permute-start | bytes 4616 | tf_op jit(solution)/shard_map/ppermute | solution.py:466
  20.0 44.0 %collective-permute-start.6 = (bf16[2,384]{1,0:T(2,128)(2,1)S(1)}, bf16[2,384]{1,0:T(2,128)(2,1)S(1)}, u32[]{:S(2)}, u32[]{:S(2)}) collective-permute-start(bf16[2,384]{1,0:T(2,128)(2,1)S(1)} %pad_maximum_fusion.18), channel_id=1, source_target_pairs={{0,3},{1,2},{2,1},{3,0},{4,7},{5,6},{6,5},{7,4},{8,11},{9,10},{10,... | collective-permute-start | bytes 4616 | tf_op jit(solution)/shard_map/ppermute | solution.py:466
  21.5 42.6 %collective-permute-start.4 = (bf16[2,384]{1,0:T(2,128)(2,1)S(1)}, bf16[2,384]{1,0:T(2,128)(2,1)S(1)}, u32[]{:S(2)}, u32[]{:S(2)}) collective-permute-start(bf16[2,384]{1,0:T(2,128)(2,1)S(1)} %pad_maximum_fusion.18), channel_id=1, source_target_pairs={{0,1},{1,0},{2,3},{3,2},{4,5},{5,4},{6,7},{7,6},{8,9},{9,8},{10,11... | collective-permute-start | bytes 4616 | tf_op jit(solution)/shard_map/ppermute | solution.py:466
  21.6 39.6 %collective-permute-start = (bf16[512,1536]{1,0:T(8,128)(2,1)S(1)}, bf16[512,1536]{1,0:T(8,128)(2,1)}, u32[]{:S(2)}, u32[]{:S(2)}) collective-permute-start(bf16[512,1536]{1,0:T(8,128)(2,1)S(1)} %copy-done.13), channel_id=1, source_target_pairs={{0,1},{1,0},{2,3},{3,2},{4,5},{5,4},{6,7},{7,6},{8,9},{9,8},{10,11... | collective-permute-start | bytes 4718600 | tf_op jit(solution)/shard_map/ppermute | solution.py:466
  23.5 35.1 %collective-permute-start.1 = (bf16[512,1536]{1,0:T(8,128)(2,1)S(1)}, bf16[512,1536]{1,0:T(8,128)(2,1)}, u32[]{:S(2)}, u32[]{:S(2)}) collective-permute-start(bf16[512,1536]{1,0:T(8,128)(2,1)S(1)} %copy-done.13), channel_id=1, source_target_pairs={{0,2},{1,3},{2,0},{3,1},{4,6},{5,7},{6,4},{7,5},{8,10},{9,11},{10,... | collective-permute-start | bytes 4718600 | tf_op jit(solution)/shard_map/ppermute | solution.py:466
  28.4 586.6 %reduce-scatter.8.cloned.1.call-start = ((), (), s32[]{:S(2)}) async-start(), calls=%async_computation.10 | async-start | bytes 15925248 | tf_op jit(solution)/shard_map/reduce_scatter | solution.py:678
  96.4 46.8 %collective-permute-start.10 = (bf16[384,1536]{0,1:T(8,128)(2,1)}, bf16[384,1536]{0,1:T(8,128)(2,1)S(1)}, u32[]{:S(2)}, u32[]{:S(2)}) collective-permute-start(bf16[384,1536]{0,1:T(8,128)(2,1)} %all-gather.8.cloned.1.call-done), channel_id=1, source_target_pairs={{0,2},{1,3},{2,0},{3,1},{4,6},{5,7},{6,4},{7,5},{8,10},{9,11},{10,... | collective-permute-start | bytes 3538952 | tf_op jit(solution)/shard_map/ppermute | solution.py:466
  97.5 48.2 %collective-permute-start.8 = (bf16[384,1536]{0,1:T(8,128)(2,1)}, bf16[384,1536]{0,1:T(8,128)(2,1)S(1)}, u32[]{:S(2)}, u32[]{:S(2)}) collective-permute-start(bf16[384,1536]{0,1:T(8,128)(2,1)} %all-gather.8.cloned.1.call-done), channel_id=1, source_target_pairs={{0,1},{1,0},{2,3},{3,2},{4,5},{5,4},{6,7},{7,6},{8,9},{9,8},{10,11... | collective-permute-start | bytes 3538952 | tf_op jit(solution)/shard_map/ppermute | solution.py:466
  98.9 74.4 %collective-permute-start.19 = (bf16[512,1536]{1,0:T(8,128)(2,1)S(1)}, bf16[512,1536]{1,0:T(8,128)(2,1)}, u32[]{:S(2)}, u32[]{:S(2)}) collective-permute-start(bf16[512,1536]{1,0:T(8,128)(2,1)S(1)} %copy-done.2), channel_id=1, source_target_pairs={{0,2},{1,3},{2,0},{3,1},{4,6},{5,7},{6,4},{7,5},{8,10},{9,11},{10,... | collective-permute-start | bytes 4718600 | tf_op jit(solution)/shard_map/ppermute | solution.py:466
  99.4 78.0 %collective-permute-start.18 = (bf16[512,1536]{1,0:T(8,128)(2,1)S(1)}, bf16[512,1536]{1,0:T(8,128)(2,1)}, u32[]{:S(2)}, u32[]{:S(2)}) collective-permute-start(bf16[512,1536]{1,0:T(8,128)(2,1)S(1)} %copy-done.2), channel_id=1, source_target_pairs={{0,1},{1,0},{2,3},{3,2},{4,5},{5,4},{6,7},{7,6},{8,9},{9,8},{10,11... | collective-permute-start | bytes 4718600 | tf_op jit(solution)/shard_map/ppermute | solution.py:466
  143.2 45.5 %collective-permute-start.9 = (bf16[384,512]{1,0:T(8,128)(2,1)}, bf16[384,512]{1,0:T(8,128)(2,1)}, u32[]{:S(2)}, u32[]{:S(2)}) collective-permute-start(bf16[384,512]{1,0:T(8,128)(2,1)} %get-tuple-element.221), channel_id=1, source_target_pairs={{0,2},{1,3},{2,0},{3,1},{4,6},{5,7},{6,4},{7,5},{8,10},{9,11},{10,... | collective-permute-start | bytes 1179656 | tf_op jit(solution)/shard_map/ppermute | solution.py:466
  193.6 50.9 %collective-permute-start.15 = (bf16[512,1536]{1,0:T(8,128)(2,1)S(1)}, bf16[512,1536]{1,0:T(8,128)(2,1)}, u32[]{:S(2)}, u32[]{:S(2)}) collective-permute-start(bf16[512,1536]{1,0:T(8,128)(2,1)S(1)} %get-tuple-element.76.refs_0_), channel_id=1, source_target_pairs={{0,2},{1,3},{2,0},{3,1},{4,6},{5,7},{6,4},{7,5},{8,10},{9,11},{10,... | collective-permute-start | bytes 4718600 | tf_op jit(solution)/shard_map/ppermute | solution.py:466
  194.6 52.3 %collective-permute-start.14 = (bf16[512,1536]{1,0:T(8,128)(2,1)S(1)}, bf16[512,1536]{1,0:T(8,128)(2,1)}, u32[]{:S(2)}, u32[]{:S(2)}) collective-permute-start(bf16[512,1536]{1,0:T(8,128)(2,1)S(1)} %get-tuple-element.76.refs_0_), channel_id=1, source_target_pairs={{0,1},{1,0},{2,3},{3,2},{4,5},{5,4},{6,7},{7,6},{8,9},{9,8},{10,11... | collective-permute-start | bytes 4718600 | tf_op jit(solution)/shard_map/ppermute | solution.py:466
  195.5 46.3 %collective-permute-start.20 = (bf16[256,1536]{1,0:T(8,128)(2,1)}, bf16[256,1536]{1,0:T(8,128)(2,1)}, u32[]{:S(2)}, u32[]{:S(2)}) collective-permute-start(bf16[256,1536]{1,0:T(8,128)(2,1)} %slice.290), channel_id=1, source_target_pairs={{0,1},{1,0},{2,3},{3,2},{4,5},{5,4},{6,7},{7,6},{8,9},{9,8},{10,11... | collective-permute-start | bytes 2359304 | tf_op jit(solution)/shard_map/ppermute | solution.py:466
  196.6 45.2 %collective-permute-start.21 = (bf16[256,1536]{1,0:T(8,128)(2,1)}, bf16[256,1536]{1,0:T(8,128)(2,1)}, u32[]{:S(2)}, u32[]{:S(2)}) collective-permute-start(bf16[256,1536]{1,0:T(8,128)(2,1)} %slice.291), channel_id=1, source_target_pairs={{0,2},{1,3},{2,0},{3,1},{4,6},{5,7},{6,4},{7,5},{8,10},{9,11},{10,... | collective-permute-start | bytes 2359304 | tf_op jit(solution)/shard_map/ppermute | solution.py:466
  358.0 351.2 %reduce-scatter.10.cloned.1.call-start = ((), (), s32[]{:S(2)}) async-start(), calls=%async_computation.11 | async-start | bytes 15925248 | tf_op jit(solution)/shard_map/reduce_scatter | solution.py:678
  414.7 401.9 %reduce-scatter.14.cloned.1.call-start = ((), (), s32[]{:S(2)}) async-start(), calls=%async_computation.13 | async-start | bytes 10616832 | tf_op jit(solution)/shard_map/reduce_scatter | solution.py:678
  464.2 36.9 %collective-permute-start.22 = (bf16[512,1536]{1,0:T(8,128)(2,1)}, bf16[512,1536]{1,0:T(8,128)(2,1)}, u32[]{:S(2)}, u32[]{:S(2)}) collective-permute-start(bf16[512,1536]{1,0:T(8,128)(2,1)} %pad_maximum_fusion.6), channel_id=1, source_target_pairs={{0,1},{1,0},{2,3},{3,2},{4,5},{5,4},{6,7},{7,6},{8,9},{9,8},{10,11... | collective-permute-start | bytes 4718600 | tf_op jit(solution)/shard_map/ppermute | solution.py:466
  465.6 37.3 %collective-permute-start.23 = (bf16[512,1536]{1,0:T(8,128)(2,1)}, bf16[512,1536]{1,0:T(8,128)(2,1)}, u32[]{:S(2)}, u32[]{:S(2)}) collective-permute-start(bf16[512,1536]{1,0:T(8,128)(2,1)} %pad_maximum_fusion.7), channel_id=1, source_target_pairs={{0,2},{1,3},{2,0},{3,1},{4,6},{5,7},{6,4},{7,5},{8,10},{9,11},{10,... | collective-permute-start | bytes 4718600 | tf_op jit(solution)/shard_map/ppermute | solution.py:466
  518.1 332.9 %reduce-scatter.12.cloned.1.call-start = ((), (), s32[]{:S(2)}) async-start(), calls=%async_computation.12 | async-start | bytes 2211840 | tf_op jit(solution)/shard_map/reduce_scatter | solution.py:756
  622.9 32.0 %collective-permute-start.32 = (bf16[512,1536]{1,0:T(8,128)(2,1)S(1)}, bf16[512,1536]{1,0:T(8,128)(2,1)S(1)}, u32[]{:S(2)}, u32[]{:S(2)}) collective-permute-start(bf16[512,1536]{1,0:T(8,128)(2,1)S(1)} %pad_maximum_fusion.9), channel_id=1, source_target_pairs={{0,1},{1,0},{2,3},{3,2},{4,5},{5,4},{6,7},{7,6},{8,9},{9,8},{10,11... | collective-permute-start | bytes 4718600 | tf_op jit(solution)/shard_map/ppermute | solution.py:466
  624.2 33.4 %collective-permute-start.33 = (bf16[512,1536]{1,0:T(8,128)(2,1)S(1)}, bf16[512,1536]{1,0:T(8,128)(2,1)S(1)}, u32[]{:S(2)}, u32[]{:S(2)}) collective-permute-start(bf16[512,1536]{1,0:T(8,128)(2,1)S(1)} %pad_maximum_fusion.10), channel_id=1, source_target_pairs={{0,2},{1,3},{2,0},{3,1},{4,6},{5,7},{6,4},{7,5},{8,10},{9,11},{10,... | collective-permute-start | bytes 4718600 | tf_op jit(solution)/shard_map/ppermute | solution.py:466
  709.2 65.7 %collective-permute-start.45 = (bf16[384,1536]{1,0:T(8,128)(2,1)}, bf16[384,1536]{1,0:T(8,128)(2,1)}, u32[]{:S(2)}, u32[]{:S(2)}) collective-permute-start(bf16[384,1536]{1,0:T(8,128)(2,1)} %pad_maximum_fusion.14), channel_id=1, source_target_pairs={{0,1},{1,0},{2,3},{3,2},{4,5},{5,4},{6,7},{7,6},{8,9},{9,8},{10,11... | collective-permute-start | bytes 3538952 | tf_op jit(solution)/shard_map/ppermute | solution.py:466
  710.7 65.8 %collective-permute-start.46 = (bf16[384,1536]{1,0:T(8,128)(2,1)}, bf16[384,1536]{1,0:T(8,128)(2,1)}, u32[]{:S(2)}, u32[]{:S(2)}) collective-permute-start(bf16[384,1536]{1,0:T(8,128)(2,1)} %pad_maximum_fusion.15), channel_id=1, source_target_pairs={{0,2},{1,3},{2,0},{3,1},{4,6},{5,7},{6,4},{7,5},{8,10},{9,11},{10,... | collective-permute-start | bytes 3538952 | tf_op jit(solution)/shard_map/ppermute | solution.py:466
  712.2 172.3 %reduce-scatter.16.cloned.1.call-start = ((), (), s32[]{:S(2)}) async-start(), calls=%async_computation.14 | async-start | bytes 1327104
  734.0 47.2 %collective-permute-start.36 = (bf16[512,1536]{1,0:T(8,128)(2,1)S(1)}, bf16[512,1536]{1,0:T(8,128)(2,1)}, u32[]{:S(2)}, u32[]{:S(2)}) collective-permute-start(bf16[512,1536]{1,0:T(8,128)(2,1)S(1)} %pad_maximum_fusion.11), channel_id=1, source_target_pairs={{0,1},{1,0},{2,3},{3,2},{4,5},{5,4},{6,7},{7,6},{8,9},{9,8},{10,11... | collective-permute-start | bytes 4718600 | tf_op jit(solution)/shard_map/ppermute | solution.py:466
  735.9 47.2 %collective-permute-start.37 = (bf16[512,1536]{1,0:T(8,128)(2,1)}, bf16[512,1536]{1,0:T(8,128)(2,1)}, u32[]{:S(2)}, u32[]{:S(2)}) collective-permute-start(bf16[512,1536]{1,0:T(8,128)(2,1)} %pad_maximum_fusion.12), channel_id=1, source_target_pairs={{0,2},{1,3},{2,0},{3,1},{4,6},{5,7},{6,4},{7,5},{8,10},{9,11},{10,... | collective-permute-start | bytes 4718600 | tf_op jit(solution)/shard_map/ppermute | solution.py:466
  (102 other events, 1251.1 us)
Sparse Core Ops, SparseCore 0:
  10.2 34.3 all-gather.5
  46.2 21.7 all-gather.7
  70.2 129.2 all-gather.9
  201.5 127.8 all-gather.11
  330.8 88.9 all-gather.13
  421.9 142.4 reduce-scatter.7
  566.8 142.4 reduce-scatter.9
  711.5 101.1 reduce-scatter.13
  815.0 35.9 reduce-scatter.11
  853.3 31.1 reduce-scatter.15

commit v4 on v3

--- a/solution.py
+++ b/solution.py
@@ -19,7 +19,7 @@
 LANES = 128
 PITCH = 13
 UNROLL = 8
-CHUNKS = (6, 6, 4)
+CHUNKS = (4, 6, 6)
 EPSILON = 1e-05
 F32 = jnp.float32
 BF16 = jnp.bfloat16
@@ -484,9 +484,9 @@
     yield [value, one, two, far]
 
 
-def gather_start(value):
+def gather_start(value, axis=0):
     if lax.axis_size("narrow") != 4:
-        return [lax.all_gather(value, "narrow", axis=0, tiled=True)]
+        return [lax.all_gather(value, "narrow", axis=axis, tiled=True)]
     rounds = gather_blocks(value)
     next(rounds)
     return rounds
@@ -624,18 +624,23 @@
     inputs = gather_rows(block_input)
     gains = gather_columns(jnp.stack([first_gain, second_gain])).astype(F32)
     gain_one, gain_two = gains[0], gains[1]
-    input_router = lax.all_gather(
+    packed = lax.all_gather(
         jnp.concatenate(
-            [query_key_value_weight, jnp.pad(router_weight, ((0, 0), (0, LANES - E)))], axis=1
+            [
+                query_key_value_weight,
+                jnp.pad(router_weight, ((0, 0), (0, LANES - E))),
+                output_weight.T,
+            ],
+            axis=1,
         ),
         "wide",
         axis=0,
         tiled=True,
     )
-    input_full = input_router[:, :head_columns]
-    router_padded = input_router[:, head_columns:]
+    input_full = packed[:, :head_columns]
+    router_padded = packed[:, head_columns : head_columns + LANES]
     router_full = router_padded[:, :E]
-    output_part = lax.all_gather(output_weight, "wide", axis=1, tiled=True)
+    output_part = packed[:, head_columns + LANES :]
     lows = [sum(CHUNKS[:index]) for index in range(len(CHUNKS))]
     chunk_weights = []
     for low, size in zip(lows, CHUNKS):
@@ -649,12 +654,12 @@
     projected = jnp.einsum(
         "td,dc->ct", attn_in, input_full, preferred_element_type=F32
     ).astype(BF16)
-    output_rounds = gather_start(after(output_part, projected))
+    output_rounds = gather_start(after(output_part, projected), 1)
     cot_rounds = gather_start(after(cotangent, projected))
     mixed, log_totals = attend_forward(projected, groups, heads)
     mixed_own = to_rows(mixed)
     output_blocks = gather_end(output_rounds, mixed)
-    middle_own = block_input.astype(F32) + product_sum("ct,cd->td", mixed_own, output_blocks)
+    middle_own = block_input.astype(F32) + product_sum("ct,dc->td", mixed_own, output_blocks)
     middle_low = middle_own.astype(BF16)
     cot_blocks = gather_end(cot_rounds, middle_low)
     live = block_ends[E - 1 :]
@@ -705,7 +710,7 @@
     )
     branch_grad = mid_grad.astype(BF16)
     mixed_grad_own = [
-        jnp.einsum("td,cd->ct", branch_grad, block, preferred_element_type=F32).astype(BF16)
+        jnp.einsum("td,dc->ct", branch_grad, block, preferred_element_type=F32).astype(BF16)
         for block in output_blocks
     ]
     mixed_grad = to_heads(mixed_grad_own)
@@ -753,12 +758,16 @@
     input_grad = mid_grad + scale_one_own * (
         gain_one * input_sum - normed_one_own * input_dot / width
     )
-    input_w_grad = lax.psum_scatter(
-        after(grad_input_w, grads[1], input_grad), "wide", scatter_dimension=0, tiled=True
-    )
-    output_w_grad = lax.psum_scatter(
-        after(grad_output_w, grads[1]), "wide", scatter_dimension=1, tiled=True
-    )
+    packed_grad = lax.psum_scatter(
+        after(
+            jnp.concatenate([grad_input_w, grad_output_w.T], axis=1), grads[1], input_grad
+        ),
+        "wide",
+        scatter_dimension=0,
+        tiled=True,
+    ).astype(F32)
+    input_w_grad = packed_grad[:, :head_columns]
+    output_w_grad = packed_grad[:, head_columns:].T
     grads = after(grads, block_output, small_sum, grad_output_w, input_grad)
     gate_grad, up_grad, down_grad = (
         jnp.concatenate([grad[index] for grad in grads], axis=0).astype(F32) for index in range(3)
@@ -767,8 +776,8 @@
         block_output,
         input_grad,
         gain_own[0],
-        input_w_grad.astype(F32),
-        output_w_grad.astype(F32),
+        input_w_grad,
+        output_w_grad,
         gain_own[1],
         router_grad,
         gate_grad,

time: 903 us -> 861 us (0.953)
  other arithmetic: 101 us -> 87.1 us
  matrix products: 50.9 us -> 39.4 us
    ppermute x44, waiting for transfers between devices: 189 us -> 244 us  [swap(): lax.ppermute(value, 'narrow', [(index, index ^ bit) for index in range(co...]
    reduce_scatter x1 -> x0, waiting for transfers between devices: 25.2 us -> none  [local(): lax.psum_scatter(after(grad_input_w, grads[1], input_grad), 'wide', scatt...]
    ppermute x5, waiting for transfers between devices: 48.4 us -> 31.7 us  [sum_all(): lax.ppermute(value, axis, [(index, index ^ bit) for index in range(count)])]
    reduce_scatter x3, waiting for transfers between devices: 13.1 us -> 0.01 us  [local(): lax.psum_scatter(grad, 'wide', scatter_dimension=2, tiled=True)]
    unnamed x11 -> x9, waiting for transfers between devices: 32.6 us -> 27.9 us
    unnamed x153 -> x158, local copies, waits for them, and re-layouts: 23.8 us -> 24.7 us
  transfers between devices with their start and end apart: 59 -> 57, of which waited for: 26 -> 26; matrix products, arithmetic and copies ran while one was open for 22% -> 20% of each run, Pallas kernels for 32% -> 33%
where the time goes in v4:
time: 861 us; the launch traced here: 853 us
  waiting for transfers between devices  304 us (35%)
  Pallas kernels  285 us (33%)
  other arithmetic  87.1 us (10%)
  local copies, waits for them, and re-layouts  62.1 us (7%)
  starting transfers between devices  57.3 us (7%)
  matrix products  39.4 us (5%)
  between operations  18.3 us (2%)
    ppermute x44, waiting for transfers between devices, swap(): lax.ppermute(value, 'narrow', [(index, index ^ bit) for index in range(co...  244 us
    pallas_call x3, Pallas kernels, run_experts(): pl.pallas_call(expert_kernel, grid_spec=pltpu.PrefetchScalarGridSpec(num_...  149 us
    ppermute x44, starting transfers between devices, swap(): lax.ppermute(value, 'narrow', [(index, index ^ bit) for index in range(co...  54 us
    pallas_call x2, Pallas kernels, dispatch(): pl.pallas_call(functools.partial(dispatch_kernel, len(sources), gated), g...  49.1 us
    pallas_call x1, Pallas kernels, attend_backward(): pl.pallas_call(functools.partial(backward_kernel, heads), grid=(groups, b...  48.5 us
    pallas_call x1, Pallas kernels, attend_forward(): pl.pallas_call(functools.partial(forward_kernel, heads), grid=(groups, bl...  38.5 us
    ppermute x5, waiting for transfers between devices, sum_all(): lax.ppermute(value, axis, [(index, index ^ bit) for index in range(count)])  31.7 us
    unnamed x9, waiting for transfers between devices  27.9 us
  transfers between devices with their start and end apart: 57, of which 26 were waited for; matrix products, arithmetic and copies ran while one was open for 20% of the time, Pallas kernels for 33%

profile of v4, /device:TPU:0, one launch (start us, length us, event | category | flops | bytes accessed | tf_op | source)
XLA Modules:
  0.0 852.7 jit_solution(2127289734100002005)
XLA Ops:
  32.5 4.6 reduce-window.11
  37.9 19.0 %collective-permute-done.1 = bf16[512,1536]{1,0:T(8,128)(2,1)} collective-permute-done((bf16[512,1536]{1,0:T(8,128)(2,1)S(1)}, bf16[512,1536]{1,0:T(8,128)(2,1)}, u32[]{:S(2)}, u32[]{:S(2)}) %collective-permute-start.1) | collective-permute-done | bytes 1572896 | tf_op jit(solution)/shard_map/ppermute | solution.py:466
  64.4 13.7 %collective-permute-done.2 = bf16[256,1536]{1,0:T(8,128)(2,1)} collective-permute-done((bf16[256,1536]{1,0:T(8,128)(2,1)}, bf16[256,1536]{1,0:T(8,128)(2,1)}, u32[]{:S(2)}, u32[]{:S(2)}) %collective-permute-start.2) | collective-permute-done | bytes 786464 | tf_op jit(solution)/shard_map/ppermute | solution.py:466
  87.0 9.5 %convolution_convert_fusion.2.qkv_ref = bf16[640,2048]{1,0:T(8,128)(2,1)S(1)} fusion(f32[1536]{0:T(1024)S(1)} %get-tuple-element.161, f32[2048]{0:T(1024)S(1)} %add_rsqrt_fusion, bf16[1536,1152]{1,0:T(8,128)(2,1)} %all-gather.5.cloned.1.call-done, bf16[512,1536]{1,0:T(8,128)(2,1)} %copy-done.27, bf16[512,1536]{1,0:T(8,128)(2,1)} %copy-done.29, ...), kind=kOutput, calls=%fused_computation.22 | convolution fusion | flops 4062445568 | bytes 10893312 | tf_op jit(solution)/shard_map/td,dc->ct/dot_general | solution.py:654
  100.6 38.5 %shard_map.186 = (bf16[384,2048]{1,0:T(8,128)(2,1)S(1)}, f32[2,8,1,768]{3,2,1,0:T(1,128)S(1)}) custom-call(bf16[640,2048]{1,0:T(8,128)(2,1)S(1)} %convolution_convert_fusion.2.qkv_ref), custom_call_target="tpu_custom_call" | custom-call | flops 45097156608 | bytes 5242880 | tf_op jit(solution)/shard_map/pallas_call | solution.py:77
  145.3 23.8 %collective-permute-done.7 = bf16[384,512]{1,0:T(8,128)(2,1)S(1)} collective-permute-done((bf16[384,512]{1,0:T(8,128)(2,1)S(1)}, bf16[384,512]{1,0:T(8,128)(2,1)S(1)}, u32[]{:S(2)}, u32[]{:S(2)}) %collective-permute-start.7) | collective-permute-done | bytes 393248 | tf_op jit(solution)/shard_map/ppermute | solution.py:466
  174.1 7.6 collective-permute-done.12
  194.6 15.5 %scatter_custom_fusion.token_ref = s32[8192]{0:T(1024)S(1)} fusion(s32[4096]{0:T(1024)S(1)} %bitcast.129, s32[4096]{0:T(1024)S(1)} %add_select_fusion, s32[]{:T(128)} %constant.86.clone.1), kind=kCustom, calls=%fused_computation.193 | custom fusion | bytes 32772 | tf_op jit(solution)/shard_map/scatter | solution.py:170
  213.1 28.4 %collective-permute-done.20 = bf16[256,1536]{1,0:T(8,128)(2,1)} collective-permute-done((bf16[256,1536]{1,0:T(8,128)(2,1)}, bf16[256,1536]{1,0:T(8,128)(2,1)}, u32[]{:S(2)}, u32[]{:S(2)}) %collective-permute-start.20) | collective-permute-done | bytes 786464 | tf_op jit(solution)/shard_map/ppermute | solution.py:466
  249.1 21.4 %shard_map.188.cot_ref = bf16[8192,1536]{1,0:T(8,128)(2,1)} custom-call(s32[8192]{0:T(1024)S(1)} %scatter_custom_fusion.token_ref, s32[32]{0:T(128)S(1)} %broadcast_minimum_fusion.expert_ref, s32[1]{0:T(128)} %bitcast.6.live_ref, s32[1]{0:T(128)} %bitcast.7.me_ref, bf16[512,1536]{1,0:T(8,128)(2,1)S(1)} %copy-done.3, bf16[512,1536]{1,0:T(8,128)(2,1)S(1)} %copy-done.10, ...), custom_call_target="tpu_custom_call" | custom-call | flops 41999998976 | bytes 18874368 | tf_op jit(solution)/shard_map/pallas_call | solution.py:270
  271.8 27.7 %shard_map.187 = (bf16[8192,1536]{1,0:T(8,128)(2,1)}, f32[8192,1]{1,0:T(8,128)}) custom-call(s32[8192]{0:T(1024)S(1)} %scatter_custom_fusion.token_ref, s32[32]{0:T(128)S(1)} %broadcast_minimum_fusion.expert_ref, s32[1]{0:T(128)} %bitcast.6.live_ref, s32[1]{0:T(128)} %bitcast.7.me_ref, bf16[512,1536]{1,0:T(8,128)(2,1)S(1)} %get-tuple-element.75.refs_0_, ...), custom_call_target="tpu_custom_call" | custom-call | flops 41999998976 | bytes 18874368 | tf_op jit(solution)/shard_map/pallas_call | solution.py:270
  299.5 40.4 %shard_map.189 = (bf16[2048,1536]{1,0:T(8,128)(2,1)}, bf16[2048,1536]{1,0:T(8,128)(2,1)}, f32[2048,128]{1,0:T(8,128)}, bf16[3,4,1536,256]{3,2,1,0:T(8,128)(2,1)}) custom-call(s32[3]{0:T(128)} %pad_add_fusion.span_ref, s32[32]{0:T(128)} %copy-done.12, s32[8192]{0:T(1024)} %copy-done.11, bf16[8192,1536]{1,0:T(8,128)(2,1)} %get-tuple-element.66.row_ref, ...), custom_call_target="tpu_custom_call" | custom-call | flops 65229815808 | bytes 28311552 | tf_op jit(solution)/shard_map/pallas_call | solution.py:424
  342.4 61.9 %shard_map.190 = (bf16[2048,1536]{1,0:T(8,128)(2,1)}, bf16[2048,1536]{1,0:T(8,128)(2,1)}, f32[2048,128]{1,0:T(8,128)}, bf16[3,6,1536,256]{3,2,1,0:T(8,128)(2,1)}) custom-call(s32[3]{0:T(128)} %pad_add_fusion.1.span_ref, s32[32]{0:T(128)} %copy-done.12, s32[8192]{0:T(1024)} %copy-done.11, bf16[8192,1536]{1,0:T(8,128)(2,1)} %get-tuple-element.66.row_ref, ...), custom_call_target="tpu_custom_call" | custom-call | flops 97844723712 | bytes 42467328 | tf_op jit(solution)/shard_map/pallas_call | solution.py:424
  406.9 46.4 %shard_map.191 = (bf16[2048,1536]{1,0:T(8,128)(2,1)}, bf16[2048,1536]{1,0:T(8,128)(2,1)}, f32[2048,128]{1,0:T(8,128)}, bf16[3,6,1536,256]{3,2,1,0:T(8,128)(2,1)}) custom-call(s32[3]{0:T(128)} %pad_add_fusion.2.span_ref, s32[32]{0:T(128)} %copy-done.12, s32[8192]{0:T(1024)} %copy-done.11, bf16[8192,1536]{1,0:T(8,128)(2,1)} %get-tuple-element.66.row_ref, ...), custom_call_target="tpu_custom_call" | custom-call | flops 97844723712 | bytes 42467328 | tf_op jit(solution)/shard_map/pallas_call | solution.py:424
  453.6 5.1 add_convert_fusion.5
  467.6 29.4 %collective-permute-done.22 = bf16[512,1536]{1,0:T(8,128)(2,1)} collective-permute-done((bf16[512,1536]{1,0:T(8,128)(2,1)}, bf16[512,1536]{1,0:T(8,128)(2,1)}, u32[]{:S(2)}, u32[]{:S(2)}) %collective-permute-start.22) | collective-permute-done | bytes 1572896 | tf_op jit(solution)/shard_map/ppermute | solution.py:466
  510.5 13.4 %collective-permute-done.26 = f32[2,512]{1,0:T(2,128)S(1)} collective-permute-done((f32[2,512]{1,0:T(2,128)S(1)}, f32[2,512]{1,0:T(2,128)S(1)}, u32[]{:S(2)}, u32[]{:S(2)}) %collective-permute-start.26) | collective-permute-done | bytes 4128 | tf_op jit(solution)/shard_map/ppermute | solution.py:466
  539.4 5.3 collective-permute-done.29
  544.7 9.0 %collective-permute-done.30 = bf16[384,512]{1,0:T(8,128)(2,1)S(1)} collective-permute-done((bf16[384,512]{1,0:T(8,128)(2,1)S(1)}, bf16[384,512]{1,0:T(8,128)(2,1)S(1)}, u32[]{:S(2)}, u32[]{:S(2)}) %collective-permute-start.30) | collective-permute-done | bytes 393248 | tf_op jit(solution)/shard_map/ppermute | solution.py:466
  555.9 48.5 %shard_map.192 = bf16[640,2048]{1,0:T(8,128)(2,1)S(1)} custom-call(bf16[640,2048]{1,0:T(8,128)(2,1)S(1)} %copy-done.16, bf16[384,2048]{1,0:T(8,128)(2,1)S(1)} %copy-done.6, f32[2,8,1,768]{3,2,1,0:T(1,128)S(1)} %get-tuple-element.74.total_ref, bf16[384,2048]{1,0:T(8,128)(2,1)S(1)} %pad_maximum_fusion.9.grad_ref), custom_call_target="tpu_custom_call" | custom-call | flops 56371445760 | bytes 10485760 | tf_op jit(solution)/shard_map/pallas_call | solution.py:139
  605.9 7.5 convolution_convert_fusion
  617.0 28.6 %collective-permute-done.32 = bf16[512,1536]{1,0:T(8,128)(2,1)S(1)} collective-permute-done((bf16[512,1536]{1,0:T(8,128)(2,1)S(1)}, bf16[512,1536]{1,0:T(8,128)(2,1)S(1)}, u32[]{:S(2)}, u32[]{:S(2)}) %collective-permute-start.32) | collective-permute-done | bytes 1572896 | tf_op jit(solution)/shard_map/ppermute | solution.py:466
  653.0 5.7 convolution_convert_fusion.1
  658.8 7.6 collective-permute-done.34
  681.4 17.1 %collective-permute-done.45 = bf16[384,1536]{1,0:T(8,128)(2,1)S(1)} collective-permute-done((bf16[384,1536]{1,0:T(8,128)(2,1)S(1)}, bf16[384,1536]{1,0:T(8,128)(2,1)S(1)}, u32[]{:S(2)}, u32[]{:S(2)}) %collective-permute-start.45) | collective-permute-done | bytes 1179680 | tf_op jit(solution)/shard_map/ppermute | solution.py:466
  708.0 5.0 collective-permute-done.47
  718.8 4.7 copy.54
  728.5 26.1 %collective-permute-done.36 = bf16[512,1536]{1,0:T(8,128)(2,1)S(1)} collective-permute-done((bf16[512,1536]{1,0:T(8,128)(2,1)S(1)}, bf16[512,1536]{1,0:T(8,128)(2,1)S(1)}, u32[]{:S(2)}, u32[]{:S(2)}) %collective-permute-start.36) | collective-permute-done | bytes 1572896 | tf_op jit(solution)/shard_map/ppermute | solution.py:466
  756.1 5.7 fusion.29
  763.7 11.8 %collective-permute-done.41 = f32[18,1536]{1,0:T(8,128)S(1)} collective-permute-done((f32[18,1536]{1,0:T(8,128)S(1)}, f32[18,1536]{1,0:T(8,128)S(1)}, u32[]{:S(2)}, u32[]{:S(2)}) %collective-permute-start.41) | collective-permute-done | bytes 110624 | tf_op jit(solution)/shard_map/ppermute | solution.py:590
  775.7 11.9 %collective-permute-done.42 = f32[18,1536]{1,0:T(8,128)S(1)} collective-permute-done((f32[18,1536]{1,0:T(8,128)S(1)}, f32[18,1536]{1,0:T(8,128)S(1)}, u32[]{:S(2)}, u32[]{:S(2)}) %collective-permute-start.42) | collective-permute-done | bytes 110624 | tf_op jit(solution)/shard_map/ppermute | solution.py:590
  814.7 27.7 %reduce-scatter.13.cloned.1.call-done = bf16[192,1024]{1,0:T(8,128)(2,1)} async-done(((bf16[1536,1024]{1,0:T(8,128)(2,1)}), bf16[192,1024]{1,0:T(8,128)(2,1)}) %reduce-scatter.13.cloned.1.call-update) | async-done | bytes 393232
  (408 shorter events, 205.9 us)
Async XLA Ops:
  7.2 78.0 %all-gather.5.cloned.1.call-start = ((), (), s32[]{:S(2)}) async-start(), calls=%async_computation.4 | async-start | bytes 3981312 | tf_op jit(solution)/shard_map/all_gather | solution.py:627
  9.9 289.6 %all-gather.7.cloned.1.call-start = ((), (), s32[]{:S(2)}) async-start(), calls=%async_computation.5 | async-start | bytes 10616832 | tf_op jit(solution)/shard_map/all_gather | solution.py:648
  13.4 329.0 %all-gather.9.cloned.1.call-start = ((), (), s32[]{:S(2)}) async-start(), calls=%async_computation.6 | async-start | bytes 15925248 | tf_op jit(solution)/shard_map/all_gather | solution.py:648
  18.0 388.8 %all-gather.11.cloned.1.call-start = ((), (), s32[]{:S(2)}) async-start(), calls=%async_computation.7 | async-start | bytes 15925248 | tf_op jit(solution)/shard_map/all_gather | solution.py:648
  19.4 37.5 %collective-permute-start.1 = (bf16[512,1536]{1,0:T(8,128)(2,1)S(1)}, bf16[512,1536]{1,0:T(8,128)(2,1)}, u32[]{:S(2)}, u32[]{:S(2)}) collective-permute-start(bf16[512,1536]{1,0:T(8,128)(2,1)S(1)} %copy-done.17), channel_id=1, source_target_pairs={{0,2},{1,3},{2,0},{3,1},{4,6},{5,7},{6,4},{7,5},{8,10},{9,11},{10,... | collective-permute-start | bytes 4718600 | tf_op jit(solution)/shard_map/ppermute | solution.py:466
  22.5 38.4 %collective-permute-start = (bf16[512,1536]{1,0:T(8,128)(2,1)S(1)}, bf16[512,1536]{1,0:T(8,128)(2,1)}, u32[]{:S(2)}, u32[]{:S(2)}) collective-permute-start(bf16[512,1536]{1,0:T(8,128)(2,1)S(1)} %copy-done.17), channel_id=1, source_target_pairs={{0,1},{1,0},{2,3},{3,2},{4,5},{5,4},{6,7},{7,6},{8,9},{9,8},{10,11... | collective-permute-start | bytes 4718600 | tf_op jit(solution)/shard_map/ppermute | solution.py:466
  24.0 39.7 %collective-permute-start.5 = (bf16[2,384]{1,0:T(2,128)(2,1)S(1)}, bf16[2,384]{1,0:T(2,128)(2,1)S(1)}, u32[]{:S(2)}, u32[]{:S(2)}) collective-permute-start(bf16[2,384]{1,0:T(2,128)(2,1)S(1)} %pad_maximum_fusion.19), channel_id=1, source_target_pairs={{0,2},{1,3},{2,0},{3,1},{4,6},{5,7},{6,4},{7,5},{8,10},{9,11},{10,... | collective-permute-start | bytes 4616 | tf_op jit(solution)/shard_map/ppermute | solution.py:466
  24.6 39.1 %collective-permute-start.6 = (bf16[2,384]{1,0:T(2,128)(2,1)S(1)}, bf16[2,384]{1,0:T(2,128)(2,1)S(1)}, u32[]{:S(2)}, u32[]{:S(2)}) collective-permute-start(bf16[2,384]{1,0:T(2,128)(2,1)S(1)} %pad_maximum_fusion.19), channel_id=1, source_target_pairs={{0,3},{1,2},{2,1},{3,0},{4,7},{5,6},{6,5},{7,4},{8,11},{9,10},{10,... | collective-permute-start | bytes 4616 | tf_op jit(solution)/shard_map/ppermute | solution.py:466
  26.1 37.6 %collective-permute-start.4 = (bf16[2,384]{1,0:T(2,128)(2,1)S(1)}, bf16[2,384]{1,0:T(2,128)(2,1)S(1)}, u32[]{:S(2)}, u32[]{:S(2)}) collective-permute-start(bf16[2,384]{1,0:T(2,128)(2,1)S(1)} %pad_maximum_fusion.19), channel_id=1, source_target_pairs={{0,1},{1,0},{2,3},{3,2},{4,5},{5,4},{6,7},{7,6},{8,9},{9,8},{10,11... | collective-permute-start | bytes 4616 | tf_op jit(solution)/shard_map/ppermute | solution.py:466
  30.1 575.8 %reduce-scatter.7.cloned.1.call-start = ((), (), s32[]{:S(2)}) async-start(), calls=%async_computation.8 | async-start | bytes 10616832 | tf_op jit(solution)/shard_map/reduce_scatter | solution.py:683
  96.5 44.5 %collective-permute-start.10 = (bf16[1536,384]{1,0:T(8,128)(2,1)S(1)}, bf16[1536,384]{1,0:T(8,128)(2,1)S(1)}, u32[]{:S(2)}, u32[]{:S(2)}) collective-permute-start(bf16[1536,384]{1,0:T(8,128)(2,1)S(1)} %slice.292), channel_id=1, source_target_pairs={{0,2},{1,3},{2,0},{3,1},{4,6},{5,7},{6,4},{7,5},{8,10},{9,11},{10,... | collective-permute-start | bytes 3538952 | tf_op jit(solution)/shard_map/ppermute | solution.py:466
  98.1 43.0 %collective-permute-start.8 = (bf16[1536,384]{1,0:T(8,128)(2,1)S(1)}, bf16[1536,384]{1,0:T(8,128)(2,1)S(1)}, u32[]{:S(2)}, u32[]{:S(2)}) collective-permute-start(bf16[1536,384]{1,0:T(8,128)(2,1)S(1)} %slice.292), channel_id=1, source_target_pairs={{0,1},{1,0},{2,3},{3,2},{4,5},{5,4},{6,7},{7,6},{8,9},{9,8},{10,11... | collective-permute-start | bytes 3538952 | tf_op jit(solution)/shard_map/ppermute | solution.py:466
  98.5 72.1 %collective-permute-start.19 = (bf16[512,1536]{1,0:T(8,128)(2,1)S(1)}, bf16[512,1536]{1,0:T(8,128)(2,1)S(1)}, u32[]{:S(2)}, u32[]{:S(2)}) collective-permute-start(bf16[512,1536]{1,0:T(8,128)(2,1)S(1)} %copy-done.2), channel_id=1, source_target_pairs={{0,2},{1,3},{2,0},{3,1},{4,6},{5,7},{6,4},{7,5},{8,10},{9,11},{10,... | collective-permute-start | bytes 4718600 | tf_op jit(solution)/shard_map/ppermute | solution.py:466
  99.1 74.0 %collective-permute-start.18 = (bf16[512,1536]{1,0:T(8,128)(2,1)S(1)}, bf16[512,1536]{1,0:T(8,128)(2,1)S(1)}, u32[]{:S(2)}, u32[]{:S(2)}) collective-permute-start(bf16[512,1536]{1,0:T(8,128)(2,1)S(1)} %copy-done.2), channel_id=1, source_target_pairs={{0,1},{1,0},{2,3},{3,2},{4,5},{5,4},{6,7},{7,6},{8,9},{9,8},{10,11... | collective-permute-start | bytes 4718600 | tf_op jit(solution)/shard_map/ppermute | solution.py:466
  141.2 40.6 %collective-permute-start.12 = (bf16[768,384]{1,0:T(8,128)(2,1)S(1)}, bf16[768,384]{1,0:T(8,128)(2,1)S(1)}, u32[]{:S(2)}, u32[]{:S(2)}) collective-permute-start(bf16[768,384]{1,0:T(8,128)(2,1)S(1)} %slice.293), channel_id=1, source_target_pairs={{0,1},{1,0},{2,3},{3,2},{4,5},{5,4},{6,7},{7,6},{8,9},{9,8},{10,11... | collective-permute-start | bytes 1769480 | tf_op jit(solution)/shard_map/ppermute | solution.py:466
  142.7 39.1 %collective-permute-start.13 = (bf16[768,384]{1,0:T(8,128)(2,1)S(1)}, bf16[768,384]{1,0:T(8,128)(2,1)S(1)}, u32[]{:S(2)}, u32[]{:S(2)}) collective-permute-start(bf16[768,384]{1,0:T(8,128)(2,1)S(1)} %slice.294), channel_id=1, source_target_pairs={{0,2},{1,3},{2,0},{3,1},{4,6},{5,7},{6,4},{7,5},{8,10},{9,11},{10,... | collective-permute-start | bytes 1769480 | tf_op jit(solution)/shard_map/ppermute | solution.py:466
  190.5 53.7 %collective-permute-start.15 = (bf16[512,1536]{1,0:T(8,128)(2,1)S(1)}, bf16[512,1536]{1,0:T(8,128)(2,1)}, u32[]{:S(2)}, u32[]{:S(2)}) collective-permute-start(bf16[512,1536]{1,0:T(8,128)(2,1)S(1)} %get-tuple-element.75.refs_0_), channel_id=1, source_target_pairs={{0,2},{1,3},{2,0},{3,1},{4,6},{5,7},{6,4},{7,5},{8,10},{9,11},{10,... | collective-permute-start | bytes 4718600 | tf_op jit(solution)/shard_map/ppermute | solution.py:466
  192.0 54.8 %collective-permute-start.14 = (bf16[512,1536]{1,0:T(8,128)(2,1)S(1)}, bf16[512,1536]{1,0:T(8,128)(2,1)}, u32[]{:S(2)}, u32[]{:S(2)}) collective-permute-start(bf16[512,1536]{1,0:T(8,128)(2,1)S(1)} %get-tuple-element.75.refs_0_), channel_id=1, source_target_pairs={{0,1},{1,0},{2,3},{3,2},{4,5},{5,4},{6,7},{7,6},{8,9},{9,8},{10,11... | collective-permute-start | bytes 4718600 | tf_op jit(solution)/shard_map/ppermute | solution.py:466
  192.8 48.6 %collective-permute-start.20 = (bf16[256,1536]{1,0:T(8,128)(2,1)}, bf16[256,1536]{1,0:T(8,128)(2,1)}, u32[]{:S(2)}, u32[]{:S(2)}) collective-permute-start(bf16[256,1536]{1,0:T(8,128)(2,1)} %slice.303), channel_id=1, source_target_pairs={{0,1},{1,0},{2,3},{3,2},{4,5},{5,4},{6,7},{7,6},{8,9},{9,8},{10,11... | collective-permute-start | bytes 2359304 | tf_op jit(solution)/shard_map/ppermute | solution.py:466
  194.0 47.4 %collective-permute-start.21 = (bf16[256,1536]{1,0:T(8,128)(2,1)}, bf16[256,1536]{1,0:T(8,128)(2,1)}, u32[]{:S(2)}, u32[]{:S(2)}) collective-permute-start(bf16[256,1536]{1,0:T(8,128)(2,1)} %slice.304), channel_id=1, source_target_pairs={{0,2},{1,3},{2,0},{3,1},{4,6},{5,7},{6,4},{7,5},{8,10},{9,11},{10,... | collective-permute-start | bytes 2359304 | tf_op jit(solution)/shard_map/ppermute | solution.py:466
  339.9 378.9 %reduce-scatter.9.cloned.1.call-start = ((), (), s32[]{:S(2)}) async-start(), calls=%async_computation.9 | async-start | bytes 15925248 | tf_op jit(solution)/shard_map/reduce_scatter | solution.py:683
  404.3 401.4 %reduce-scatter.11.cloned.1.call-start = ((), (), s32[]{:S(2)}) async-start(), calls=%async_computation.10 | async-start | bytes 15925248 | tf_op jit(solution)/shard_map/reduce_scatter | solution.py:683
  453.3 389.1 %reduce-scatter.13.cloned.1.call-start = ((), (), s32[]{:S(2)}) async-start(), calls=%async_computation.11 | async-start | bytes 3538944
  461.1 35.9 %collective-permute-start.22 = (bf16[512,1536]{1,0:T(8,128)(2,1)}, bf16[512,1536]{1,0:T(8,128)(2,1)}, u32[]{:S(2)}, u32[]{:S(2)}) collective-permute-start(bf16[512,1536]{1,0:T(8,128)(2,1)} %pad_maximum_fusion.7), channel_id=1, source_target_pairs={{0,1},{1,0},{2,3},{3,2},{4,5},{5,4},{6,7},{7,6},{8,9},{9,8},{10,11... | collective-permute-start | bytes 4718600 | tf_op jit(solution)/shard_map/ppermute | solution.py:466
  461.6 37.2 %collective-permute-start.23 = (bf16[512,1536]{1,0:T(8,128)(2,1)}, bf16[512,1536]{1,0:T(8,128)(2,1)}, u32[]{:S(2)}, u32[]{:S(2)}) collective-permute-start(bf16[512,1536]{1,0:T(8,128)(2,1)} %pad_maximum_fusion.8), channel_id=1, source_target_pairs={{0,2},{1,3},{2,0},{3,1},{4,6},{5,7},{6,4},{7,5},{8,10},{9,11},{10,... | collective-permute-start | bytes 4718600 | tf_op jit(solution)/shard_map/ppermute | solution.py:466
  613.9 31.7 %collective-permute-start.32 = (bf16[512,1536]{1,0:T(8,128)(2,1)S(1)}, bf16[512,1536]{1,0:T(8,128)(2,1)S(1)}, u32[]{:S(2)}, u32[]{:S(2)}) collective-permute-start(bf16[512,1536]{1,0:T(8,128)(2,1)S(1)} %pad_maximum_fusion.10), channel_id=1, source_target_pairs={{0,1},{1,0},{2,3},{3,2},{4,5},{5,4},{6,7},{7,6},{8,9},{9,8},{10,11... | collective-permute-start | bytes 4718600 | tf_op jit(solution)/shard_map/ppermute | solution.py:466
  615.1 32.4 %collective-permute-start.33 = (bf16[512,1536]{1,0:T(8,128)(2,1)S(1)}, bf16[512,1536]{1,0:T(8,128)(2,1)S(1)}, u32[]{:S(2)}, u32[]{:S(2)}) collective-permute-start(bf16[512,1536]{1,0:T(8,128)(2,1)S(1)} %pad_maximum_fusion.11), channel_id=1, source_target_pairs={{0,2},{1,3},{2,0},{3,1},{4,6},{5,7},{6,4},{7,5},{8,10},{9,11},{10,... | collective-permute-start | bytes 4718600 | tf_op jit(solution)/shard_map/ppermute | solution.py:466
  725.2 29.4 %collective-permute-start.36 = (bf16[512,1536]{1,0:T(8,128)(2,1)S(1)}, bf16[512,1536]{1,0:T(8,128)(2,1)S(1)}, u32[]{:S(2)}, u32[]{:S(2)}) collective-permute-start(bf16[512,1536]{1,0:T(8,128)(2,1)S(1)} %pad_maximum_fusion.12), channel_id=1, source_target_pairs={{0,1},{1,0},{2,3},{3,2},{4,5},{5,4},{6,7},{7,6},{8,9},{9,8},{10,11... | collective-permute-start | bytes 4718600 | tf_op jit(solution)/shard_map/ppermute | solution.py:466
  726.4 29.3 %collective-permute-start.37 = (bf16[512,1536]{1,0:T(8,128)(2,1)S(1)}, bf16[512,1536]{1,0:T(8,128)(2,1)S(1)}, u32[]{:S(2)}, u32[]{:S(2)}) collective-permute-start(bf16[512,1536]{1,0:T(8,128)(2,1)S(1)} %pad_maximum_fusion.13), channel_id=1, source_target_pairs={{0,2},{1,3},{2,0},{3,1},{4,6},{5,7},{6,4},{7,5},{8,10},{9,11},{10,... | collective-permute-start | bytes 4718600 | tf_op jit(solution)/shard_map/ppermute | solution.py:466
  728.4 35.2 %collective-permute-start.40 = (f32[18,1536]{1,0:T(8,128)S(1)}, f32[18,1536]{1,0:T(8,128)S(1)}, u32[]{:S(2)}, u32[]{:S(2)}) collective-permute-start(f32[18,1536]{1,0:T(8,128)S(1)} %pad_maximum_fusion.18), channel_id=1, source_target_pairs={{0,4},{4,0},{8,12},{12,8},{16,20},{20,16},{24,28},{28,24},{1,5},{5... | collective-permute-start | bytes 331784 | tf_op jit(solution)/shard_map/ppermute | solution.py:590
  761.8 37.7 %collective-permute-start.38 = (bf16[256,1536]{1,0:T(8,128)(2,1)}, bf16[256,1536]{1,0:T(8,128)(2,1)}, u32[]{:S(2)}, u32[]{:S(2)}) collective-permute-start(bf16[256,1536]{1,0:T(8,128)(2,1)} %get-tuple-element.97), channel_id=1, source_target_pairs={{0,2},{1,3},{2,0},{3,1},{4,6},{5,7},{6,4},{7,5},{8,10},{9,11},{10,... | collective-permute-start | bytes 2359304 | tf_op jit(solution)/shard_map/ppermute | solution.py:466
  763.1 36.4 %collective-permute-start.39 = (bf16[256,1536]{1,0:T(8,128)(2,1)}, bf16[256,1536]{1,0:T(8,128)(2,1)}, u32[]{:S(2)}, u32[]{:S(2)}) collective-permute-start(bf16[256,1536]{1,0:T(8,128)(2,1)} %get-tuple-element.98), channel_id=1, source_target_pairs={{0,1},{1,0},{2,3},{3,2},{4,5},{5,4},{6,7},{7,6},{8,9},{9,8},{10,11... | collective-permute-start | bytes 2359304 | tf_op jit(solution)/shard_map/ppermute | solution.py:466
  (102 other events, 1245.0 us)
Sparse Core Ops, SparseCore 0:
  10.2 44.2 all-gather.4
  56.1 89.6 all-gather.6
  147.9 128.0 all-gather.8
  278.0 127.8 all-gather.10
  408.0 97.6 reduce-scatter.6
  507.9 142.4 reduce-scatter.8
  652.6 148.7 reduce-scatter.10
  803.7 38.6 reduce-scatter.12

commit v5 on v4

--- a/solution.py
+++ b/solution.py
@@ -288,6 +288,7 @@
 
 
 def expert_kernel(
+    shards,
     span_ref,
     expert_ref,
     token_ref,
@@ -298,16 +299,9 @@
     out_ref,
     back_ref,
     score_ref,
-    grad_ref,
-    gate_sum,
-    up_sum,
-    down_sum,
-    out_sum,
-    back_sum,
-    moved,
-    staging,
-    sems,
+    *refs,
 ):
+    *grad_refs, gate_sum, up_sum, down_sum, out_sum, back_sum, moved, staging, sems = refs
     step = pl.program_id(0)
     total = span_ref[1]
     block = span_ref[0] + jnp.minimum(step, total - 1)
@@ -375,9 +369,24 @@
 
         @pl.when(closing)
         def _():
+            rows_each = width // shards
             for index, ref in enumerate((gate_sum, up_sum, down_sum)):
-                grad_ref[index, 0] = ref[...].T.astype(BF16)
+                grad = ref[...].T.astype(BF16)
                 ref[...] = jnp.zeros_like(ref)
+                if len(grad_refs) == 1:
+                    grad_refs[0][index, 0] = grad
+                    continue
+                keep_ref, send_ref = grad_refs
+                for core in range(2):
+
+                    @pl.when(span_ref[3] == core)
+                    def _():
+                        for shard in range(shards):
+                            target = keep_ref if shard % 2 == core else send_ref
+                            first = shard // 2 * rows_each
+                            target[index, 0, first : first + rows_each, :] = grad[
+                                shard * rows_each : (shard + 1) * rows_each
+                            ]
 
     @pl.when(step == total - 1)
     def _():
@@ -411,7 +420,7 @@
         copy(len(jobs) - 1).wait()
 
 
-def run_experts(span, slot_token, block_expert, rows, cots, gates, weights, tokens):
+def run_experts(span, slot_token, block_expert, rows, cots, gates, weights, tokens, shards, halved):
     width = rows.shape[1]
     experts, hidden = weights.shape[1], weights.shape[3]
     index = lambda i, s: s[0] + jnp.minimum(i, s[1] - 1)
@@ -419,10 +428,13 @@
     pick = pl.BlockSpec(
         (3, 1, width, hidden), lambda i, s, e, t: (0, e[index(i, s)] - s[2], 0, 0)
     )
+    half = pl.BlockSpec(
+        (3, 1, width // 2, hidden), lambda i, s, e, t: (0, e[index(i, s)] - s[2], 0, 0)
+    )
     anywhere = pl.BlockSpec(memory_space=pl.ANY)
     block_count = experts * 3 // 2
     return pl.pallas_call(
-        expert_kernel,
+        functools.partial(expert_kernel, shards),
         grid_spec=pltpu.PrefetchScalarGridSpec(
             num_scalar_prefetch=3,
             grid=(tokens * TOPK // BLOCK + experts,),
@@ -436,8 +448,8 @@
                 anywhere,
                 anywhere,
                 pl.BlockSpec((tokens, LANES), lambda i, s, e, t: (0, 0)),
-                pick,
-            ],
+            ]
+            + ([half, half] if halved else [pick]),
             scratch_shapes=[pltpu.VMEM((hidden, width), F32)] * 3
             + [pltpu.VMEM(((tokens + 1) * PITCH, LANES), F32)] * 2
             + [
@@ -450,8 +462,12 @@
             jax.ShapeDtypeStruct((tokens, width), BF16),
             jax.ShapeDtypeStruct((tokens, width), BF16),
             jax.ShapeDtypeStruct((tokens, LANES), F32),
-            jax.ShapeDtypeStruct(weights.shape, BF16),
-        ],
+        ]
+        + (
+            [jax.ShapeDtypeStruct((3, experts, width // 2, hidden), BF16)] * 2
+            if halved
+            else [jax.ShapeDtypeStruct(weights.shape, BF16)]
+        ),
         cost_estimate=pl.CostEstimate(
             flops=block_count * 2 * BLOCK * width * hidden * 9 * 6,
             bytes_accessed=weights.size * 4 + block_count * BLOCK * width * 4,
@@ -506,6 +522,14 @@
 
 
 def sum_rows(parts, turned):
+    return sum_rows_end(sum_rows_start(parts, turned))
+
+
+def sum_rows_end(rounds, before=None):
+    return rounds if isinstance(rounds, jax.Array) else rounds[1](rounds[0], before)
+
+
+def sum_rows_start(parts, turned):
     count = lax.axis_size("narrow")
     if count != 4:
         low = sum(part.astype(F32) for part in parts).astype(BF16)
@@ -531,13 +555,17 @@
         low_send, high_send = lax.optimization_barrier(both)
         return swap(low_send, low_bit).astype(F32), swap(high_send, high_bit).astype(F32)
 
-    low, high = send([block(1, 0), block(3, 0)], 1, [block(2, half), block(3, half)], 2)
-    low_far, high_far = send(
-        [block(2, 0) + low[half:]], 2, [block(1, half) + high[half:]], 1
-    )
-    return jnp.concatenate(
-        [block(0, 0) + low[:half] + low_far, block(0, half) + high[:half] + high_far], axis=0
-    )
+    def finish(came, before):
+        low, high = came if before is None else after(came, before)
+        low_far, high_far = send(
+            [block(2, 0) + low[half:]], 2, [block(1, half) + high[half:]], 1
+        )
+        return jnp.concatenate(
+            [block(0, 0) + low[:half] + low_far, block(0, half) + high[:half] + high_far], axis=0
+        )
+
+    first = send([block(1, 0), block(3, 0)], 1, [block(2, half), block(3, half)], 2)
+    return first, finish
 
 
 def to_rows(value):
@@ -669,18 +697,37 @@
         middle_blocks, (gain_two[None], router_padded, routes), slot_token, block_expert, live
     )
 
-    outs, backs, scores, grads = [], [], [], []
+    shards = lax.axis_size("wide")
+    core = lax.rem(lax.axis_index("wide"), 2).astype(jnp.int32)[None]
+    mates = [(index, index ^ 1) for index in range(shards)]
+    parities = [list(range(parity, shards, 2)) for parity in range(2)]
+    outs, backs, scores, kept = [], [], [], []
     for low, size, weights in zip(lows, CHUNKS, chunk_weights):
         first = block_ends[low - 1 : low] if low else jnp.zeros((1,), jnp.int32)
         count = block_ends[low + size - 1 : low + size] - first
-        out, back, score, grad = run_experts(
-            jnp.concatenate([first, count, jnp.full((1,), low, jnp.int32)]),
-            slot_token, block_expert, rows, cot_rows, slot_gates, weights, tokens
+        halved = len(outs) == len(CHUNKS) - 1
+        if outs:
+            first = after(first, scores[-1])
+        out, back, score, *halves = run_experts(
+            jnp.concatenate([first, count, jnp.full((1,), low, jnp.int32), core]),
+            slot_token, block_expert, rows, cot_rows, slot_gates, weights, tokens, shards, halved
         )
         outs.append(out)
         backs.append(back)
         scores.append(score)
-        grads.append(lax.psum_scatter(grad, "wide", scatter_dimension=2, tiled=True))
+        kept.append(halves)
+
+    def sum_cores(keep, send):
+        return (keep.astype(F32) + lax.ppermute(send, "wide", mates).astype(F32)).astype(BF16)
+
+    def sum_chips(value):
+        return lax.psum_scatter(
+            value, "wide", scatter_dimension=2, tiled=True, axis_index_groups=parities
+        )
+
+    grads = [
+        lax.psum_scatter(grad, "wide", scatter_dimension=2, tiled=True) for (grad,) in kept[:-1]
+    ]
 
     def total(values):
         return sum(value.astype(F32) for value in values)
@@ -713,15 +760,19 @@
         jnp.einsum("td,dc->ct", branch_grad, block, preferred_element_type=F32).astype(BF16)
         for block in output_blocks
     ]
-    mixed_grad = to_heads(mixed_grad_own)
+    third = sum_cores(*after(kept[-1], branch_grad))
+    grads.append(sum_chips(third))
+    mixed_grad = after(to_heads(mixed_grad_own), third)
     projected_grad = attend_backward(projected, mixed, log_totals, mixed_grad, groups, heads)
     grad_input_w = jnp.einsum(
         "td,ct->dc", attn_in, projected_grad, preferred_element_type=F32
     ).astype(BF16)
+    block_rounds = sum_rows_start(after(outs, mixed_grad), False)
+    came = block_rounds if isinstance(block_rounds, jax.Array) else block_rounds[0]
     input_part = jnp.einsum(
-        "ct,dc->td", after(projected_grad, grads[0]), input_full, preferred_element_type=F32
+        "ct,dc->td", after(projected_grad, grads[0], came), input_full, preferred_element_type=F32
     ).astype(BF16)
-    input_sum = sum_rows([input_part], False)
+    input_sum = sum_rows_end(sum_rows_start([input_part], False), grads[1])
     grad_output_w = sum_rows(
         [
             jnp.concatenate(
@@ -736,9 +787,7 @@
         ],
         True,
     ).astype(BF16)
-    block_output = (
-        middle_own + sum_rows(after(outs, input_sum), False)
-    ).astype(BF16)
+    block_output = (middle_own + sum_rows_end(block_rounds, input_sum)).astype(BF16)
     grad_router = jnp.einsum(
         "te,td->ed", logit_grad, expert_in_own, preferred_element_type=F32
     )
@@ -747,7 +796,10 @@
     normed_one_own = x_own * scale_one_own
     gain_one_part = jnp.sum(input_sum * normed_one_own, axis=0)
     small_sum = sum_all(
-        jnp.concatenate([grad_router, gain_one_part[None], gain_two_part[None]], axis=0)
+        after(
+            jnp.concatenate([grad_router, gain_one_part[None], gain_two_part[None]], axis=0),
+            grads[2],
+        )
     )
     gain_own = lax.dynamic_slice_in_dim(small_sum[E:], me * gain_part, gain_part, 1)
     router_part = router_weight.shape[0]
@@ -760,7 +812,7 @@
     )
     packed_grad = lax.psum_scatter(
         after(
-            jnp.concatenate([grad_input_w, grad_output_w.T], axis=1), grads[1], input_grad
+            jnp.concatenate([grad_input_w, grad_output_w.T], axis=1), input_grad
         ),
         "wide",
         scatter_dimension=0,

time: 861 us -> 843 us (0.979)
  waiting for transfers between devices: 304 us -> 271 us
  other arithmetic: 87.1 us -> 102 us
    unnamed x9, waiting for transfers between devices: 27.9 us -> 0.13 us
    ppermute x44, waiting for transfers between devices: 244 us -> 232 us  [swap(): lax.ppermute(value, 'narrow', [(index, index ^ bit) for index in range(co...]
    convert_element_type x1 -> x2, other arithmetic: 1.58 us -> 11.9 us  [the longest x1 10.3 us: sum_cores(): (keep.astype(F32) + lax.ppermute(send, 'wide', mates).astype(F32)).astype...]
    reduce_scatter x0 -> x1, waiting for transfers between devices: none -> 9.58 us  [sum_chips(): lax.psum_scatter(value, 'wide', scatter_dimension=2, tiled=True, axis_ind...]
    unnamed x158 -> x152, local copies, waits for them, and re-layouts: 24.7 us -> 23.7 us
  transfers between devices with their start and end apart: 57 -> 58, of which waited for: 26 -> 25; matrix products, arithmetic and copies ran while one was open for 20% -> 22% of each run, Pallas kernels for 33% -> 34%
where the time goes in v5:
time: 843 us; the launch traced here: 834 us
  Pallas kernels  282 us (33%)
  waiting for transfers between devices  271 us (32%)
  other arithmetic  102 us (12%)
  local copies, waits for them, and re-layouts  61.4 us (7%)
  starting transfers between devices  61.3 us (7%)
  matrix products  38.3 us (5%)
  between operations  18.6 us (2%)
    ppermute x44, waiting for transfers between devices, swap(): lax.ppermute(value, 'narrow', [(index, index ^ bit) for index in range(co...  232 us
    pallas_call x3, Pallas kernels, run_experts(): pl.pallas_call(functools.partial(expert_kernel, shards), grid_spec=pltpu....  148 us
    ppermute x44, starting transfers between devices, swap(): lax.ppermute(value, 'narrow', [(index, index ^ bit) for index in range(co...  53.3 us
    pallas_call x1, Pallas kernels, attend_backward(): pl.pallas_call(functools.partial(backward_kernel, heads), grid=(groups, b...  48.1 us
    pallas_call x2, Pallas kernels, dispatch(): pl.pallas_call(functools.partial(dispatch_kernel, len(sources), gated), g...  47.7 us
    pallas_call x1, Pallas kernels, attend_forward(): pl.pallas_call(functools.partial(forward_kernel, heads), grid=(groups, bl...  38.2 us
    ppermute x5, waiting for transfers between devices, sum_all(): lax.ppermute(value, axis, [(index, index ^ bit) for index in range(count)])  25.2 us
    unnamed x152, local copies, waits for them, and re-layouts  23.7 us
  transfers between devices with their start and end apart: 58, of which 25 were waited for; matrix products, arithmetic and copies ran while one was open for 22% of the time, Pallas kernels for 34%

profile of v5, /device:TPU:0, one launch (start us, length us, event | category | flops | bytes accessed | tf_op | source)
XLA Modules:
  0.0 834.4 jit_solution(7936208171619011707)
XLA Ops:
  32.5 4.6 reduce-window.11
  37.9 19.0 %collective-permute-done.1 = bf16[512,1536]{1,0:T(8,128)(2,1)} collective-permute-done((bf16[512,1536]{1,0:T(8,128)(2,1)S(1)}, bf16[512,1536]{1,0:T(8,128)(2,1)}, u32[]{:S(2)}, u32[]{:S(2)}) %collective-permute-start.1) | collective-permute-done | bytes 1572896 | tf_op jit(solution)/shard_map/ppermute | solution.py:482
  64.4 13.7 %collective-permute-done.2 = bf16[256,1536]{1,0:T(8,128)(2,1)} collective-permute-done((bf16[256,1536]{1,0:T(8,128)(2,1)}, bf16[256,1536]{1,0:T(8,128)(2,1)}, u32[]{:S(2)}, u32[]{:S(2)}) %collective-permute-start.2) | collective-permute-done | bytes 786464 | tf_op jit(solution)/shard_map/ppermute | solution.py:482
  87.0 9.5 %convolution_convert_fusion.2.qkv_ref = bf16[640,2048]{1,0:T(8,128)(2,1)S(1)} fusion(f32[1536]{0:T(1024)S(1)} %get-tuple-element.183, f32[2048]{0:T(1024)S(1)} %add_rsqrt_fusion, bf16[1536,1152]{1,0:T(8,128)(2,1)} %all-gather.5.cloned.1.call-done, bf16[512,1536]{1,0:T(8,128)(2,1)} %copy-done.30, bf16[512,1536]{1,0:T(8,128)(2,1)} %copy-done.32, ...), kind=kOutput, calls=%fused_computation.23 | convolution fusion | flops 4062445568 | bytes 10893312 | tf_op jit(solution)/shard_map/td,dc->ct/dot_general | solution.py:682
  100.6 38.2 %shard_map.186 = (bf16[384,2048]{1,0:T(8,128)(2,1)S(1)}, f32[2,8,1,768]{3,2,1,0:T(1,128)S(1)}) custom-call(bf16[640,2048]{1,0:T(8,128)(2,1)S(1)} %convolution_convert_fusion.2.qkv_ref), custom_call_target="tpu_custom_call" | custom-call | flops 45097156608 | bytes 5242880 | tf_op jit(solution)/shard_map/pallas_call | solution.py:77
  145.1 24.1 %collective-permute-done.7 = bf16[384,512]{1,0:T(8,128)(2,1)S(1)} collective-permute-done((bf16[384,512]{1,0:T(8,128)(2,1)S(1)}, bf16[384,512]{1,0:T(8,128)(2,1)S(1)}, u32[]{:S(2)}, u32[]{:S(2)}) %collective-permute-start.7) | collective-permute-done | bytes 393248 | tf_op jit(solution)/shard_map/ppermute | solution.py:482
  174.1 7.7 collective-permute-done.12
  182.0 4.6 collective-permute-done.11
  194.6 15.5 %scatter_custom_fusion.token_ref = s32[8192]{0:T(1024)S(1)} fusion(s32[4096]{0:T(1024)S(1)} %bitcast.124, s32[4096]{0:T(1024)S(1)} %add_select_fusion, s32[]{:T(128)} %constant.88.clone.1), kind=kCustom, calls=%fused_computation.186 | custom fusion | bytes 32772 | tf_op jit(solution)/shard_map/scatter | solution.py:170
  213.1 28.3 %collective-permute-done.20 = bf16[256,1536]{1,0:T(8,128)(2,1)} collective-permute-done((bf16[256,1536]{1,0:T(8,128)(2,1)}, bf16[256,1536]{1,0:T(8,128)(2,1)}, u32[]{:S(2)}, u32[]{:S(2)}) %collective-permute-start.20) | collective-permute-done | bytes 786464 | tf_op jit(solution)/shard_map/ppermute | solution.py:482
  249.1 20.9 %shard_map.188.cot_ref = bf16[8192,1536]{1,0:T(8,128)(2,1)} custom-call(s32[8192]{0:T(1024)S(1)} %scatter_custom_fusion.token_ref, s32[32]{0:T(128)S(1)} %broadcast_minimum_fusion.expert_ref, s32[1]{0:T(128)} %bitcast.7.live_ref, s32[1]{0:T(128)} %bitcast.8.me_ref, bf16[512,1536]{1,0:T(8,128)(2,1)S(1)} %copy-done.3, bf16[512,1536]{1,0:T(8,128)(2,1)S(1)} %copy-done.11, ...), custom_call_target="tpu_custom_call" | custom-call | flops 41999998976 | bytes 18874368 | tf_op jit(solution)/shard_map/pallas_call | solution.py:270
  271.2 26.8 %shard_map.187 = (bf16[8192,1536]{1,0:T(8,128)(2,1)}, f32[8192,1]{1,0:T(8,128)}) custom-call(s32[8192]{0:T(1024)S(1)} %scatter_custom_fusion.token_ref, s32[32]{0:T(128)S(1)} %broadcast_minimum_fusion.expert_ref, s32[1]{0:T(128)} %bitcast.7.live_ref, s32[1]{0:T(128)} %bitcast.8.me_ref, bf16[512,1536]{1,0:T(8,128)(2,1)S(1)} %get-tuple-element.89.refs_0_, ...), custom_call_target="tpu_custom_call" | custom-call | flops 41999998976 | bytes 18874368 | tf_op jit(solution)/shard_map/pallas_call | solution.py:270
  298.0 48.3 %shard_map.189 = (bf16[2048,1536]{1,0:T(8,128)(2,1)}, bf16[2048,1536]{1,0:T(8,128)(2,1)}, f32[2048,128]{1,0:T(8,128)}, bf16[3,4,1536,256]{3,2,1,0:T(8,128)(2,1)}) custom-call(s32[4]{0:T(128)} %add_add_fusion.span_ref, s32[32]{0:T(128)} %copy-done.13, s32[8192]{0:T(1024)} %copy-done.12, bf16[8192,1536]{1,0:T(8,128)(2,1)} %get-tuple-element.77.row_ref, ...), custom_call_target="tpu_custom_call" | custom-call | flops 65229815808 | bytes 28311552 | tf_op jit(solution)/shard_map/pallas_call | solution.py:436
  349.0 50.2 %shard_map.190 = (bf16[2048,1536]{1,0:T(8,128)(2,1)}, bf16[2048,1536]{1,0:T(8,128)(2,1)}, f32[2048,128]{1,0:T(8,128)}, bf16[3,6,1536,256]{3,2,1,0:T(8,128)(2,1)}) custom-call(s32[4]{0:T(128)} %add_add_fusion.1.span_ref, s32[32]{0:T(128)} %copy-done.13, s32[8192]{0:T(1024)} %copy-done.12, bf16[8192,1536]{1,0:T(8,128)(2,1)} %get-tuple-element.77.row_ref, ...), custom_call_target="tpu_custom_call" | custom-call | flops 97844723712 | bytes 42467328 | tf_op jit(solution)/shard_map/pallas_call | solution.py:436
  405.9 49.3 %shard_map.191 = (bf16[2048,1536]{1,0:T(8,128)(2,1)}, bf16[2048,1536]{1,0:T(8,128)(2,1)}, f32[2048,128]{1,0:T(8,128)}, bf16[3,6,768,256]{3,2,1,0:T(8,128)(2,1)}, bf16[3,6,768,256]{3,2,1,0:T(8,128)(2,1)}) custom-call(s32[4]{0:T(128)} %add_add_fusion.2.span_ref, s32[32]{0:T(128)} %copy-done.13, s32[8192]{0:T(1024)} %copy-done.12, ...), custom_call_target="tpu_custom_call" | custom-call | flops 97844723712 | bytes 42467328 | tf_op jit(solution)/shard_map/pallas_call | solution.py:436
  455.1 5.0 add_convert_fusion.10
  470.2 29.4 %collective-permute-done.22 = bf16[512,1536]{1,0:T(8,128)(2,1)} collective-permute-done((bf16[512,1536]{1,0:T(8,128)(2,1)}, bf16[512,1536]{1,0:T(8,128)(2,1)}, u32[]{:S(2)}, u32[]{:S(2)}) %collective-permute-start.22) | collective-permute-done | bytes 1572896 | tf_op jit(solution)/shard_map/ppermute | solution.py:482
  513.0 13.9 %collective-permute-done.26 = f32[2,512]{1,0:T(2,128)S(1)} collective-permute-done((f32[2,512]{1,0:T(2,128)S(1)}, f32[2,512]{1,0:T(2,128)S(1)}, u32[]{:S(2)}, u32[]{:S(2)}) %collective-permute-start.26) | collective-permute-done | bytes 4128 | tf_op jit(solution)/shard_map/ppermute | solution.py:482
  542.0 5.9 collective-permute-done.29
  547.9 10.5 %collective-permute-done.30 = bf16[384,512]{1,0:T(8,128)(2,1)S(1)} collective-permute-done((bf16[384,512]{1,0:T(8,128)(2,1)S(1)}, bf16[384,512]{1,0:T(8,128)(2,1)S(1)}, u32[]{:S(2)}, u32[]{:S(2)}) %collective-permute-start.30) | collective-permute-done | bytes 393248 | tf_op jit(solution)/shard_map/ppermute | solution.py:482
  560.0 10.3 %add_convert_fusion = bf16[3,6,768,256]{3,2,1,0:T(8,128)(2,1)} fusion(bf16[3,6,768,256]{3,2,1,0:T(8,128)(2,1)} %collective-permute-done.32, bf16[3,6,768,256]{3,2,1,0:T(8,128)(2,1)} %get-tuple-element.100), kind=kLoop, calls=%fused_computation.3 | loop fusion | flops 14155776 | bytes 21233664 | tf_op jit(solution)/shard_map/convert_element_type | solution.py:721
  570.4 5.0 add_convert_fusion.6
  578.1 48.1 %shard_map.192 = bf16[640,2048]{1,0:T(8,128)(2,1)S(1)} custom-call(bf16[640,2048]{1,0:T(8,128)(2,1)S(1)} %copy-done.17, bf16[384,2048]{1,0:T(8,128)(2,1)S(1)} %copy-done.7, f32[2,8,1,768]{3,2,1,0:T(1,128)S(1)} %get-tuple-element.108.total_ref, bf16[384,2048]{1,0:T(8,128)(2,1)S(1)} %copy-done.5), custom_call_target="tpu_custom_call" | custom-call | flops 56371445760 | bytes 10485760 | tf_op jit(solution)/shard_map/pallas_call | solution.py:139
  630.8 7.6 convolution_convert_fusion
  643.7 33.2 %collective-permute-done.35 = bf16[512,1536]{1,0:T(8,128)(2,1)S(1)} collective-permute-done((bf16[512,1536]{1,0:T(8,128)(2,1)S(1)}, bf16[512,1536]{1,0:T(8,128)(2,1)S(1)}, u32[]{:S(2)}, u32[]{:S(2)}) %collective-permute-start.35) | collective-permute-done | bytes 1572896 | tf_op jit(solution)/shard_map/ppermute | solution.py:482
  686.9 15.1 %collective-permute-done.37 = bf16[256,1536]{1,0:T(8,128)(2,1)S(1)} collective-permute-done((bf16[256,1536]{1,0:T(8,128)(2,1)S(1)}, bf16[256,1536]{1,0:T(8,128)(2,1)S(1)}, u32[]{:S(2)}, u32[]{:S(2)}) %collective-permute-start.37) | collective-permute-done | bytes 786464 | tf_op jit(solution)/shard_map/ppermute | solution.py:482
  717.1 18.0 %collective-permute-done.46 = bf16[384,1536]{1,0:T(8,128)(2,1)S(1)} collective-permute-done((bf16[384,1536]{1,0:T(8,128)(2,1)S(1)}, bf16[384,1536]{1,0:T(8,128)(2,1)S(1)}, u32[]{:S(2)}, u32[]{:S(2)}) %collective-permute-start.46) | collective-permute-done | bytes 1179680 | tf_op jit(solution)/shard_map/ppermute | solution.py:482
  743.6 5.5 collective-permute-done.48
  751.7 4.7 copy.54
  757.1 5.4 add_convert_fusion.1
  764.9 9.6 %reduce-scatter.11.cloned.1.call-done = bf16[3,6,192,256]{3,2,1,0:T(8,128)(2,1)} async-done(((bf16[3,6,768,256]{3,2,1,0:T(8,128)(2,1)}), bf16[3,6,192,256]{3,2,1,0:T(8,128)(2,1)}) %reduce-scatter.11.cloned.1.call-update) | async-done | bytes 1769488 | tf_op jit(solution)/shard_map/reduce_scatter | solution.py:724
  784.9 12.1 %collective-permute-done.43 = f32[18,1536]{1,0:T(8,128)S(1)} collective-permute-done((f32[18,1536]{1,0:T(8,128)S(1)}, f32[18,1536]{1,0:T(8,128)S(1)}, u32[]{:S(2)}, u32[]{:S(2)}) %collective-permute-start.43) | collective-permute-done | bytes 110624 | tf_op jit(solution)/shard_map/ppermute | solution.py:618
  (402 shorter events, 215.9 us)
Async XLA Ops:
  7.2 78.0 %all-gather.5.cloned.1.call-start = ((), (), s32[]{:S(2)}) async-start(), calls=%async_computation.4 | async-start | bytes 3981312 | tf_op jit(solution)/shard_map/all_gather | solution.py:655
  9.9 288.1 %all-gather.7.cloned.1.call-start = ((), (), s32[]{:S(2)}) async-start(), calls=%async_computation.5 | async-start | bytes 10616832 | tf_op jit(solution)/shard_map/all_gather | solution.py:676
  13.3 335.7 %all-gather.9.cloned.1.call-start = ((), (), s32[]{:S(2)}) async-start(), calls=%async_computation.6 | async-start | bytes 15925248 | tf_op jit(solution)/shard_map/all_gather | solution.py:676
  18.0 387.8 %all-gather.11.cloned.1.call-start = ((), (), s32[]{:S(2)}) async-start(), calls=%async_computation.7 | async-start | bytes 15925248 | tf_op jit(solution)/shard_map/all_gather | solution.py:676
  19.4 37.5 %collective-permute-start.1 = (bf16[512,1536]{1,0:T(8,128)(2,1)S(1)}, bf16[512,1536]{1,0:T(8,128)(2,1)}, u32[]{:S(2)}, u32[]{:S(2)}) collective-permute-start(bf16[512,1536]{1,0:T(8,128)(2,1)S(1)} %copy-done.18), channel_id=1, source_target_pairs={{0,2},{1,3},{2,0},{3,1},{4,6},{5,7},{6,4},{7,5},{8,10},{9,11},{10,... | collective-permute-start | bytes 4718600 | tf_op jit(solution)/shard_map/ppermute | solution.py:482
  22.5 38.4 %collective-permute-start = (bf16[512,1536]{1,0:T(8,128)(2,1)S(1)}, bf16[512,1536]{1,0:T(8,128)(2,1)}, u32[]{:S(2)}, u32[]{:S(2)}) collective-permute-start(bf16[512,1536]{1,0:T(8,128)(2,1)S(1)} %copy-done.18), channel_id=1, source_target_pairs={{0,1},{1,0},{2,3},{3,2},{4,5},{5,4},{6,7},{7,6},{8,9},{9,8},{10,11... | collective-permute-start | bytes 4718600 | tf_op jit(solution)/shard_map/ppermute | solution.py:482
  24.0 39.7 %collective-permute-start.5 = (bf16[2,384]{1,0:T(2,128)(2,1)S(1)}, bf16[2,384]{1,0:T(2,128)(2,1)S(1)}, u32[]{:S(2)}, u32[]{:S(2)}) collective-permute-start(bf16[2,384]{1,0:T(2,128)(2,1)S(1)} %pad_maximum_fusion.19), channel_id=1, source_target_pairs={{0,2},{1,3},{2,0},{3,1},{4,6},{5,7},{6,4},{7,5},{8,10},{9,11},{10,... | collective-permute-start | bytes 4616 | tf_op jit(solution)/shard_map/ppermute | solution.py:482
  24.6 39.1 %collective-permute-start.6 = (bf16[2,384]{1,0:T(2,128)(2,1)S(1)}, bf16[2,384]{1,0:T(2,128)(2,1)S(1)}, u32[]{:S(2)}, u32[]{:S(2)}) collective-permute-start(bf16[2,384]{1,0:T(2,128)(2,1)S(1)} %pad_maximum_fusion.19), channel_id=1, source_target_pairs={{0,3},{1,2},{2,1},{3,0},{4,7},{5,6},{6,5},{7,4},{8,11},{9,10},{10,... | collective-permute-start | bytes 4616 | tf_op jit(solution)/shard_map/ppermute | solution.py:482
  26.1 37.6 %collective-permute-start.4 = (bf16[2,384]{1,0:T(2,128)(2,1)S(1)}, bf16[2,384]{1,0:T(2,128)(2,1)S(1)}, u32[]{:S(2)}, u32[]{:S(2)}) collective-permute-start(bf16[2,384]{1,0:T(2,128)(2,1)S(1)} %pad_maximum_fusion.19), channel_id=1, source_target_pairs={{0,1},{1,0},{2,3},{3,2},{4,5},{5,4},{6,7},{7,6},{8,9},{9,8},{10,11... | collective-permute-start | bytes 4616 | tf_op jit(solution)/shard_map/ppermute | solution.py:482
  30.1 600.7 %reduce-scatter.7.cloned.1.call-start = ((), (), s32[]{:S(2)}) async-start(), calls=%async_computation.8 | async-start | bytes 10616832 | tf_op jit(solution)/shard_map/reduce_scatter | solution.py:729
  96.5 44.3 %collective-permute-start.10 = (bf16[1536,384]{1,0:T(8,128)(2,1)S(1)}, bf16[1536,384]{1,0:T(8,128)(2,1)S(1)}, u32[]{:S(2)}, u32[]{:S(2)}) collective-permute-start(bf16[1536,384]{1,0:T(8,128)(2,1)S(1)} %slice.292), channel_id=1, source_target_pairs={{0,2},{1,3},{2,0},{3,1},{4,6},{5,7},{6,4},{7,5},{8,10},{9,11},{10,... | collective-permute-start | bytes 3538952 | tf_op jit(solution)/shard_map/ppermute | solution.py:482
  98.1 42.8 %collective-permute-start.8 = (bf16[1536,384]{1,0:T(8,128)(2,1)S(1)}, bf16[1536,384]{1,0:T(8,128)(2,1)S(1)}, u32[]{:S(2)}, u32[]{:S(2)}) collective-permute-start(bf16[1536,384]{1,0:T(8,128)(2,1)S(1)} %slice.292), channel_id=1, source_target_pairs={{0,1},{1,0},{2,3},{3,2},{4,5},{5,4},{6,7},{7,6},{8,9},{9,8},{10,11... | collective-permute-start | bytes 3538952 | tf_op jit(solution)/shard_map/ppermute | solution.py:482
  98.5 72.1 %collective-permute-start.19 = (bf16[512,1536]{1,0:T(8,128)(2,1)S(1)}, bf16[512,1536]{1,0:T(8,128)(2,1)S(1)}, u32[]{:S(2)}, u32[]{:S(2)}) collective-permute-start(bf16[512,1536]{1,0:T(8,128)(2,1)S(1)} %copy-done.2), channel_id=1, source_target_pairs={{0,2},{1,3},{2,0},{3,1},{4,6},{5,7},{6,4},{7,5},{8,10},{9,11},{10,... | collective-permute-start | bytes 4718600 | tf_op jit(solution)/shard_map/ppermute | solution.py:482
  99.1 74.0 %collective-permute-start.18 = (bf16[512,1536]{1,0:T(8,128)(2,1)S(1)}, bf16[512,1536]{1,0:T(8,128)(2,1)S(1)}, u32[]{:S(2)}, u32[]{:S(2)}) collective-permute-start(bf16[512,1536]{1,0:T(8,128)(2,1)S(1)} %copy-done.2), channel_id=1, source_target_pairs={{0,1},{1,0},{2,3},{3,2},{4,5},{5,4},{6,7},{7,6},{8,9},{9,8},{10,11... | collective-permute-start | bytes 4718600 | tf_op jit(solution)/shard_map/ppermute | solution.py:482
  140.0 29.1 %collective-permute-start.7 = (bf16[384,512]{1,0:T(8,128)(2,1)S(1)}, bf16[384,512]{1,0:T(8,128)(2,1)S(1)}, u32[]{:S(2)}, u32[]{:S(2)}) collective-permute-start(bf16[384,512]{1,0:T(8,128)(2,1)S(1)} %get-tuple-element.233), channel_id=1, source_target_pairs={{0,1},{1,0},{2,3},{3,2},{4,5},{5,4},{6,7},{7,6},{8,9},{9,8},{10,11... | collective-permute-start | bytes 1179656 | tf_op jit(solution)/shard_map/ppermute | solution.py:482
  140.9 40.8 %collective-permute-start.12 = (bf16[768,384]{1,0:T(8,128)(2,1)S(1)}, bf16[768,384]{1,0:T(8,128)(2,1)S(1)}, u32[]{:S(2)}, u32[]{:S(2)}) collective-permute-start(bf16[768,384]{1,0:T(8,128)(2,1)S(1)} %slice.293), channel_id=1, source_target_pairs={{0,1},{1,0},{2,3},{3,2},{4,5},{5,4},{6,7},{7,6},{8,9},{9,8},{10,11... | collective-permute-start | bytes 1769480 | tf_op jit(solution)/shard_map/ppermute | solution.py:482
  142.5 39.4 %collective-permute-start.13 = (bf16[768,384]{1,0:T(8,128)(2,1)S(1)}, bf16[768,384]{1,0:T(8,128)(2,1)S(1)}, u32[]{:S(2)}, u32[]{:S(2)}) collective-permute-start(bf16[768,384]{1,0:T(8,128)(2,1)S(1)} %slice.294), channel_id=1, source_target_pairs={{0,2},{1,3},{2,0},{3,1},{4,6},{5,7},{6,4},{7,5},{8,10},{9,11},{10,... | collective-permute-start | bytes 1769480 | tf_op jit(solution)/shard_map/ppermute | solution.py:482
  190.5 53.7 %collective-permute-start.15 = (bf16[512,1536]{1,0:T(8,128)(2,1)S(1)}, bf16[512,1536]{1,0:T(8,128)(2,1)}, u32[]{:S(2)}, u32[]{:S(2)}) collective-permute-start(bf16[512,1536]{1,0:T(8,128)(2,1)S(1)} %get-tuple-element.89.refs_0_), channel_id=1, source_target_pairs={{0,2},{1,3},{2,0},{3,1},{4,6},{5,7},{6,4},{7,5},{8,10},{9,11},{10,... | collective-permute-start | bytes 4718600 | tf_op jit(solution)/shard_map/ppermute | solution.py:482
  192.0 54.8 %collective-permute-start.14 = (bf16[512,1536]{1,0:T(8,128)(2,1)S(1)}, bf16[512,1536]{1,0:T(8,128)(2,1)}, u32[]{:S(2)}, u32[]{:S(2)}) collective-permute-start(bf16[512,1536]{1,0:T(8,128)(2,1)S(1)} %get-tuple-element.89.refs_0_), channel_id=1, source_target_pairs={{0,1},{1,0},{2,3},{3,2},{4,5},{5,4},{6,7},{7,6},{8,9},{9,8},{10,11... | collective-permute-start | bytes 4718600 | tf_op jit(solution)/shard_map/ppermute | solution.py:482
  192.8 48.6 %collective-permute-start.20 = (bf16[256,1536]{1,0:T(8,128)(2,1)}, bf16[256,1536]{1,0:T(8,128)(2,1)}, u32[]{:S(2)}, u32[]{:S(2)}) collective-permute-start(bf16[256,1536]{1,0:T(8,128)(2,1)} %slice.303), channel_id=1, source_target_pairs={{0,1},{1,0},{2,3},{3,2},{4,5},{5,4},{6,7},{7,6},{8,9},{9,8},{10,11... | collective-permute-start | bytes 2359304 | tf_op jit(solution)/shard_map/ppermute | solution.py:482
  194.0 47.4 %collective-permute-start.21 = (bf16[256,1536]{1,0:T(8,128)(2,1)}, bf16[256,1536]{1,0:T(8,128)(2,1)}, u32[]{:S(2)}, u32[]{:S(2)}) collective-permute-start(bf16[256,1536]{1,0:T(8,128)(2,1)} %slice.304), channel_id=1, source_target_pairs={{0,2},{1,3},{2,0},{3,1},{4,6},{5,7},{6,4},{7,5},{8,10},{9,11},{10,... | collective-permute-start | bytes 2359304 | tf_op jit(solution)/shard_map/ppermute | solution.py:482
  346.3 334.7 %reduce-scatter.9.cloned.1.call-start = ((), (), s32[]{:S(2)}) async-start(), calls=%async_computation.9 | async-start | bytes 15925248 | tf_op jit(solution)/shard_map/reduce_scatter | solution.py:729
  399.2 375.3 %reduce-scatter.11.cloned.1.call-start = ((), (), s32[]{:S(2)}) async-start(), calls=%async_computation.10 | async-start | bytes 8847360 | tf_op jit(solution)/shard_map/reduce_scatter | solution.py:724
  462.7 36.9 %collective-permute-start.22 = (bf16[512,1536]{1,0:T(8,128)(2,1)}, bf16[512,1536]{1,0:T(8,128)(2,1)}, u32[]{:S(2)}, u32[]{:S(2)}) collective-permute-start(bf16[512,1536]{1,0:T(8,128)(2,1)} %pad_maximum_fusion.7), channel_id=1, source_target_pairs={{0,1},{1,0},{2,3},{3,2},{4,5},{5,4},{6,7},{7,6},{8,9},{9,8},{10,11... | collective-permute-start | bytes 4718600 | tf_op jit(solution)/shard_map/ppermute | solution.py:482
  464.1 37.3 %collective-permute-start.23 = (bf16[512,1536]{1,0:T(8,128)(2,1)}, bf16[512,1536]{1,0:T(8,128)(2,1)}, u32[]{:S(2)}, u32[]{:S(2)}) collective-permute-start(bf16[512,1536]{1,0:T(8,128)(2,1)} %pad_maximum_fusion.8), channel_id=1, source_target_pairs={{0,2},{1,3},{2,0},{3,1},{4,6},{5,7},{6,4},{7,5},{8,10},{9,11},{10,... | collective-permute-start | bytes 4718600 | tf_op jit(solution)/shard_map/ppermute | solution.py:482
  570.4 253.5 %reduce-scatter.13.cloned.1.call-start = ((), (), s32[]{:S(2)}) async-start(), calls=%async_computation.11 | async-start | bytes 3538944
  575.6 50.5 %collective-permute-start.33 = (bf16[512,1536]{1,0:T(8,128)(2,1)S(1)}, bf16[512,1536]{1,0:T(8,128)(2,1)S(1)}, u32[]{:S(2)}, u32[]{:S(2)}) collective-permute-start(bf16[512,1536]{1,0:T(8,128)(2,1)S(1)} %pad_maximum_fusion.10), channel_id=1, source_target_pairs={{0,1},{1,0},{2,3},{3,2},{4,5},{5,4},{6,7},{7,6},{8,9},{9,8},{10,11... | collective-permute-start | bytes 4718600 | tf_op jit(solution)/shard_map/ppermute | solution.py:482
  576.6 52.2 %collective-permute-start.34 = (bf16[512,1536]{1,0:T(8,128)(2,1)S(1)}, bf16[512,1536]{1,0:T(8,128)(2,1)S(1)}, u32[]{:S(2)}, u32[]{:S(2)}) collective-permute-start(bf16[512,1536]{1,0:T(8,128)(2,1)S(1)} %pad_maximum_fusion.11), channel_id=1, source_target_pairs={{0,2},{1,3},{2,0},{3,1},{4,6},{5,7},{6,4},{7,5},{8,10},{9,11},{10,... | collective-permute-start | bytes 4718600 | tf_op jit(solution)/shard_map/ppermute | solution.py:482
  641.3 35.6 %collective-permute-start.35 = (bf16[512,1536]{1,0:T(8,128)(2,1)S(1)}, bf16[512,1536]{1,0:T(8,128)(2,1)S(1)}, u32[]{:S(2)}, u32[]{:S(2)}) collective-permute-start(bf16[512,1536]{1,0:T(8,128)(2,1)S(1)} %pad_maximum_fusion.12), channel_id=1, source_target_pairs={{0,1},{1,0},{2,3},{3,2},{4,5},{5,4},{6,7},{7,6},{8,9},{9,8},{10,11... | collective-permute-start | bytes 4718600 | tf_op jit(solution)/shard_map/ppermute | solution.py:482
  642.6 36.4 %collective-permute-start.36 = (bf16[512,1536]{1,0:T(8,128)(2,1)S(1)}, bf16[512,1536]{1,0:T(8,128)(2,1)S(1)}, u32[]{:S(2)}, u32[]{:S(2)}) collective-permute-start(bf16[512,1536]{1,0:T(8,128)(2,1)S(1)} %pad_maximum_fusion.13), channel_id=1, source_target_pairs={{0,2},{1,3},{2,0},{3,1},{4,6},{5,7},{6,4},{7,5},{8,10},{9,11},{10,... | collective-permute-start | bytes 4718600 | tf_op jit(solution)/shard_map/ppermute | solution.py:482
  762.5 46.4 %collective-permute-start.39 = (bf16[256,1536]{1,0:T(8,128)(2,1)}, bf16[256,1536]{1,0:T(8,128)(2,1)}, u32[]{:S(2)}, u32[]{:S(2)}) collective-permute-start(bf16[256,1536]{1,0:T(8,128)(2,1)} %get-tuple-element.120), channel_id=1, source_target_pairs={{0,2},{1,3},{2,0},{3,1},{4,6},{5,7},{6,4},{7,5},{8,10},{9,11},{10,... | collective-permute-start | bytes 2359304 | tf_op jit(solution)/shard_map/ppermute | solution.py:482
  764.1 44.8 %collective-permute-start.40 = (bf16[256,1536]{1,0:T(8,128)(2,1)}, bf16[256,1536]{1,0:T(8,128)(2,1)}, u32[]{:S(2)}, u32[]{:S(2)}) collective-permute-start(bf16[256,1536]{1,0:T(8,128)(2,1)} %get-tuple-element.121), channel_id=1, source_target_pairs={{0,1},{1,0},{2,3},{3,2},{4,5},{5,4},{6,7},{7,6},{8,9},{9,8},{10,11... | collective-permute-start | bytes 2359304 | tf_op jit(solution)/shard_map/ppermute | solution.py:482
  (99 other events, 1159.7 us)
Sparse Core Ops, SparseCore 0:
  10.2 44.2 all-gather.4
  56.1 89.6 all-gather.6
  147.9 128.0 all-gather.8
  278.0 127.7 all-gather.10
  408.0 97.6 reduce-scatter.6
  507.9 142.4 reduce-scatter.8
  652.6 121.8 reduce-scatter.10
  776.8 42.2 reduce-scatter.12

commit v6 on v5

--- a/solution.py
+++ b/solution.py
@@ -14,8 +14,8 @@
 TOPK = 2
 SEQUENCE_LENGTH = 2048
 BLOCK = 256
-QB = 256
-KB = 256
+QB = 512
+KB = 512
 LANES = 128
 PITCH = 13
 UNROLL = 8
@@ -610,13 +610,12 @@
     return result
 
 
-def sum_all(value):
-    for axis in ("wide", "narrow"):
-        count = lax.axis_size(axis)
-        bit = 1
-        while bit < count:
-            value = value + lax.ppermute(value, axis, [(index, index ^ bit) for index in range(count)])
-            bit *= 2
+def sum_along(value, axis):
+    count = lax.axis_size(axis)
+    bit = 1
+    while bit < count:
+        value = value + lax.ppermute(value, axis, [(index, index ^ bit) for index in range(count)])
+        bit *= 2
     return value
 
 
@@ -795,12 +794,8 @@
     scale_one_own = lax.rsqrt(jnp.mean(x_own * x_own, axis=1, keepdims=True) + EPSILON)
     normed_one_own = x_own * scale_one_own
     gain_one_part = jnp.sum(input_sum * normed_one_own, axis=0)
-    small_sum = sum_all(
-        after(
-            jnp.concatenate([grad_router, gain_one_part[None], gain_two_part[None]], axis=0),
-            grads[2],
-        )
-    )
+    small_part = jnp.concatenate([grad_router, gain_one_part[None], gain_two_part[None]], axis=0)
+    small_sum = sum_along(after(sum_along(small_part, "wide"), grads[2]), "narrow")
     gain_own = lax.dynamic_slice_in_dim(small_sum[E:], me * gain_part, gain_part, 1)
     router_part = router_weight.shape[0]
     router_grad = lax.dynamic_slice_in_dim(
@@ -820,7 +815,7 @@
     ).astype(F32)
     input_w_grad = packed_grad[:, :head_columns]
     output_w_grad = packed_grad[:, head_columns:].T
-    grads = after(grads, block_output, small_sum, grad_output_w, input_grad)
+    grads = after(grads, input_grad)
     gate_grad, up_grad, down_grad = (
         jnp.concatenate([grad[index] for grad in grads], axis=0).astype(F32) for index in range(3)
     )

time: 843 us -> 845 us (level)
  waiting for transfers between devices: 271 us -> 292 us
  Pallas kernels: 282 us -> 267 us
    pallas_call x1, Pallas kernels: 38.2 us -> 25.4 us  [attend_forward(): pl.pallas_call(functools.partial(forward_kernel, heads), grid=(groups, bl...]
    ppermute x44, waiting for transfers between devices: 232 us -> 244 us  [swap(): lax.ppermute(value, 'narrow', [(index, index ^ bit) for index in range(co...]
    unnamed x152 -> x154, local copies, waits for them, and re-layouts: 23.7 us -> 21.8 us
  transfers between devices with their start and end apart: 58 -> 58, of which waited for: 25 -> 23; matrix products, arithmetic and copies ran while one was open for 22% -> 21% of each run, Pallas kernels for 34% -> 32%
where the time goes in v6:
time: 845 us; the launch traced here: 835 us
  waiting for transfers between devices  292 us (35%)
  Pallas kernels  267 us (32%)
  other arithmetic  100 us (12%)
  starting transfers between devices  59.5 us (7%)
  local copies, waits for them, and re-layouts  59.4 us (7%)
  matrix products  38.3 us (5%)
  between operations  18.6 us (2%)
    ppermute x44, waiting for transfers between devices, swap(): lax.ppermute(value, 'narrow', [(index, index ^ bit) for index in range(co...  244 us
    pallas_call x3, Pallas kernels, run_experts(): pl.pallas_call(functools.partial(expert_kernel, shards), grid_spec=pltpu....  148 us
    ppermute x44, starting transfers between devices, swap(): lax.ppermute(value, 'narrow', [(index, index ^ bit) for index in range(co...  53.5 us
    pallas_call x2, Pallas kernels, dispatch(): pl.pallas_call(functools.partial(dispatch_kernel, len(sources), gated), g...  47.8 us
    pallas_call x1, Pallas kernels, attend_backward(): pl.pallas_call(functools.partial(backward_kernel, heads), grid=(groups, b...  46.2 us
    pallas_call x1, Pallas kernels, attend_forward(): pl.pallas_call(functools.partial(forward_kernel, heads), grid=(groups, bl...  25.4 us
    ppermute x5, waiting for transfers between devices, sum_along(): lax.ppermute(value, axis, [(index, index ^ bit) for index in range(count)])  24.5 us
    unnamed x154, local copies, waits for them, and re-layouts  21.8 us
  transfers between devices with their start and end apart: 58, of which 23 were waited for; matrix products, arithmetic and copies ran while one was open for 21% of the time, Pallas kernels for 32%

profile of v6, /device:TPU:0, one launch (start us, length us, event | category | flops | bytes accessed | tf_op | source)
XLA Modules:
  0.0 835.3 jit_solution(9680344321713881010)
XLA Ops:
  32.5 4.6 reduce-window.11
  37.9 19.0 %collective-permute-done.1 = bf16[512,1536]{1,0:T(8,128)(2,1)} collective-permute-done((bf16[512,1536]{1,0:T(8,128)(2,1)S(1)}, bf16[512,1536]{1,0:T(8,128)(2,1)}, u32[]{:S(2)}, u32[]{:S(2)}) %collective-permute-start.1) | collective-permute-done | bytes 1572896 | tf_op jit(solution)/shard_map/ppermute | solution.py:482
  64.4 13.7 %collective-permute-done.2 = bf16[256,1536]{1,0:T(8,128)(2,1)} collective-permute-done((bf16[256,1536]{1,0:T(8,128)(2,1)}, bf16[256,1536]{1,0:T(8,128)(2,1)}, u32[]{:S(2)}, u32[]{:S(2)}) %collective-permute-start.2) | collective-permute-done | bytes 786464 | tf_op jit(solution)/shard_map/ppermute | solution.py:482
  87.0 9.5 %convolution_convert_fusion.2.qkv_ref = bf16[640,2048]{1,0:T(8,128)(2,1)S(1)} fusion(f32[1536]{0:T(1024)S(1)} %get-tuple-element.183, f32[2048]{0:T(1024)S(1)} %add_rsqrt_fusion, bf16[1536,1152]{1,0:T(8,128)(2,1)} %all-gather.5.cloned.1.call-done, bf16[512,1536]{1,0:T(8,128)(2,1)} %copy-done.31, bf16[512,1536]{1,0:T(8,128)(2,1)} %copy-done.33, ...), kind=kOutput, calls=%fused_computation.23 | convolution fusion | flops 4062445568 | bytes 10893312 | tf_op jit(solution)/shard_map/td,dc->ct/dot_general | solution.py:681
  100.6 25.4 %shard_map.186 = (bf16[384,2048]{1,0:T(8,128)(2,1)S(1)}, f32[2,4,1,1536]{3,2,1,0:T(1,128)S(1)}) custom-call(bf16[640,2048]{1,0:T(8,128)(2,1)S(1)} %convolution_convert_fusion.2.qkv_ref), custom_call_target="tpu_custom_call" | custom-call | flops 45097156608 | bytes 5242880 | tf_op jit(solution)/shard_map/pallas_call | solution.py:77
  132.3 36.8 %collective-permute-done.7 = bf16[384,512]{1,0:T(8,128)(2,1)S(1)} collective-permute-done((bf16[384,512]{1,0:T(8,128)(2,1)S(1)}, bf16[384,512]{1,0:T(8,128)(2,1)S(1)}, u32[]{:S(2)}, u32[]{:S(2)}) %collective-permute-start.7) | collective-permute-done | bytes 393248 | tf_op jit(solution)/shard_map/ppermute | solution.py:482
  174.1 7.7 collective-permute-done.12
  194.6 15.5 %scatter_custom_fusion.token_ref = s32[8192]{0:T(1024)S(1)} fusion(s32[4096]{0:T(1024)S(1)} %bitcast.124, s32[4096]{0:T(1024)S(1)} %add_select_fusion, s32[]{:T(128)} %constant.88.clone.1), kind=kCustom, calls=%fused_computation.186 | custom fusion | bytes 32772 | tf_op jit(solution)/shard_map/scatter | solution.py:170
  213.1 28.4 %collective-permute-done.20 = bf16[256,1536]{1,0:T(8,128)(2,1)} collective-permute-done((bf16[256,1536]{1,0:T(8,128)(2,1)}, bf16[256,1536]{1,0:T(8,128)(2,1)}, u32[]{:S(2)}, u32[]{:S(2)}) %collective-permute-start.20) | collective-permute-done | bytes 786464 | tf_op jit(solution)/shard_map/ppermute | solution.py:482
  249.1 20.9 %shard_map.188.cot_ref = bf16[8192,1536]{1,0:T(8,128)(2,1)} custom-call(s32[8192]{0:T(1024)S(1)} %scatter_custom_fusion.token_ref, s32[32]{0:T(128)S(1)} %broadcast_minimum_fusion.expert_ref, s32[1]{0:T(128)} %bitcast.7.live_ref, s32[1]{0:T(128)} %bitcast.8.me_ref, bf16[512,1536]{1,0:T(8,128)(2,1)S(1)} %copy-done.3, bf16[512,1536]{1,0:T(8,128)(2,1)S(1)} %copy-done.11, ...), custom_call_target="tpu_custom_call" | custom-call | flops 41999998976 | bytes 18874368 | tf_op jit(solution)/shard_map/pallas_call | solution.py:270
  271.2 26.9 %shard_map.187 = (bf16[8192,1536]{1,0:T(8,128)(2,1)}, f32[8192,1]{1,0:T(8,128)}) custom-call(s32[8192]{0:T(1024)S(1)} %scatter_custom_fusion.token_ref, s32[32]{0:T(128)S(1)} %broadcast_minimum_fusion.expert_ref, s32[1]{0:T(128)} %bitcast.7.live_ref, s32[1]{0:T(128)} %bitcast.8.me_ref, bf16[512,1536]{1,0:T(8,128)(2,1)S(1)} %get-tuple-element.89.refs_0_, ...), custom_call_target="tpu_custom_call" | custom-call | flops 41999998976 | bytes 18874368 | tf_op jit(solution)/shard_map/pallas_call | solution.py:270
  298.1 44.4 %shard_map.189 = (bf16[2048,1536]{1,0:T(8,128)(2,1)}, bf16[2048,1536]{1,0:T(8,128)(2,1)}, f32[2048,128]{1,0:T(8,128)}, bf16[3,4,1536,256]{3,2,1,0:T(8,128)(2,1)}) custom-call(s32[4]{0:T(128)} %add_add_fusion.span_ref, s32[32]{0:T(128)} %copy-done.13, s32[8192]{0:T(1024)} %copy-done.12, bf16[8192,1536]{1,0:T(8,128)(2,1)} %get-tuple-element.77.row_ref, ...), custom_call_target="tpu_custom_call" | custom-call | flops 65229815808 | bytes 28311552 | tf_op jit(solution)/shard_map/pallas_call | solution.py:436
  345.1 50.1 %shard_map.190 = (bf16[2048,1536]{1,0:T(8,128)(2,1)}, bf16[2048,1536]{1,0:T(8,128)(2,1)}, f32[2048,128]{1,0:T(8,128)}, bf16[3,6,1536,256]{3,2,1,0:T(8,128)(2,1)}) custom-call(s32[4]{0:T(128)} %add_add_fusion.1.span_ref, s32[32]{0:T(128)} %copy-done.13, s32[8192]{0:T(1024)} %copy-done.12, bf16[8192,1536]{1,0:T(8,128)(2,1)} %get-tuple-element.77.row_ref, ...), custom_call_target="tpu_custom_call" | custom-call | flops 97844723712 | bytes 42467328 | tf_op jit(solution)/shard_map/pallas_call | solution.py:436
  397.9 8.0 all-gather.11.cloned.1.call-done.weight_ref
  405.9 53.3 %shard_map.191 = (bf16[2048,1536]{1,0:T(8,128)(2,1)}, bf16[2048,1536]{1,0:T(8,128)(2,1)}, f32[2048,128]{1,0:T(8,128)}, bf16[3,6,768,256]{3,2,1,0:T(8,128)(2,1)}, bf16[3,6,768,256]{3,2,1,0:T(8,128)(2,1)}) custom-call(s32[4]{0:T(128)} %add_add_fusion.2.span_ref, s32[32]{0:T(128)} %copy-done.13, s32[8192]{0:T(1024)} %copy-done.12, ...), custom_call_target="tpu_custom_call" | custom-call | flops 97844723712 | bytes 42467328 | tf_op jit(solution)/shard_map/pallas_call | solution.py:436
  459.1 5.1 add_convert_fusion.10
  474.2 29.4 %collective-permute-done.22 = bf16[512,1536]{1,0:T(8,128)(2,1)} collective-permute-done((bf16[512,1536]{1,0:T(8,128)(2,1)}, bf16[512,1536]{1,0:T(8,128)(2,1)}, u32[]{:S(2)}, u32[]{:S(2)}) %collective-permute-start.22) | collective-permute-done | bytes 1572896 | tf_op jit(solution)/shard_map/ppermute | solution.py:482
  516.9 13.8 %collective-permute-done.26 = f32[2,512]{1,0:T(2,128)S(1)} collective-permute-done((f32[2,512]{1,0:T(2,128)S(1)}, f32[2,512]{1,0:T(2,128)S(1)}, u32[]{:S(2)}, u32[]{:S(2)}) %collective-permute-start.26) | collective-permute-done | bytes 4128 | tf_op jit(solution)/shard_map/ppermute | solution.py:482
  545.9 5.9 collective-permute-done.29
  551.8 10.5 %collective-permute-done.30 = bf16[384,512]{1,0:T(8,128)(2,1)S(1)} collective-permute-done((bf16[384,512]{1,0:T(8,128)(2,1)S(1)}, bf16[384,512]{1,0:T(8,128)(2,1)S(1)}, u32[]{:S(2)}, u32[]{:S(2)}) %collective-permute-start.30) | collective-permute-done | bytes 393248 | tf_op jit(solution)/shard_map/ppermute | solution.py:482
  563.8 10.5 %add_convert_fusion = bf16[3,6,768,256]{3,2,1,0:T(8,128)(2,1)} fusion(bf16[3,6,768,256]{3,2,1,0:T(8,128)(2,1)} %collective-permute-done.32, bf16[3,6,768,256]{3,2,1,0:T(8,128)(2,1)} %get-tuple-element.100), kind=kLoop, calls=%fused_computation.3 | loop fusion | flops 14155776 | bytes 21233664 | tf_op jit(solution)/shard_map/convert_element_type | solution.py:720
  574.3 5.0 add_convert_fusion.6
  582.1 46.2 %shard_map.192 = bf16[640,2048]{1,0:T(8,128)(2,1)S(1)} custom-call(bf16[640,2048]{1,0:T(8,128)(2,1)S(1)} %copy-done.17, bf16[384,2048]{1,0:T(8,128)(2,1)S(1)} %copy-done.7, f32[2,4,1,1536]{3,2,1,0:T(1,128)S(1)} %get-tuple-element.108.total_ref, bf16[384,2048]{1,0:T(8,128)(2,1)S(1)} %copy-done.5), custom_call_target="tpu_custom_call" | custom-call | flops 56371445760 | bytes 10485760 | tf_op jit(solution)/shard_map/pallas_call | solution.py:139
  632.8 7.7 convolution_convert_fusion
  645.8 33.2 %collective-permute-done.35 = bf16[512,1536]{1,0:T(8,128)(2,1)S(1)} collective-permute-done((bf16[512,1536]{1,0:T(8,128)(2,1)S(1)}, bf16[512,1536]{1,0:T(8,128)(2,1)S(1)}, u32[]{:S(2)}, u32[]{:S(2)}) %collective-permute-start.35) | collective-permute-done | bytes 1572896 | tf_op jit(solution)/shard_map/ppermute | solution.py:482
  688.7 15.4 %collective-permute-done.37 = bf16[256,1536]{1,0:T(8,128)(2,1)S(1)} collective-permute-done((bf16[256,1536]{1,0:T(8,128)(2,1)S(1)}, bf16[256,1536]{1,0:T(8,128)(2,1)S(1)}, u32[]{:S(2)}, u32[]{:S(2)}) %collective-permute-start.37) | collective-permute-done | bytes 786464 | tf_op jit(solution)/shard_map/ppermute | solution.py:482
  719.3 17.9 %collective-permute-done.46 = bf16[384,1536]{1,0:T(8,128)(2,1)S(1)} collective-permute-done((bf16[384,1536]{1,0:T(8,128)(2,1)S(1)}, bf16[384,1536]{1,0:T(8,128)(2,1)S(1)}, u32[]{:S(2)}, u32[]{:S(2)}) %collective-permute-start.46) | collective-permute-done | bytes 1179680 | tf_op jit(solution)/shard_map/ppermute | solution.py:482
  745.8 4.9 collective-permute-done.48
  753.7 4.7 copy.54
  759.0 15.5 %reduce-scatter.11.cloned.1.call-done = bf16[3,6,192,256]{3,2,1,0:T(8,128)(2,1)} async-done(((bf16[3,6,768,256]{3,2,1,0:T(8,128)(2,1)}), bf16[3,6,192,256]{3,2,1,0:T(8,128)(2,1)}) %reduce-scatter.11.cloned.1.call-update) | async-done | bytes 1769488 | tf_op jit(solution)/shard_map/reduce_scatter | solution.py:723
  783.9 6.7 collective-permute-done.42
  796.4 11.3 %collective-permute-done.43 = f32[18,1536]{1,0:T(8,128)S(1)} collective-permute-done((f32[18,1536]{1,0:T(8,128)S(1)}, f32[18,1536]{1,0:T(8,128)S(1)}, u32[]{:S(2)}, u32[]{:S(2)}) %collective-permute-start.43) | collective-permute-done | bytes 110624 | tf_op jit(solution)/shard_map/ppermute | solution.py:617
  (404 shorter events, 208.9 us)
Async XLA Ops:
  7.2 78.0 %all-gather.5.cloned.1.call-start = ((), (), s32[]{:S(2)}) async-start(), calls=%async_computation.4 | async-start | bytes 3981312 | tf_op jit(solution)/shard_map/all_gather | solution.py:654
  9.9 288.2 %all-gather.7.cloned.1.call-start = ((), (), s32[]{:S(2)}) async-start(), calls=%async_computation.5 | async-start | bytes 10616832 | tf_op jit(solution)/shard_map/all_gather | solution.py:675
  13.3 331.8 %all-gather.9.cloned.1.call-start = ((), (), s32[]{:S(2)}) async-start(), calls=%async_computation.6 | async-start | bytes 15925248 | tf_op jit(solution)/shard_map/all_gather | solution.py:675
  18.0 387.8 %all-gather.11.cloned.1.call-start = ((), (), s32[]{:S(2)}) async-start(), calls=%async_computation.7 | async-start | bytes 15925248 | tf_op jit(solution)/shard_map/all_gather | solution.py:675
  19.4 37.5 %collective-permute-start.1 = (bf16[512,1536]{1,0:T(8,128)(2,1)S(1)}, bf16[512,1536]{1,0:T(8,128)(2,1)}, u32[]{:S(2)}, u32[]{:S(2)}) collective-permute-start(bf16[512,1536]{1,0:T(8,128)(2,1)S(1)} %copy-done.18), channel_id=1, source_target_pairs={{0,2},{1,3},{2,0},{3,1},{4,6},{5,7},{6,4},{7,5},{8,10},{9,11},{10,... | collective-permute-start | bytes 4718600 | tf_op jit(solution)/shard_map/ppermute | solution.py:482
  22.5 38.4 %collective-permute-start = (bf16[512,1536]{1,0:T(8,128)(2,1)S(1)}, bf16[512,1536]{1,0:T(8,128)(2,1)}, u32[]{:S(2)}, u32[]{:S(2)}) collective-permute-start(bf16[512,1536]{1,0:T(8,128)(2,1)S(1)} %copy-done.18), channel_id=1, source_target_pairs={{0,1},{1,0},{2,3},{3,2},{4,5},{5,4},{6,7},{7,6},{8,9},{9,8},{10,11... | collective-permute-start | bytes 4718600 | tf_op jit(solution)/shard_map/ppermute | solution.py:482
  24.0 39.7 %collective-permute-start.5 = (bf16[2,384]{1,0:T(2,128)(2,1)S(1)}, bf16[2,384]{1,0:T(2,128)(2,1)S(1)}, u32[]{:S(2)}, u32[]{:S(2)}) collective-permute-start(bf16[2,384]{1,0:T(2,128)(2,1)S(1)} %pad_maximum_fusion.18), channel_id=1, source_target_pairs={{0,2},{1,3},{2,0},{3,1},{4,6},{5,7},{6,4},{7,5},{8,10},{9,11},{10,... | collective-permute-start | bytes 4616 | tf_op jit(solution)/shard_map/ppermute | solution.py:482
  24.6 39.1 %collective-permute-start.6 = (bf16[2,384]{1,0:T(2,128)(2,1)S(1)}, bf16[2,384]{1,0:T(2,128)(2,1)S(1)}, u32[]{:S(2)}, u32[]{:S(2)}) collective-permute-start(bf16[2,384]{1,0:T(2,128)(2,1)S(1)} %pad_maximum_fusion.18), channel_id=1, source_target_pairs={{0,3},{1,2},{2,1},{3,0},{4,7},{5,6},{6,5},{7,4},{8,11},{9,10},{10,... | collective-permute-start | bytes 4616 | tf_op jit(solution)/shard_map/ppermute | solution.py:482
  26.1 37.6 %collective-permute-start.4 = (bf16[2,384]{1,0:T(2,128)(2,1)S(1)}, bf16[2,384]{1,0:T(2,128)(2,1)S(1)}, u32[]{:S(2)}, u32[]{:S(2)}) collective-permute-start(bf16[2,384]{1,0:T(2,128)(2,1)S(1)} %pad_maximum_fusion.18), channel_id=1, source_target_pairs={{0,1},{1,0},{2,3},{3,2},{4,5},{5,4},{6,7},{7,6},{8,9},{9,8},{10,11... | collective-permute-start | bytes 4616 | tf_op jit(solution)/shard_map/ppermute | solution.py:482
  30.1 602.7 %reduce-scatter.7.cloned.1.call-start = ((), (), s32[]{:S(2)}) async-start(), calls=%async_computation.8 | async-start | bytes 10616832 | tf_op jit(solution)/shard_map/reduce_scatter | solution.py:728
  96.5 31.5 %collective-permute-start.10 = (bf16[1536,384]{1,0:T(8,128)(2,1)S(1)}, bf16[1536,384]{1,0:T(8,128)(2,1)S(1)}, u32[]{:S(2)}, u32[]{:S(2)}) collective-permute-start(bf16[1536,384]{1,0:T(8,128)(2,1)S(1)} %slice.292), channel_id=1, source_target_pairs={{0,2},{1,3},{2,0},{3,1},{4,6},{5,7},{6,4},{7,5},{8,10},{9,11},{10,... | collective-permute-start | bytes 3538952 | tf_op jit(solution)/shard_map/ppermute | solution.py:482
  98.1 30.0 %collective-permute-start.8 = (bf16[1536,384]{1,0:T(8,128)(2,1)S(1)}, bf16[1536,384]{1,0:T(8,128)(2,1)S(1)}, u32[]{:S(2)}, u32[]{:S(2)}) collective-permute-start(bf16[1536,384]{1,0:T(8,128)(2,1)S(1)} %slice.292), channel_id=1, source_target_pairs={{0,1},{1,0},{2,3},{3,2},{4,5},{5,4},{6,7},{7,6},{8,9},{9,8},{10,11... | collective-permute-start | bytes 3538952 | tf_op jit(solution)/shard_map/ppermute | solution.py:482
  98.5 72.1 %collective-permute-start.19 = (bf16[512,1536]{1,0:T(8,128)(2,1)S(1)}, bf16[512,1536]{1,0:T(8,128)(2,1)S(1)}, u32[]{:S(2)}, u32[]{:S(2)}) collective-permute-start(bf16[512,1536]{1,0:T(8,128)(2,1)S(1)} %copy-done.2), channel_id=1, source_target_pairs={{0,2},{1,3},{2,0},{3,1},{4,6},{5,7},{6,4},{7,5},{8,10},{9,11},{10,... | collective-permute-start | bytes 4718600 | tf_op jit(solution)/shard_map/ppermute | solution.py:482
  99.1 74.0 %collective-permute-start.18 = (bf16[512,1536]{1,0:T(8,128)(2,1)S(1)}, bf16[512,1536]{1,0:T(8,128)(2,1)S(1)}, u32[]{:S(2)}, u32[]{:S(2)}) collective-permute-start(bf16[512,1536]{1,0:T(8,128)(2,1)S(1)} %copy-done.2), channel_id=1, source_target_pairs={{0,1},{1,0},{2,3},{3,2},{4,5},{5,4},{6,7},{7,6},{8,9},{9,8},{10,11... | collective-permute-start | bytes 4718600 | tf_op jit(solution)/shard_map/ppermute | solution.py:482
  127.3 41.9 %collective-permute-start.7 = (bf16[384,512]{1,0:T(8,128)(2,1)S(1)}, bf16[384,512]{1,0:T(8,128)(2,1)S(1)}, u32[]{:S(2)}, u32[]{:S(2)}) collective-permute-start(bf16[384,512]{1,0:T(8,128)(2,1)S(1)} %get-tuple-element.233), channel_id=1, source_target_pairs={{0,1},{1,0},{2,3},{3,2},{4,5},{5,4},{6,7},{7,6},{8,9},{9,8},{10,11... | collective-permute-start | bytes 1179656 | tf_op jit(solution)/shard_map/ppermute | solution.py:482
  128.2 53.6 %collective-permute-start.12 = (bf16[768,384]{1,0:T(8,128)(2,1)S(1)}, bf16[768,384]{1,0:T(8,128)(2,1)S(1)}, u32[]{:S(2)}, u32[]{:S(2)}) collective-permute-start(bf16[768,384]{1,0:T(8,128)(2,1)S(1)} %slice.293), channel_id=1, source_target_pairs={{0,1},{1,0},{2,3},{3,2},{4,5},{5,4},{6,7},{7,6},{8,9},{9,8},{10,11... | collective-permute-start | bytes 1769480 | tf_op jit(solution)/shard_map/ppermute | solution.py:482
  129.7 52.1 %collective-permute-start.13 = (bf16[768,384]{1,0:T(8,128)(2,1)S(1)}, bf16[768,384]{1,0:T(8,128)(2,1)S(1)}, u32[]{:S(2)}, u32[]{:S(2)}) collective-permute-start(bf16[768,384]{1,0:T(8,128)(2,1)S(1)} %slice.294), channel_id=1, source_target_pairs={{0,2},{1,3},{2,0},{3,1},{4,6},{5,7},{6,4},{7,5},{8,10},{9,11},{10,... | collective-permute-start | bytes 1769480 | tf_op jit(solution)/shard_map/ppermute | solution.py:482
  190.5 53.8 %collective-permute-start.15 = (bf16[512,1536]{1,0:T(8,128)(2,1)S(1)}, bf16[512,1536]{1,0:T(8,128)(2,1)}, u32[]{:S(2)}, u32[]{:S(2)}) collective-permute-start(bf16[512,1536]{1,0:T(8,128)(2,1)S(1)} %get-tuple-element.89.refs_0_), channel_id=1, source_target_pairs={{0,2},{1,3},{2,0},{3,1},{4,6},{5,7},{6,4},{7,5},{8,10},{9,11},{10,... | collective-permute-start | bytes 4718600 | tf_op jit(solution)/shard_map/ppermute | solution.py:482
  192.0 54.8 %collective-permute-start.14 = (bf16[512,1536]{1,0:T(8,128)(2,1)S(1)}, bf16[512,1536]{1,0:T(8,128)(2,1)}, u32[]{:S(2)}, u32[]{:S(2)}) collective-permute-start(bf16[512,1536]{1,0:T(8,128)(2,1)S(1)} %get-tuple-element.89.refs_0_), channel_id=1, source_target_pairs={{0,1},{1,0},{2,3},{3,2},{4,5},{5,4},{6,7},{7,6},{8,9},{9,8},{10,11... | collective-permute-start | bytes 4718600 | tf_op jit(solution)/shard_map/ppermute | solution.py:482
  192.8 48.7 %collective-permute-start.20 = (bf16[256,1536]{1,0:T(8,128)(2,1)}, bf16[256,1536]{1,0:T(8,128)(2,1)}, u32[]{:S(2)}, u32[]{:S(2)}) collective-permute-start(bf16[256,1536]{1,0:T(8,128)(2,1)} %slice.303), channel_id=1, source_target_pairs={{0,1},{1,0},{2,3},{3,2},{4,5},{5,4},{6,7},{7,6},{8,9},{9,8},{10,11... | collective-permute-start | bytes 2359304 | tf_op jit(solution)/shard_map/ppermute | solution.py:482
  194.0 47.4 %collective-permute-start.21 = (bf16[256,1536]{1,0:T(8,128)(2,1)}, bf16[256,1536]{1,0:T(8,128)(2,1)}, u32[]{:S(2)}, u32[]{:S(2)}) collective-permute-start(bf16[256,1536]{1,0:T(8,128)(2,1)} %slice.304), channel_id=1, source_target_pairs={{0,2},{1,3},{2,0},{3,1},{4,6},{5,7},{6,4},{7,5},{8,10},{9,11},{10,... | collective-permute-start | bytes 2359304 | tf_op jit(solution)/shard_map/ppermute | solution.py:482
  342.6 340.6 %reduce-scatter.9.cloned.1.call-start = ((), (), s32[]{:S(2)}) async-start(), calls=%async_computation.9 | async-start | bytes 15925248 | tf_op jit(solution)/shard_map/reduce_scatter | solution.py:728
  395.3 379.2 %reduce-scatter.11.cloned.1.call-start = ((), (), s32[]{:S(2)}) async-start(), calls=%async_computation.10 | async-start | bytes 8847360 | tf_op jit(solution)/shard_map/reduce_scatter | solution.py:723
  466.7 36.9 %collective-permute-start.22 = (bf16[512,1536]{1,0:T(8,128)(2,1)}, bf16[512,1536]{1,0:T(8,128)(2,1)}, u32[]{:S(2)}, u32[]{:S(2)}) collective-permute-start(bf16[512,1536]{1,0:T(8,128)(2,1)} %pad_maximum_fusion.7), channel_id=1, source_target_pairs={{0,1},{1,0},{2,3},{3,2},{4,5},{5,4},{6,7},{7,6},{8,9},{9,8},{10,11... | collective-permute-start | bytes 4718600 | tf_op jit(solution)/shard_map/ppermute | solution.py:482
  468.2 37.2 %collective-permute-start.23 = (bf16[512,1536]{1,0:T(8,128)(2,1)}, bf16[512,1536]{1,0:T(8,128)(2,1)}, u32[]{:S(2)}, u32[]{:S(2)}) collective-permute-start(bf16[512,1536]{1,0:T(8,128)(2,1)} %pad_maximum_fusion.8), channel_id=1, source_target_pairs={{0,2},{1,3},{2,0},{3,1},{4,6},{5,7},{6,4},{7,5},{8,10},{9,11},{10,... | collective-permute-start | bytes 4718600 | tf_op jit(solution)/shard_map/ppermute | solution.py:482
  574.3 250.5 %reduce-scatter.13.cloned.1.call-start = ((), (), s32[]{:S(2)}) async-start(), calls=%async_computation.11 | async-start | bytes 3538944
  579.6 48.7 %collective-permute-start.33 = (bf16[512,1536]{1,0:T(8,128)(2,1)S(1)}, bf16[512,1536]{1,0:T(8,128)(2,1)S(1)}, u32[]{:S(2)}, u32[]{:S(2)}) collective-permute-start(bf16[512,1536]{1,0:T(8,128)(2,1)S(1)} %pad_maximum_fusion.10), channel_id=1, source_target_pairs={{0,1},{1,0},{2,3},{3,2},{4,5},{5,4},{6,7},{7,6},{8,9},{9,8},{10,11... | collective-permute-start | bytes 4718600 | tf_op jit(solution)/shard_map/ppermute | solution.py:482
  580.4 50.4 %collective-permute-start.34 = (bf16[512,1536]{1,0:T(8,128)(2,1)S(1)}, bf16[512,1536]{1,0:T(8,128)(2,1)S(1)}, u32[]{:S(2)}, u32[]{:S(2)}) collective-permute-start(bf16[512,1536]{1,0:T(8,128)(2,1)S(1)} %pad_maximum_fusion.11), channel_id=1, source_target_pairs={{0,2},{1,3},{2,0},{3,1},{4,6},{5,7},{6,4},{7,5},{8,10},{9,11},{10,... | collective-permute-start | bytes 4718600 | tf_op jit(solution)/shard_map/ppermute | solution.py:482
  643.4 35.6 %collective-permute-start.35 = (bf16[512,1536]{1,0:T(8,128)(2,1)S(1)}, bf16[512,1536]{1,0:T(8,128)(2,1)S(1)}, u32[]{:S(2)}, u32[]{:S(2)}) collective-permute-start(bf16[512,1536]{1,0:T(8,128)(2,1)S(1)} %pad_maximum_fusion.12), channel_id=1, source_target_pairs={{0,1},{1,0},{2,3},{3,2},{4,5},{5,4},{6,7},{7,6},{8,9},{9,8},{10,11... | collective-permute-start | bytes 4718600 | tf_op jit(solution)/shard_map/ppermute | solution.py:482
  644.6 36.5 %collective-permute-start.36 = (bf16[512,1536]{1,0:T(8,128)(2,1)S(1)}, bf16[512,1536]{1,0:T(8,128)(2,1)S(1)}, u32[]{:S(2)}, u32[]{:S(2)}) collective-permute-start(bf16[512,1536]{1,0:T(8,128)(2,1)S(1)} %pad_maximum_fusion.13), channel_id=1, source_target_pairs={{0,2},{1,3},{2,0},{3,1},{4,6},{5,7},{6,4},{7,5},{8,10},{9,11},{10,... | collective-permute-start | bytes 4718600 | tf_op jit(solution)/shard_map/ppermute | solution.py:482
  778.9 40.8 %collective-permute-start.39 = (bf16[256,1536]{1,0:T(8,128)(2,1)S(1)}, bf16[256,1536]{1,0:T(8,128)(2,1)S(1)}, u32[]{:S(2)}, u32[]{:S(2)}) collective-permute-start(bf16[256,1536]{1,0:T(8,128)(2,1)S(1)} %get-tuple-element.120), channel_id=1, source_target_pairs={{0,2},{1,3},{2,0},{3,1},{4,6},{5,7},{6,4},{7,5},{8,10},{9,11},{10,... | collective-permute-start | bytes 2359304 | tf_op jit(solution)/shard_map/ppermute | solution.py:482
  780.4 39.2 %collective-permute-start.40 = (bf16[256,1536]{1,0:T(8,128)(2,1)S(1)}, bf16[256,1536]{1,0:T(8,128)(2,1)S(1)}, u32[]{:S(2)}, u32[]{:S(2)}) collective-permute-start(bf16[256,1536]{1,0:T(8,128)(2,1)S(1)} %get-tuple-element.121), channel_id=1, source_target_pairs={{0,1},{1,0},{2,3},{3,2},{4,5},{5,4},{6,7},{7,6},{8,9},{9,8},{10,11... | collective-permute-start | bytes 2359304 | tf_op jit(solution)/shard_map/ppermute | solution.py:482
  (100 other events, 1142.1 us)
Sparse Core Ops, SparseCore 0:
  10.2 44.2 all-gather.4
  56.1 89.6 all-gather.6
  147.9 128.0 all-gather.8
  278.0 127.7 all-gather.10
  408.0 97.6 reduce-scatter.6
  507.9 142.4 reduce-scatter.8
  652.7 121.8 reduce-scatter.10
  776.8 46.9 reduce-scatter.12
